TPU v7x, 512 devices: a whole 4x4x16 slice. The times are simulated.
512 devices in a mesh: pair: 64 (over y, z), tm: 8 (over x, core).
Axes of the slice: x: 4, y: 4, z: 16, core: 2. Of those that a mesh axis runs over, the one named last changes fastest.
Arguments:
- traces: bfloat16 [16, 2048, 8192], P('tm', None, 'pair'), may hold values from -6 to 6
- source_list: int32 [64, 8], replicated, may hold values from 0 to 63
- source_count: int32 [64], replicated, may hold values from 1 to 8, 320 in all
- receiver_start: int32 [64], replicated, may hold values from 65 to 127
- segment_slot: int32 [16], replicated, may hold values from 0 to 1, as said below
Outputs:
- stacks: bfloat16 [8, 2, 512, 64, 128], P('tm', None, 'pair')
Inputs may be any that keep to these rules, and one draw needn't show every extreme that they name: `source_list`: block index of a virtual source. The live slots of owner p are its first source_count[p] slots. `receiver_start`: every receiver window reaches into the next block. `segment_slot`: every stack receives exactly 8 segments.
All inputs are finite; a program needn't handle non-finite values.
Results may differ from a plain program's by a relative error of at most 0.0067.
Values may be sent and summed in bfloat16 or wider, within the bound.
No kernel may reach another device: no remote copies, remote signals or barrier semaphores. Data moves between devices by JAX's collectives and lax.ppermute only.
A program may use at most 64 MiB of HBM per device.

v0:
```python
import math

import jax
import jax.numpy as jnp
from jax import lax
from jax.sharding import PartitionSpec as P

SAMPLES = 2048
NF = 512
BAND = 32
R_CH = 64
LAGS = 8
SLOTS = 2
F0 = 64


whiten_eps = 1e-06


def from_behind(block, axis, distance):
    devices = range(lax.axis_size(axis))
    route = [(i - distance, i) for i in devices if i - distance in devices]
    return lax.ppermute(block, axis, route)


def transform_table(sample_count, bin_count, lowest):
    bins = lowest + jnp.arange(bin_count, dtype=jnp.int32)
    sample_steps = jnp.arange(sample_count, dtype=jnp.int32)
    phase = bins[:, None] * sample_steps[None, :] % sample_count
    angle = 2.0 * jnp.pi / sample_count * phase.astype(jnp.float32)
    table = jnp.concatenate([jnp.cos(angle), -jnp.sin(angle)], axis=0)
    return table.astype(jnp.bfloat16)


def whiten_spectra(spectra, channel_count):
    seg_count = spectra.shape[0]
    grouped = spectra.reshape(seg_count, 2, NF // BAND, BAND, channel_count)
    band_power = jnp.mean(grouped * grouped, axis=(1, 3), keepdims=True)
    whitened = grouped / jnp.sqrt(band_power + whiten_eps)
    return whitened.reshape(seg_count, 2, NF, channel_count).astype(jnp.bfloat16)


def lag_kernel(window, slot_ids, total_segments, lag_steps):
    seg_count = window.shape[0]
    lag_total = lag_steps.shape[0]
    bins = F0 + jnp.arange(NF, dtype=jnp.int32)
    phase = lag_steps[:, None] * bins[None, :] % SAMPLES
    angle = 2.0 * jnp.pi / SAMPLES * phase.astype(jnp.float32)
    lag_cos = jnp.cos(angle)[:, None, None, :]
    lag_sin = jnp.sin(angle)[:, None, None, :]
    window_t = jnp.transpose(window.astype(jnp.float32), (3, 0, 1, 2))
    recv_real = window_t[:, :, 0][None]
    recv_imag = window_t[:, :, 1][None]
    for_real = lag_cos * recv_real + lag_sin * recv_imag
    for_imag = lag_cos * recv_imag - lag_sin * recv_real
    both = jnp.stack([for_real, for_imag], axis=3)
    onehot = (slot_ids[None, :] == jnp.arange(SLOTS, dtype=jnp.int32)[:, None]).astype(jnp.float32)
    norm_factor = 1.0 / math.sqrt(2.0 * NF * total_segments / SLOTS)
    weighted = both[:, None] * onehot[None, :, None, :, None, None] * norm_factor
    return weighted.reshape(lag_total, SLOTS, R_CH, seg_count * 2 * NF).astype(jnp.bfloat16)


def body(traces, source_list, source_count, receiver_start, segment_slot):
    seg_count = traces.shape[0]
    channel_count = traces.shape[2]
    pair_size = lax.axis_size("pair")
    time_size = lax.axis_size("tm")
    total_segments = seg_count * time_size
    slot_count = source_list.shape[1]
    table = transform_table(traces.shape[1], NF, F0)
    spectra = jnp.einsum("fn,snc->sfc", table, traces, preferred_element_type=jnp.float32)
    whitened = whiten_spectra(spectra, channel_count)
    banded = lax.all_to_all(whitened[None], "pair", split_axis=3, concat_axis=0, tiled=True)
    flat_ids = source_list.reshape(-1)
    picked = jnp.take(banded, flat_ids, axis=0)
    live_slots = (jnp.arange(slot_count, dtype=jnp.int32)[None, :] < source_count[:, None]).reshape(
        -1
    )
    picked = picked * live_slots.astype(jnp.bfloat16)[:, None, None, None, None]
    outgoing = picked.reshape((pair_size, slot_count) + banded.shape[1:])
    beyond = from_behind(whitened, "pair", -1)
    joined = jnp.concatenate([whitened, beyond], axis=3)
    offset = receiver_start[lax.axis_index("pair")]
    window = lax.dynamic_slice_in_dim(joined, offset, R_CH, 3)
    every_lag = jnp.arange(LAGS, dtype=jnp.int32) - LAGS // 2
    first_segment = lax.axis_index("tm") * seg_count
    local_slots = lax.dynamic_slice_in_dim(segment_slot, first_segment, seg_count, 0)
    kernel = lag_kernel(window, local_slots, total_segments, every_lag)
    arrived = lax.all_to_all(outgoing, "pair", split_axis=0, concat_axis=4, tiled=True)
    sources = arrived[0].reshape(arrived.shape[1], -1, arrived.shape[-1])
    partial_sums = jnp.einsum(
        "lqjc,kci->lqkji", kernel, sources, preferred_element_type=jnp.float32
    )
    stacked = lax.psum_scatter(partial_sums, "tm", scatter_dimension=0, tiled=True)
    return stacked.astype(jnp.bfloat16)


def solution(mesh):
    placed = (P("tm", None, "pair"), P(), P(), P(), P())
    return jax.shard_map(
        body,
        mesh=mesh,
        in_specs=placed,
        out_specs=P("tm", None, "pair", None, None),
        check_vma=False,
    )
```

profile of v0, /device:TPU:1, one launch (start us, length us, event | category | flops | bytes accessed | tf_op | source)
XLA Modules:
  0.0 366.9 jit_solution(10064083227919488987)
XLA Ops:
  0.0 0.0 copy-start
  0.0 18.0 %cosine_convert_fusion = (bf16[512,2048]{1,0:T(8,128)(2,1)S(1)}, bf16[512,2048]{1,0:T(8,128)(2,1)S(1)}) fusion(s32[512]{0:T(512)S(1)} %iota_add_fusion), kind=kLoop, calls=%fused_computation.20 | loop fusion | flops 17825792 | bytes 4196352 | tf_op jit(solution)/shard_map/convert.1
  18.1 0.0 copy-done
  18.1 1.3 bitcast_multiply_fusion
  19.3 0.0 copy-start.3
  19.4 0.0 copy-start.4
  19.4 0.1 reduce_sum.9
  19.6 0.1 divide_convert_fusion.1
  19.7 1.3 copy.53
  21.0 19.3 %all-to-all-start = ((bf16[1,2,2,512,128]{4,2,1,0,3:T(2,128)(2,1)}), bf16[1,2,2,512,128]{4,2,1,0,3:T(2,128)(2,1)S(1)}, u32[]{:S(2)}, u32[]{:S(2)}) async-start(bf16[1,2,2,512,128]{4,2,1,0,3:T(2,128)(2,1)} %copy.53), calls=%async_computation | async-start | bytes 1048576 | tf_op jit(solution)/shard_map/all_to_all | solution.py:73
  40.3 0.0 copy-done.3
  40.3 0.1 copy.56
  40.4 0.1 reshape.205
  40.5 0.1 copy.52
  40.6 0.0 copy-done.4
  40.6 0.1 fusion.19
  40.7 29.0 %all-to-all-done = bf16[1,2,2,512,128]{4,2,1,0,3:T(2,128)(2,1)S(1)} async-done(((bf16[1,2,2,512,128]{4,2,1,0,3:T(2,128)(2,1)}), bf16[1,2,2,512,128]{4,2,1,0,3:T(2,128)(2,1)S(1)}, u32[]{:S(2)}, u32[]{:S(2)}) %all-to-all-start) | async-done | bytes 524320 | tf_op jit(solution)/shard_map/all_to_all | solution.py:73
  69.7 0.0 copy-start.2
  69.7 0.8 copy-done.2
  70.5 1.1 copy.67
  71.6 3.5 gather_fusion
  75.1 5.6 %select_multiply_fusion = bf16[64,8,2,2,8,128]{5,4,3,2,1,0:T(8,128)(2,1)} fusion(bf16[64,8,2,2,8,128]{5,4,3,2,1,0:T(8,128)(2,1)} %bitcast.55, pred[64,8]{1,0:T(8,128)(4,1)S(1)} %copy.52, bf16[64,8]{1,0:T(8,128)(2,1)S(1)} %fusion.19), kind=kLoop, calls=%fused_computation.18 | loop fusion | flops 4194304 | bytes 8390144 | tf_op jit(solution)/shard_map/mul | solution.py:79
  80.7 0.0 copy-start.5
  80.7 0.0 copy-start.6
  80.7 9.0 %all-to-all-start.1 = ((bf16[64,8,2,2,8,128]{5,4,3,2,1,0:T(8,128)(2,1)}), bf16[64,8,2,2,8,128]{5,4,3,2,1,0:T(8,128)(2,1)}, u32[]{:S(2)}, u32[]{:S(2)}) async-start(bf16[64,8,2,2,8,128]{5,4,3,2,1,0:T(8,128)(2,1)} %select_multiply_fusion), calls=%async_computation.1 | async-start | bytes 8388608 | tf_op jit(solution)/shard_map/all_to_all | solution.py:89
  89.8 0.1 divide_convert_fusion
  89.9 1.5 collective-permute-start
  91.4 0.0 copy-done.5
  91.4 0.1 dynamic_slice.11
  91.5 0.1 mul.236
  91.6 0.0 copy-done.6
  91.6 0.6 dynamic_slice.9
  94.1 1.3 dynamic-slice
  95.4 0.2 fusion.24
  95.6 186.0 %collective-permute-done = bf16[2,2,512,128]{3,2,1,0:T(8,128)(2,1)S(1)} collective-permute-done((bf16[2,2,512,128]{3,2,1,0:T(8,128)(2,1)S(1)}, bf16[2,2,512,128]{3,2,1,0:T(8,128)(2,1)S(1)}, u32[]{:S(2)}, u32[]{:S(2)}) %collective-permute-start) | collective-permute-done | bytes 524320 | tf_op jit(solution)/shard_map/ppermute | solution.py:23
  281.6 0.4 convert_bitcast_fusion
  282.0 0.1 slice_bitcast_fusion.1
  282.1 0.2 copy.59
  282.3 0.2 copy.58
  282.5 4.5 %multiply_add_fusion = (f32[8,64,2,1,512]{4,3,2,1,0:T(1,128)S(1)}, f32[8,64,2,1,512]{4,3,2,1,0:T(1,128)S(1)}) fusion(f32[64,2,512]{2,1,0:T(2,128)S(1)} %copy.59, f32[8,512]{1,0:T(8,128)S(1)} %get-tuple-element.10, f32[64,2,512]{2,1,0:T(2,128)S(1)} %copy.58, f32[8,512]{1,0:T(8,128)S(1)} %get-tuple-element.9), kind=kLoop, calls=%fused_computation.26 | loop fusion | flops 3145728 | bytes 4751360 | tf_op jit(solution)/shard_map/add | solution.py:54
  287.0 5.6 %pad_maximum_fusion = f32[8,64,2,2,512]{4,3,2,1,0:T(2,128)} fusion(f32[8,64,2,1,512]{4,3,2,1,0:T(1,128)S(1)} %get-tuple-element.8, f32[8,64,2,1,512]{4,3,2,1,0:T(1,128)S(1)} %get-tuple-element.7), kind=kLoop, calls=%fused_computation.14 | loop fusion | flops 1048576 | bytes 8388608 | tf_op jit(solution)/shard_map/stack | solution.py:56
  292.6 6.6 %mul.233 = f32[8,64,2048]{2,1,0:T(8,128)} reshape(f32[8,64,2,2,512]{4,3,2,1,0:T(2,128)} %pad_maximum_fusion) | data formatting | bytes 8388608 | tf_op jit(solution)/shard_map/mul | solution.py:59
  299.3 0.0 all-to-all-done.1
  299.3 0.0 copy-start.1
  299.3 3.5 copy.57
  302.8 0.0 copy-done.1
  302.8 6.1 %fusion.15 = f32[8,2,8,64,128]{4,3,1,0,2:T(8,128)} fusion(bf16[8,2048,128,1,1]{2,1,4,3,0:T(8,128)(2,1)S(1)} %bitcast.58, f32[2,2048]{1,0:T(2,128)S(1)} %mul.237, f32[8,64,2048]{2,1,0:T(8,128)S(1)} %copy-done.1), kind=kOutput, calls=%fused_computation.24 | convolution fusion | flops 4301258752 | bytes 12599296 | tf_op jit(solution)/shard_map/lqjc,kci->lqkji/dot_general | solution.py:91
  308.9 56.6 %all-reduce.2 = bf16[8,2,8,64,128]{4,3,1,0,2:T(8,128)(2,1)S(1)} all-reduce(f32[8,2,8,64,128]{4,3,1,0,2:T(8,128)} %fusion.15), channel_id=2, replica_groups=mesh['pair'=64,'tm'=8] {'tm'}, use_global_device_ids=true, to_apply=%region_1.2.clone | all-reduce | flops 1048576 | bytes 6291456
  365.5 0.7 dynamic-slice_convert_fusion
  366.1 0.7 copy.60
  (9 shorter events, 0.1 us)
Async XLA Ops:
  0.0 18.1 %copy-start = (bf16[2,2048,128]{2,1,0:T(8,128)(2,1)S(1)}, bf16[2,2048,128]{2,1,0:T(8,128)(2,1)}, u32[]{:S(2)}) copy-start(bf16[2,2048,128]{2,1,0:T(8,128)(2,1)} %param.5) | copy-start | bytes 3145732
  19.3 20.9 %copy-start.3 = (s32[64,8]{0,1:T(8,128)S(1)}, s32[64,8]{0,1:T(8,128)}, u32[]{:S(2)}) copy-start(s32[64,8]{0,1:T(8,128)} %param.6) | copy-start | bytes 6148
  19.4 21.3 %copy-start.4 = (s32[64]{0:T(128)S(1)}, s32[64]{0:T(128)}, u32[]{:S(2)}) copy-start(s32[64]{0:T(128)} %param.7) | copy-start | bytes 772
  21.0 48.7 %all-to-all-start = ((bf16[1,2,2,512,128]{4,2,1,0,3:T(2,128)(2,1)}), bf16[1,2,2,512,128]{4,2,1,0,3:T(2,128)(2,1)S(1)}, u32[]{:S(2)}, u32[]{:S(2)}) async-start(bf16[1,2,2,512,128]{4,2,1,0,3:T(2,128)(2,1)} %copy.53), calls=%async_computation | async-start | bytes 1048576 | tf_op jit(solution)/shard_map/all_to_all | solution.py:73
  69.7 0.8 copy-start.2
  80.7 10.7 %copy-start.5 = (s32[16]{0:T(128)S(1)}, s32[16]{0:T(128)}, u32[]{:S(2)}) copy-start(s32[16]{0:T(128)} %param.9) | copy-start | bytes 196
  80.7 10.9 %copy-start.6 = (s32[64]{0:T(128)S(1)}, s32[64]{0:T(128)}, u32[]{:S(2)}) copy-start(s32[64]{0:T(128)} %param.8) | copy-start | bytes 772
  80.7 218.5 %all-to-all-start.1 = ((bf16[64,8,2,2,8,128]{5,4,3,2,1,0:T(8,128)(2,1)}), bf16[64,8,2,2,8,128]{5,4,3,2,1,0:T(8,128)(2,1)}, u32[]{:S(2)}, u32[]{:S(2)}) async-start(bf16[64,8,2,2,8,128]{5,4,3,2,1,0:T(8,128)(2,1)} %select_multiply_fusion), calls=%async_computation.1 | async-start | bytes 8388608 | tf_op jit(solution)/shard_map/all_to_all | solution.py:89
  89.9 191.7 %collective-permute-start = (bf16[2,2,512,128]{3,2,1,0:T(8,128)(2,1)S(1)}, bf16[2,2,512,128]{3,2,1,0:T(8,128)(2,1)S(1)}, u32[]{:S(2)}, u32[]{:S(2)}) collective-permute-start(bf16[2,2,512,128]{3,2,1,0:T(8,128)(2,1)S(1)} %divide_convert_fusion), channel_id=1, source_target_pairs={{8,0},{16,8},{24,16},{32,24},{40,32},{48,40},{56,48},{64,56},{72,6... | collective-permute-start | bytes 1572872 | tf_op jit(solution)/shard_map/ppermute | solution.py:23
  299.3 3.5 copy-start.1
where the time goes:
time: 368 us; the launch traced here: 367 us
  waiting for transfers between devices  215 us (58%)
  blocking collectives  56.6 us (15%)
  other arithmetic  34.8 us (9%)
  starting transfers between devices  29.8 us (8%)
  local copies, waits for them, and re-layouts  21.1 us (6%)
  matrix products  7.36 us (2%)
    ppermute x1, waiting for transfers between devices, from_behind(): return lax.ppermute(block, axis, route)  186 us
    unnamed x1, blocking collectives  56.6 us
    all_to_all x1, waiting for transfers between devices, body(): lax.all_to_all(whitened[None], 'pair', split_axis=3, concat_axis=0, tiled...  29 us
    all_to_all x1, starting transfers between devices, body(): lax.all_to_all(whitened[None], 'pair', split_axis=3, concat_axis=0, tiled...  19.3 us
    another operation x1, other arithmetic  18 us
    all_to_all x1, starting transfers between devices, body(): lax.all_to_all(outgoing, 'pair', split_axis=0, concat_axis=4, tiled=True)  9.04 us
  transfers between devices with their start and end apart: 3, of which 2 were waited for; matrix products, arithmetic and copies ran while one was open for 6% of the time, Pallas kernels for 0%

commit v1 on v0

v1 whole, which is shorter than its diff:
```python
import jax
import jax.numpy as jnp
import numpy as np
from jax import lax
from jax.experimental import pallas as pl
from jax.experimental.pallas import tpu as pltpu
from jax.sharding import Mesh, PartitionSpec as P

CH = 128
SAMPLES = 2048
NF = 512
BAND = 32
K = 8
R_CH = 64
LAGS = 8
SLOTS = 2
F0 = 64
SEGS = 16
NY, NZ, NX, NC = 4, 16, 4, 2
SEG = 2
CQ = CH // NY
FB = 128
NB = NF // FB
KF = 2 * NF
EPS = 1e-06
NORM = np.float32((2.0 * NF * SEGS / SLOTS) ** (-0.5))
BF = jnp.bfloat16
F32 = jnp.float32
VMEM = 48 * 1024 * 1024


def transform_table():
    bins = F0 + np.arange(NF, dtype=np.int64)
    phase = (bins[:, None] * np.arange(SAMPLES // 2, dtype=np.int64)[None, :]) % SAMPLES
    steps = np.arange(SAMPLES, dtype=np.float32) * np.float32(2.0 * np.pi / SAMPLES)
    cos = np.cos(steps)[phase]
    sin = -np.sin(steps)[phase]
    return np.stack([cos, sin], axis=0).astype(jnp.bfloat16)


def lag_tables():
    bins = F0 + np.arange(NF, dtype=np.int64)
    lags = np.arange(LAGS, dtype=np.int64) - LAGS // 2
    phase = (lags[:, None] * bins[None, :]) % SAMPLES
    angle = phase.astype(np.float32) * np.float32(2.0 * np.pi / SAMPLES)
    return np.stack([np.cos(angle), np.sin(angle)], axis=0).astype(np.float32)


def whiten_kernel(traces_ref, table_ref, split_ref, low_ref, high_ref):
    half = SAMPLES // 2
    table = table_ref[...].reshape(2 * FB, half)
    early = jnp.concatenate([traces_ref[s, :half] for s in range(SEG)], axis=1)
    late = jnp.concatenate([traces_ref[s, half:] for s in range(SEG)], axis=1)
    early = jnp.dot(table, early, preferred_element_type=F32)
    late = jnp.dot(table, late, preferred_element_type=F32)
    odd = lax.broadcasted_iota(jnp.int32, late.shape, 0) % 2 == 1
    spectra = early + jnp.where(odd, -late, late)
    grouped = spectra.reshape(2, FB // BAND, BAND, SEG * CH)
    power = jnp.sum(grouped * grouped, axis=(0, 2)) * (1.0 / (2 * BAND))
    scale = 1.0 / jnp.sqrt(power + EPS)
    whitened = grouped * scale[None, :, None, :]
    flipped = whitened.reshape(2 * FB, SEG * CH).T.astype(BF)
    for s in range(SEG):
        low_ref[s] = flipped[s * CH : s * CH + CH // 2]
        high_ref[s] = flipped[s * CH + CH // 2 : (s + 1) * CH]
        for y in range(NY):
            split_ref[y, s] = flipped[s * CH + y * CQ : s * CH + (y + 1) * CQ]


def whiten(traces, table):
    half = jax.ShapeDtypeStruct((SEG, CH // 2, KF), BF)
    half_spec = pl.BlockSpec((SEG, CH // 2, 2 * FB), lambda g: (0, 0, g))
    return pl.pallas_call(
        whiten_kernel,
        grid=(NB,),
        in_specs=[
            pl.BlockSpec((SEG, SAMPLES, CH), lambda g: (0, 0, 0)),
            pl.BlockSpec((2, FB, SAMPLES // 2), lambda g: (0, g, 0)),
        ],
        out_specs=[
            pl.BlockSpec((NY, SEG, CQ, 2 * FB), lambda g: (0, 0, 0, g)),
            half_spec,
            half_spec,
        ],
        out_shape=[jax.ShapeDtypeStruct((NY, SEG, CQ, KF), BF), half, half],
        compiler_params=pltpu.CompilerParams(vmem_limit_bytes=VMEM),
        name="whiten",
    )(traces, table)


def lag_kernel_body(window_ref, lag_ref, out_ref):
    for b in range(NB):
        at = b * 2 * FB
        real = window_ref[0, 0, :, at : at + FB].astype(F32)
        imag = window_ref[0, 0, :, at + FB : at + 2 * FB].astype(F32)
        for l in range(LAGS):
            cos = lag_ref[0, l : l + 1, b * FB : (b + 1) * FB]
            sin = lag_ref[1, l : l + 1, b * FB : (b + 1) * FB]
            for_real = (cos * real + sin * imag) * NORM
            for_imag = (cos * imag - sin * real) * NORM
            out_ref[0, 0, l, :, at : at + FB] = for_real.astype(BF)
            out_ref[0, 0, l, :, at + FB : at + 2 * FB] = for_imag.astype(BF)


def lag_kernels(windows, lags):
    return pl.pallas_call(
        lag_kernel_body,
        grid=(NY, SEG),
        in_specs=[
            pl.BlockSpec((1, 1, R_CH, KF), lambda o, s: (o, s, 0, 0)),
            pl.BlockSpec((2, LAGS, NF), lambda o, s: (0, 0, 0)),
        ],
        out_specs=pl.BlockSpec((1, 1, LAGS, R_CH, KF), lambda o, s: (o, s, 0, 0, 0)),
        out_shape=jax.ShapeDtypeStruct((NY, SEG, LAGS, R_CH, KF), BF),
        compiler_params=pltpu.CompilerParams(vmem_limit_bytes=VMEM),
        name="lag_kernels",
    )(windows, lags)


def correlate_body(info_ref, kernel_ref, *refs):
    sources, out_ref = refs[:K], refs[K]
    o = pl.program_id(0)
    count = info_ref[64 + o]
    lane = lax.broadcasted_iota(jnp.int32, (1, K * CQ), 1)
    live = (lane < count * CQ).astype(F32)
    sums = []
    for s in range(SEG):
        left = kernel_ref[0, s].reshape(LAGS * R_CH, KF)
        right = jnp.concatenate([ref[0, 0, s] for ref in sources], axis=0)
        sums.append(lax.dot_general(left, right, (((1,), (1,)), ((), ())), preferred_element_type=F32))
    for q in range(SLOTS):
        total = 0.0
        for s in range(SEG):
            total = total + sums[s] * (live * (info_ref[68 + s] == q).astype(F32))
        out_ref[0, :, q] = total.reshape(LAGS, R_CH, K * CQ).astype(BF)


def correlate(info, kernels, gathered):
    def source_map(k):
        return lambda o, info: (info[o * K + k], info[32 + o * K + k], 0, 0, 0)

    return pl.pallas_call(
        correlate_body,
        grid_spec=pltpu.PrefetchScalarGridSpec(
            num_scalar_prefetch=1,
            grid=(NY,),
            in_specs=[
                pl.BlockSpec(
                    (1, SEG, LAGS, R_CH, KF),
                    lambda o, info: (lax.rem(info[70] + NY - o, NY), 0, 0, 0, 0),
                )
            ]
            + [pl.BlockSpec((1, 1, SEG, CQ, KF), source_map(k)) for k in range(K)],
            out_specs=pl.BlockSpec((1, LAGS, SLOTS, R_CH, K * CQ), lambda o, info: (o, 0, 0, 0, 0)),
        ),
        out_shape=jax.ShapeDtypeStruct((NY, LAGS, SLOTS, R_CH, K * CQ), BF),
        compiler_params=pltpu.CompilerParams(vmem_limit_bytes=VMEM),
        name="correlate",
    )(info, kernels, *([gathered] * K))


def finish_body(parts_ref, out_ref):
    n = NX * NC
    quarter = []
    for y in range(NY):
        total = parts_ref[y * n, 0].astype(F32)
        for t in range(1, n):
            total = total + parts_ref[y * n + t, 0].astype(F32)
        quarter.append(total)
    for k in range(K):
        row = jnp.concatenate([v[:, k * CQ : (k + 1) * CQ] for v in quarter], axis=1)
        out_ref[0, 0, k] = row.astype(BF)


def finish(parts):
    return pl.pallas_call(
        finish_body,
        grid=(SLOTS,),
        in_specs=[pl.BlockSpec((NY * NX * NC, 1, R_CH, K * CQ), lambda q: (0, q, 0, 0))],
        out_specs=pl.BlockSpec((1, 1, K, R_CH, CH), lambda q: (0, q, 0, 0, 0)),
        out_shape=jax.ShapeDtypeStruct((1, SLOTS, K, R_CH, CH), BF),
        compiler_params=pltpu.CompilerParams(vmem_limit_bytes=VMEM),
        name="finish",
    )(parts)


def body(traces, source_list, source_count, receiver_start, segment_slot):
    y = lax.axis_index("y")
    z = lax.axis_index("z")
    t = lax.axis_index(("x", "c"))
    table = jnp.asarray(transform_table())
    lags = jnp.asarray(lag_tables())
    split, low, high = whiten(traces, table)
    crossed = lax.all_to_all(split, "y", 0, 0)
    gathered = lax.all_gather(crossed, "z", axis=0, tiled=False)

    low, high, _ = lax.optimization_barrier((low, high, crossed))
    pairs = NY * NZ
    following = lax.ppermute(low, ("y", "z"), [(p, p - 1) for p in range(1, pairs)])
    joined = jnp.concatenate([high, following], axis=1)
    offset = lax.dynamic_index_in_dim(receiver_start, y * NZ + z, keepdims=False) - CH // 2
    window = lax.dynamic_slice_in_dim(joined, offset, R_CH, 1)
    windows = jnp.stack(
        [window] + [lax.ppermute(window, "y", [(i, (i + d) % NY) for i in range(NY)]) for d in range(1, NY)]
    )
    kernels = lag_kernels(windows, lags)

    lists = lax.dynamic_index_in_dim(source_list.reshape(NY, NZ, K), z, 1, keepdims=False).reshape(-1)
    counts = lax.dynamic_index_in_dim(source_count.reshape(NY, NZ), z, 1, keepdims=False)
    slots = lax.dynamic_slice_in_dim(segment_slot, t * SEG, SEG, 0)
    info = jnp.concatenate([lists % NZ, lists // NZ, counts, slots, y[None].astype(jnp.int32)])
    sums = correlate(info, kernels, gathered)
    parts = sums.reshape(NY * LAGS, SLOTS, R_CH, K * CQ)
    parts = lax.all_to_all(parts, ("y", "x", "c"), 0, 0)
    return finish(parts)


def solution(mesh):
    grid = Mesh(mesh.devices.reshape(NY, NZ, NX, NC), ("y", "z", "x", "c"))
    tm, pair = ("x", "c"), ("y", "z")
    return jax.shard_map(
        body,
        mesh=grid,
        in_specs=(P(tm, None, pair), P(), P(), P(), P()),
        out_specs=P(tm, None, pair, None, None),
        check_vma=False,
    )
```

time: 368 us -> 187 us (0.51)
  waiting for transfers between devices: 215 us -> 83.6 us
  other arithmetic: 34.8 us -> 0.33 us
  Pallas kernels: 0 us -> 17.5 us
  local copies, waits for them, and re-layouts: 21.1 us -> 4.19 us
  between operations: 2.21 us -> 14.6 us
  starting transfers between devices: 29.8 us -> 19 us
  blocking collectives: 56.6 us -> 47.6 us
  matrix products: 7.36 us -> 0 us
    ppermute x1 -> x4, waiting for transfers between devices: 186 us -> 8.91 us  [the longest x1 5.82 us: body(): lax.ppermute(low, ('y', 'z'), [(p, p - 1) for p in range(1, pairs)])]
    all_gather x0 -> x1, waiting for transfers between devices: none -> 74.6 us  [body(): gathered = lax.all_gather(crossed, 'z', axis=0, tiled=False)]
    unnamed x1 -> x0, blocking collectives: 56.6 us -> none
    all_to_all x0 -> x2, blocking collectives: none -> 47.6 us  [the longest x1 35.8 us: body(): parts = lax.all_to_all(parts, ('y', 'x', 'c'), 0, 0)]
    all_to_all x2 -> x0, waiting for transfers between devices: 29 us -> none  [the longest x1 29 us: body(): lax.all_to_all(whitened[None], 'pair', split_axis=3, concat_axis=0, tiled...]
    all_to_all x2 -> x0, starting transfers between devices: 28.3 us -> none  [the longest x1 19.3 us: body(): lax.all_to_all(whitened[None], 'pair', split_axis=3, concat_axis=0, tiled...]
    another operation x2 -> x1, other arithmetic: 23.7 us -> 0.13 us  [body(): jnp.stack([window] + [lax.ppermute(window, 'y', [(i, (i + d) % NY) for i...]
    ppermute x1 -> x4, starting transfers between devices: 1.47 us -> 19 us  [the longest x3 17.7 us: body(): lax.ppermute(window, 'y', [(i, (i + d) % NY) for i in range(NY)])]
  transfers between devices with their start and end apart: 3 -> 5, of which waited for: 2 -> 3; matrix products, arithmetic and copies ran while one was open for 6% -> 1% of each run, Pallas kernels for 0% -> 3%
where the time goes in v1:
time: 187 us
  waiting for transfers between devices  83.6 us (45%)
  blocking collectives  47.6 us (25%)
  starting transfers between devices  19 us (10%)
  Pallas kernels  17.5 us (9%)
  between operations  14.6 us (8%)
  local copies, waits for them, and re-layouts  4.19 us (2%)
    all_gather x1, waiting for transfers between devices, body(): gathered = lax.all_gather(crossed, 'z', axis=0, tiled=False)  74.6 us
    all_to_all x1, blocking collectives, body(): parts = lax.all_to_all(parts, ('y', 'x', 'c'), 0, 0)  35.8 us
    ppermute x3, starting transfers between devices, body(): lax.ppermute(window, 'y', [(i, (i + d) % NY) for i in range(NY)])  17.7 us
    all_to_all x1, blocking collectives, body(): crossed = lax.all_to_all(split, 'y', 0, 0)  11.9 us
    pallas_call x1, Pallas kernels, correlate(): pl.pallas_call(correlate_body, grid_spec=pltpu.PrefetchScalarGridSpec(num...  7.77 us
    pallas_call x1, Pallas kernels, lag_kernels(): pl.pallas_call(lag_kernel_body, grid=(NY, SEG), in_specs=[pl.BlockSpec((1...  5.89 us
    ppermute x1, waiting for transfers between devices, body(): lax.ppermute(low, ('y', 'z'), [(p, p - 1) for p in range(1, pairs)])  5.82 us
  transfers between devices with their start and end apart: 5, of which 3 were waited for; matrix products, arithmetic and copies ran while one was open for 1% of the time, Pallas kernels for 3%

profile of v1, /device:TPU:1, one launch (start us, length us, event | category | flops | bytes accessed | tf_op | source)
XLA Modules:
  0.0 186.9 jit_solution(14392423710197530711)
XLA Ops:
  6.5 0.0 all-gather.3.cloned.1.call-start
  6.5 0.0 copy-start
  6.5 1.6 copy-done
  8.1 0.0 copy-start.1
  8.1 1.2 copy-done.1
  9.4 0.0 copy-start.5
  9.4 0.0 copy-start.3
  9.4 0.0 copy-start.4
  9.4 0.0 copy-start.6
  9.4 2.5 %whiten.1 = (bf16[4,2,32,1024]{3,2,1,0:T(8,128)(2,1)S(1)}, bf16[2,64,1024]{2,1,0:T(8,128)(2,1)S(1)}, bf16[2,64,1024]{2,1,0:T(8,128)(2,1)S(1)}) custom-call(bf16[2,2048,128]{2,1,0:T(8,128)(2,1)S(1)} %copy-done.1, bf16[2,512,1024]{2,1,0:T(8,128)(2,1)S(1)} %copy-done), custom_call_target="tpu_custom_call" | custom-call | tf_op jit(solution)/shard_map/whiten/pallas_call | solution.py:73
  11.9 0.0 copy-start.2
  11.9 11.9 %all_to_all.10 = bf16[4,2,32,1024]{3,2,1,0:T(8,128)(2,1)} all-to-all(bf16[4,2,32,1024]{3,2,1,0:T(8,128)(2,1)S(1)} %get-tuple-element.12), channel_id=1, replica_groups=mesh['y'=4,'z'=16,'x'=4,'c'=2] {'y'}, dimensions={0} | all-to-all | bytes 1048576 | tf_op jit(solution)/shard_map/all_to_all | solution.py:194
  23.8 0.0 all-gather.3.cloned.1.call-update
  23.8 1.3 collective-permute-start
  25.1 0.0 copy-done.5
  25.1 0.6 dynamic_slice.21
  26.8 0.0 copy-done.3
  26.8 0.1 reshape.17
  26.9 5.8 %collective-permute-done = bf16[2,64,1024]{2,1,0:T(8,128)(2,1)S(1)} collective-permute-done((bf16[2,64,1024]{2,1,0:T(8,128)(2,1)S(1)}, bf16[2,64,1024]{2,1,0:T(8,128)(2,1)S(1)}, u32[]{:S(2)}, u32[]{:S(2)}) %collective-permute-start) | collective-permute-done | bytes 262176 | tf_op jit(solution)/shard_map/ppermute | solution.py:199
  32.7 0.2 fusion
  32.9 11.2 %collective-permute-start.2 = (bf16[2,64,1024]{2,1,0:T(8,128)(2,1)S(1)}, bf16[2,64,1024]{2,1,0:T(8,128)(2,1)S(1)}, u32[]{:S(2)}, u32[]{:S(2)}) collective-permute-start(bf16[2,64,1024]{2,1,0:T(8,128)(2,1)S(1)} %fusion), channel_id=1, source_target_pairs={{0,256},{128,384},{256,0},{384,128},{1,257},{129,385},{257,1},{385... | collective-permute-start | bytes 786440 | tf_op jit(solution)/shard_map/ppermute | solution.py:204
  44.2 1.9 %collective-permute-start.1 = (bf16[2,64,1024]{2,1,0:T(8,128)(2,1)S(1)}, bf16[2,64,1024]{2,1,0:T(8,128)(2,1)S(1)}, u32[]{:S(2)}, u32[]{:S(2)}) collective-permute-start(bf16[2,64,1024]{2,1,0:T(8,128)(2,1)S(1)} %fusion), channel_id=1, source_target_pairs={{0,128},{128,256},{256,384},{384,0},{1,129},{129,257},{257,385},{3... | collective-permute-start | bytes 786440 | tf_op jit(solution)/shard_map/ppermute | solution.py:204
  46.1 4.6 %collective-permute-start.3 = (bf16[2,64,1024]{2,1,0:T(8,128)(2,1)S(1)}, bf16[2,64,1024]{2,1,0:T(8,128)(2,1)S(1)}, u32[]{:S(2)}, u32[]{:S(2)}) collective-permute-start(bf16[2,64,1024]{2,1,0:T(8,128)(2,1)S(1)} %fusion), channel_id=1, source_target_pairs={{0,384},{128,0},{256,128},{384,256},{1,385},{129,1},{257,129},{385... | collective-permute-start | bytes 786440 | tf_op jit(solution)/shard_map/ppermute | solution.py:204
  50.7 0.1 constant_dynamic-slice_fusion
  50.8 0.0 copy-done.4
  50.8 0.1 reshape.19
  50.8 0.2 dynamic-slice_reduce_fusion
  51.0 0.1 copy.11
  51.1 0.1 reshape.18
  51.2 0.0 copy-done.6
  51.2 0.1 dynamic_slice.20
  51.3 0.1 concatenate.6.info_ref
  51.4 0.0 collective-permute-done.2
  51.4 3.1 %collective-permute-done.1 = bf16[2,64,1024]{2,1,0:T(8,128)(2,1)S(1)} collective-permute-done((bf16[2,64,1024]{2,1,0:T(8,128)(2,1)S(1)}, bf16[2,64,1024]{2,1,0:T(8,128)(2,1)S(1)}, u32[]{:S(2)}, u32[]{:S(2)}) %collective-permute-start.1) | collective-permute-done | bytes 262176 | tf_op jit(solution)/shard_map/ppermute | solution.py:204
  54.5 0.0 collective-permute-done.3
  54.5 0.1 pad_maximum_fusion.window_ref
  54.6 0.0 copy-done.2
  54.6 5.9 %lag_kernels.1.kernel_ref = bf16[4,2,8,64,1024]{4,3,2,1,0:T(8,128)(2,1)} custom-call(bf16[4,2,64,1024]{3,2,1,0:T(8,128)(2,1)S(1)} %pad_maximum_fusion.window_ref, f32[2,8,512]{2,1,0:T(8,128)S(1)} %copy-done.2), custom_call_target="tpu_custom_call" | custom-call | tf_op jit(solution)/shard_map/lag_kernels/pallas_call | solution.py:106
  60.5 74.6 %all-gather.3.cloned.1.call-done = bf16[64,2,32,1024]{3,2,1,0:T(8,128)(2,1)} async-done(((bf16[4,2,32,1024]{3,2,1,0:T(8,128)(2,1)}), bf16[64,2,32,1024]{3,2,1,0:T(8,128)(2,1)}) %all-gather.3.cloned.1.call-update) | async-done | bytes 8388624 | tf_op jit(solution)/shard_map/all_gather | solution.py:195
  135.2 7.8 %correlate.1 = bf16[4,8,2,64,256]{4,3,2,1,0:T(8,128)(2,1)S(1)} custom-call(s32[71]{0:T(128)S(1)} %concatenate.6.info_ref, bf16[4,2,8,64,1024]{4,3,2,1,0:T(8,128)(2,1)} %lag_kernels.1.kernel_ref, bf16[16,4,2,32,1024]{4,3,2,1,0:T(8,128)(2,1)} %bitcast.14, bf16[16,4,2,32,1024]{4,3,2,1,0:T(8,128)(2,1)} %bitcast.15, bf16[16,4,2,32,1024]{4,3,2,1,0:T(8,128)(2,1)} %bitcast.16, ...), custom_call_target="tpu_custom_call" | custom-call | tf_op jit(solution)/shard_map/correlate/pallas_call | solution.py:142
  142.9 35.8 %all_to_all.11.parts_ref = bf16[32,2,64,256]{3,2,1,0:T(8,128)(2,1)S(1)} all-to-all(bf16[32,2,64,256]{3,2,1,0:T(8,128)(2,1)S(1)} %bitcast.13), channel_id=1, replica_groups=mesh['y'=4,'z'=16,'x'=4,'c'=2] {'y','x','c'}, dimensions={0} | all-to-all | bytes 4194304 | tf_op jit(solution)/shard_map/all_to_all | solution.py:214
  178.7 1.3 finish.1
  (1 shorter events, 0.0 us)
Async XLA Ops:
  6.5 128.6 %all-gather.3.cloned.1.call-start = ((), (), s32[]{:S(2)}) async-start(), calls=%async_computation.2 | async-start | bytes 8912896 | tf_op jit(solution)/shard_map/all_gather | solution.py:195
  6.5 1.6 copy-start
  8.1 1.2 copy-start.1
  9.4 15.8 %copy-start.5 = (s32[64]{0:T(128)S(1)}, s32[64]{0:T(128)}, u32[]{:S(2)}) copy-start(s32[64]{0:T(128)} %param.10) | copy-start | bytes 772
  9.4 17.5 %copy-start.3 = (s32[64,8]{0,1:T(8,128)S(1)}, s32[64,8]{0,1:T(8,128)}, u32[]{:S(2)}) copy-start(s32[64,8]{0,1:T(8,128)} %param.8) | copy-start | bytes 6148
  9.4 41.4 %copy-start.4 = (s32[64]{0:T(128)S(1)}, s32[64]{0:T(128)}, u32[]{:S(2)}) copy-start(s32[64]{0:T(128)} %param.9) | copy-start | bytes 772
  9.4 41.9 %copy-start.6 = (s32[16]{0:T(128)S(1)}, s32[16]{0:T(128)}, u32[]{:S(2)}) copy-start(s32[16]{0:T(128)} %param.11) | copy-start | bytes 196
  11.9 42.7 %copy-start.2 = (f32[2,8,512]{2,1,0:T(8,128)S(1)}, f32[2,8,512]{2,1,0:T(8,128)}, u32[]{:S(2)}) copy-start(f32[2,8,512]{2,1,0:T(8,128)} %constant.74.clone.lag_ref) | copy-start | bytes 98308
  23.8 8.9 %collective-permute-start = (bf16[2,64,1024]{2,1,0:T(8,128)(2,1)S(1)}, bf16[2,64,1024]{2,1,0:T(8,128)(2,1)S(1)}, u32[]{:S(2)}, u32[]{:S(2)}) collective-permute-start(bf16[2,64,1024]{2,1,0:T(8,128)(2,1)S(1)} %get-tuple-element.14), channel_id=1, source_target_pairs={{8,0},{16,8},{24,16},{32,24},{40,32},{48,40},{56,48},{64,56},{72,6... | collective-permute-start | bytes 786440 | tf_op jit(solution)/shard_map/ppermute | solution.py:199
  32.9 18.5 %collective-permute-start.2 = (bf16[2,64,1024]{2,1,0:T(8,128)(2,1)S(1)}, bf16[2,64,1024]{2,1,0:T(8,128)(2,1)S(1)}, u32[]{:S(2)}, u32[]{:S(2)}) collective-permute-start(bf16[2,64,1024]{2,1,0:T(8,128)(2,1)S(1)} %fusion), channel_id=1, source_target_pairs={{0,256},{128,384},{256,0},{384,128},{1,257},{129,385},{257,1},{385... | collective-permute-start | bytes 786440 | tf_op jit(solution)/shard_map/ppermute | solution.py:204
  44.2 10.3 %collective-permute-start.1 = (bf16[2,64,1024]{2,1,0:T(8,128)(2,1)S(1)}, bf16[2,64,1024]{2,1,0:T(8,128)(2,1)S(1)}, u32[]{:S(2)}, u32[]{:S(2)}) collective-permute-start(bf16[2,64,1024]{2,1,0:T(8,128)(2,1)S(1)} %fusion), channel_id=1, source_target_pairs={{0,128},{128,256},{256,384},{384,0},{1,129},{129,257},{257,385},{3... | collective-permute-start | bytes 786440 | tf_op jit(solution)/shard_map/ppermute | solution.py:204
  46.1 8.4 %collective-permute-start.3 = (bf16[2,64,1024]{2,1,0:T(8,128)(2,1)S(1)}, bf16[2,64,1024]{2,1,0:T(8,128)(2,1)S(1)}, u32[]{:S(2)}, u32[]{:S(2)}) collective-permute-start(bf16[2,64,1024]{2,1,0:T(8,128)(2,1)S(1)} %fusion), channel_id=1, source_target_pairs={{0,384},{128,0},{256,128},{384,256},{1,385},{129,1},{257,129},{385... | collective-permute-start | bytes 786440 | tf_op jit(solution)/shard_map/ppermute | solution.py:204
Sparse Core Ops, SparseCore 0:
  23.9 111.2 all-gather.2

commit v2 on v1

v2 whole, which is shorter than its diff:
```python
import jax
import jax.numpy as jnp
import numpy as np
from jax import lax
from jax.experimental import pallas as pl
from jax.experimental.pallas import tpu as pltpu
from jax.sharding import Mesh, PartitionSpec as P

CH = 128
SAMPLES = 2048
NF = 512
BAND = 32
K = 8
R_CH = 64
LAGS = 8
SLOTS = 2
F0 = 64
SEGS = 16
NY, NZ, NX, NC = 4, 16, 4, 2
G = 4
NH = NZ // G
NP = NY * G
SEG = 2
CQ = CH // NP
W = SLOTS * K * CQ
FB = 128
NB = NF // FB
KF = 2 * NF
EPS = 1e-06
NORM = np.float32((2.0 * NF * SEGS / SLOTS) ** (-0.5))
BF = jnp.bfloat16
F32 = jnp.float32
VMEM = 48 * 1024 * 1024


def transform_table():
    bins = F0 + np.arange(NF, dtype=np.int64)
    phase = (bins[:, None] * np.arange(SAMPLES // 2, dtype=np.int64)[None, :]) % SAMPLES
    steps = np.arange(SAMPLES, dtype=np.float32) * np.float32(2.0 * np.pi / SAMPLES)
    cos = np.cos(steps)[phase]
    sin = -np.sin(steps)[phase]
    return np.stack([cos, sin], axis=0).astype(jnp.bfloat16)


def lag_tables():
    bins = F0 + np.arange(NF, dtype=np.int64)
    lags = np.arange(LAGS, dtype=np.int64) - LAGS // 2
    phase = (lags[:, None] * bins[None, :]) % SAMPLES
    angle = phase.astype(np.float32) * np.float32(2.0 * np.pi / SAMPLES)
    return np.stack([np.cos(angle), np.sin(angle)], axis=0).astype(np.float32)


def whiten_kernel(traces_ref, table_ref, split_ref, low_ref, high_ref):
    half = SAMPLES // 2
    table = table_ref[...].reshape(2 * FB, half)
    early = jnp.concatenate([traces_ref[s, :half] for s in range(SEG)], axis=1)
    late = jnp.concatenate([traces_ref[s, half:] for s in range(SEG)], axis=1)
    early = jnp.dot(table, early, preferred_element_type=F32)
    late = jnp.dot(table, late, preferred_element_type=F32)
    odd = lax.broadcasted_iota(jnp.int32, late.shape, 0) % 2 == 1
    spectra = early + jnp.where(odd, -late, late)
    grouped = spectra.reshape(2, FB // BAND, BAND, SEG * CH)
    power = jnp.sum(grouped * grouped, axis=(0, 2)) * (1.0 / (2 * BAND))
    scale = 1.0 / jnp.sqrt(power + EPS)
    whitened = grouped * scale[None, :, None, :]
    flipped = whitened.reshape(2 * FB, SEG * CH).T
    for s in range(SEG):
        low_ref[s] = flipped[s * CH : s * CH + CH // 2].astype(BF)
        high_ref[s] = flipped[s * CH + CH // 2 : (s + 1) * CH].astype(BF)
        for r in range(NP):
            split_ref[r, s] = flipped[s * CH + r * CQ : s * CH + (r + 1) * CQ].astype(BF)


def whiten(traces, table):
    half = jax.ShapeDtypeStruct((SEG, CH // 2, KF), BF)
    half_spec = pl.BlockSpec((SEG, CH // 2, 2 * FB), lambda g: (0, 0, g))
    return pl.pallas_call(
        whiten_kernel,
        grid=(NB,),
        in_specs=[
            pl.BlockSpec((SEG, SAMPLES, CH), lambda g: (0, 0, 0)),
            pl.BlockSpec((2, FB, SAMPLES // 2), lambda g: (0, g, 0)),
        ],
        out_specs=[
            pl.BlockSpec((NP, SEG, CQ, 2 * FB), lambda g: (0, 0, 0, g)),
            half_spec,
            half_spec,
        ],
        out_shape=[jax.ShapeDtypeStruct((NP, SEG, CQ, KF), BF), half, half],
        compiler_params=pltpu.CompilerParams(vmem_limit_bytes=VMEM),
        name="whiten",
    )(traces, table)


def lag_kernel_body(window_ref, lag_ref, *refs):
    out_ref = refs[-1]
    for b in range(NB):
        at = b * 2 * FB
        real = window_ref[0, 0, :, at : at + FB].astype(F32)
        imag = window_ref[0, 0, :, at + FB : at + 2 * FB].astype(F32)
        for l in range(LAGS):
            cos = lag_ref[0, l : l + 1, b * FB : (b + 1) * FB]
            sin = lag_ref[1, l : l + 1, b * FB : (b + 1) * FB]
            for_real = (cos * real + sin * imag) * NORM
            for_imag = (cos * imag - sin * real) * NORM
            out_ref[0, 0, l, :, at : at + FB] = for_real.astype(BF)
            out_ref[0, 0, l, :, at + FB : at + 2 * FB] = for_imag.astype(BF)


def lag_kernels(d, windows, lags, kernels):
    earlier = [] if kernels is None else [kernels]
    return pl.pallas_call(
        lag_kernel_body,
        grid=(G, SEG),
        in_specs=[
            pl.BlockSpec((1, 1, R_CH, KF), lambda o, s: (o, s, 0, 0)),
            pl.BlockSpec((2, LAGS, NF), lambda o, s: (0, 0, 0)),
        ]
        + [pl.BlockSpec(memory_space=pl.ANY)] * len(earlier),
        out_specs=pl.BlockSpec((1, 1, LAGS, R_CH, KF), lambda o, s: (d * G + o, s, 0, 0, 0)),
        out_shape=jax.ShapeDtypeStruct((NP, SEG, LAGS, R_CH, KF), BF),
        input_output_aliases={2: 0} if earlier else {},
        compiler_params=pltpu.CompilerParams(vmem_limit_bytes=VMEM),
        name="lag_kernels",
    )(windows, lags, *earlier)


I_PIECE = NP * K
I_COUNT = 2 * NP * K
I_OWNER = I_COUNT + NP
I_SLOT = I_OWNER + NP
I_CORE = I_SLOT + SEG


def correlate_body(info_ref, kernel_ref, *refs):
    sources, keep_ref, send_ref = refs[:K], refs[K], refs[K + 1]
    o = pl.program_id(0)
    core = info_ref[I_CORE]
    total = 0.0
    for s in range(SEG):
        left = kernel_ref[0, s].reshape(LAGS * R_CH, KF)
        rows = []
        for q in range(SLOTS):
            for k in range(K):
                used = (k < info_ref[I_COUNT + o]) & (info_ref[I_SLOT + s] == q)
                rows.append(sources[k][0, 0, s].astype(F32) * used.astype(F32))
        right = jnp.concatenate(rows, axis=0).astype(BF)
        total = total + lax.dot_general(left, right, (((1,), (1,)), ((), ())), preferred_element_type=F32)
    total = total.reshape(NX, NC, R_CH, W)
    keep_ref[:, 0] = jnp.where(core == 0, total[:, 0], total[:, 1])
    send_ref[:, 0] = jnp.where(core == 0, total[:, 1], total[:, 0])


def correlate(info, kernels, gathered):
    def source_map(k):
        return lambda o, info: (info[o * K + k], info[I_PIECE + o * K + k], 0, 0, 0)

    out_spec = pl.BlockSpec((NX, 1, R_CH, W), lambda o, info: (0, info[I_OWNER + o], 0, 0))
    out = jax.ShapeDtypeStruct((NX, NP, R_CH, W), F32)
    return pl.pallas_call(
        correlate_body,
        grid_spec=pltpu.PrefetchScalarGridSpec(
            num_scalar_prefetch=1,
            grid=(NP,),
            in_specs=[pl.BlockSpec((1, SEG, LAGS, R_CH, KF), lambda o, info: (o, 0, 0, 0, 0))]
            + [pl.BlockSpec((1, 1, SEG, CQ, KF), source_map(k)) for k in range(K)],
            out_specs=[out_spec, out_spec],
        ),
        out_shape=[out, out],
        compiler_params=pltpu.CompilerParams(vmem_limit_bytes=VMEM),
        name="correlate",
    )(info, kernels, *([gathered] * K))


def finish_body(parts_ref, out_ref):
    pieces = [parts_ref[r].astype(F32) for r in range(NP)]
    for q in range(SLOTS):
        for k in range(K):
            at = (q * K + k) * CQ
            row = jnp.concatenate([v[:, at : at + CQ] for v in pieces], axis=1)
            out_ref[0, q, k] = row.astype(BF)


def finish(parts):
    return pl.pallas_call(
        finish_body,
        out_shape=jax.ShapeDtypeStruct((1, SLOTS, K, R_CH, CH), BF),
        compiler_params=pltpu.CompilerParams(vmem_limit_bytes=VMEM),
        name="finish",
    )(parts)


def around(size, distance):
    return [(i, (i + distance) % size) for i in range(size)]


def gather_planes(held):
    got = [held] + [None] * (NH - 1)
    ahead = behind = held
    for step in range(1, NH // 2):
        ahead = lax.ppermute(ahead, "zh", around(NH, 1))
        behind = lax.ppermute(behind, "zh", around(NH, -1))
        got[step], got[NH - step] = ahead, behind
    first = lax.ppermute(ahead[: NP // 2], "zh", around(NH, 1))
    second = lax.ppermute(behind[NP // 2 :], "zh", around(NH, -1))
    return got, first, second


def body(traces, source_list, source_count, receiver_start, segment_slot):
    y = lax.axis_index("y")
    zh = lax.axis_index("zh")
    zl = lax.axis_index("zl")
    t = lax.axis_index(("x", "c"))
    table = jnp.asarray(transform_table())
    lags = jnp.asarray(lag_tables())
    split, low, high = whiten(traces, table)
    pairs = NY * NZ
    following = lax.ppermute(low, ("y", "zh", "zl"), [(p, p - 1) for p in range(1, pairs)])
    crossed = lax.all_to_all(split, ("y", "zl"), 0, 0)

    joined = jnp.concatenate([high, following], axis=1)
    offset = lax.dynamic_index_in_dim(receiver_start, (y * NH + zh) * G + zl, keepdims=False) - CH // 2
    window = lax.dynamic_slice_in_dim(joined, offset, R_CH, 1)
    windows = jnp.stack([window] + [lax.ppermute(window, "zl", around(G, d)) for d in range(1, G)])
    crossed, windows = lax.optimization_barrier((crossed, windows))
    got, first, second = gather_planes(crossed)
    kernels = lag_kernels(0, windows, lags, None)
    for d in (1, 3, 2):
        kernels = lag_kernels(d, lax.ppermute(windows, "y", around(NY, d)), lags, kernels)

    kernels, first, second = lax.optimization_barrier((kernels, first, second))
    got[NH // 2] = jnp.concatenate([first, second], axis=0)
    gathered = jnp.stack(got)

    owner_y = jnp.repeat((y - jnp.arange(NY, dtype=jnp.int32)) % NY, G)
    owner_z = jnp.tile((zl - jnp.arange(G, dtype=jnp.int32)) % G, NY)
    owner = (owner_y * NH + zh) * G + owner_z
    lists = jnp.take(source_list, owner, axis=0).reshape(-1)
    counts = jnp.take(source_count, owner, axis=0)
    plane = lists % NZ
    place = (zh - plane // G) % NH
    piece = (lists // NZ) * G + plane % G
    slots = lax.dynamic_slice_in_dim(segment_slot, t * SEG, SEG, 0)
    core = lax.axis_index("c").astype(jnp.int32)[None]
    info = jnp.concatenate([place, piece, counts, owner_y * G + owner_z, slots, core]).astype(jnp.int32)
    keep, send = correlate(info, kernels, gathered)
    both = (keep + lax.ppermute(send, "c", around(NC, 1))).astype(BF)
    parts = lax.all_to_all(both, "x", 0, 0)
    total = jnp.sum(parts.astype(F32), axis=0).astype(BF)
    return finish(lax.all_to_all(total, ("y", "zl"), 0, 0))


def solution(mesh):
    grid = Mesh(mesh.devices.reshape(NY, NH, G, NX, NC), ("y", "zh", "zl", "x", "c"))
    tm, pair = ("x", "c"), ("y", "zh", "zl")
    return jax.shard_map(
        body,
        mesh=grid,
        in_specs=(P(tm, None, pair), P(), P(), P(), P()),
        out_specs=P(tm, None, pair, None, None),
        check_vma=False,
    )
```

time: 187 us -> 230 us (1.23); the launches traced: 187 us -> 227 us
  starting transfers between devices: 19 us -> 80.8 us
  waiting for transfers between devices: 83.6 us -> 46 us
  Pallas kernels: 17.5 us -> 53.1 us
  blocking collectives: 47.6 us -> 32.7 us
  between operations: 14.6 us -> 1.6 us
  other arithmetic: 0.33 us -> 5.02 us
  local copies, waits for them, and re-layouts: 4.19 us -> 7.97 us
    all_gather x1 -> x0, waiting for transfers between devices: 74.6 us -> none  [body(): gathered = lax.all_gather(crossed, 'z', axis=0, tiled=False)]
    ppermute x4 -> x12, starting transfers between devices: 19 us -> 71.5 us  [the longest x1 27.2 us: body(): both = (keep + lax.ppermute(send, 'c', around(NC, 1))).astype(BF)]
    ppermute x4 -> x12, waiting for transfers between devices: 8.91 us -> 46 us  [the longest x1 12.3 us: body(): lax.ppermute(low, ('y', 'zh', 'zl'), [(p, p - 1) for p in range(1, pairs)])]
    pallas_call x2 -> x5, Pallas kernels: 7.2 us -> 26.9 us  [the longest x4 25.1 us: lag_kernels(): pl.pallas_call(lag_kernel_body, grid=(G, SEG), in_specs=[pl.BlockSpec((1,...]
    pallas_call x1, Pallas kernels: 7.77 us -> 23 us  [correlate(): pl.pallas_call(correlate_body, grid_spec=pltpu.PrefetchScalarGridSpec(num...]
    all_to_all x2, blocking collectives: 47.6 us -> 32.7 us  [the longest x1 18 us: body(): parts = lax.all_to_all(both, 'x', 0, 0)]
    all_to_all x0 -> x1, starting transfers between devices: none -> 9.31 us  [body(): crossed = lax.all_to_all(split, ('y', 'zl'), 0, 0)]
    another operation x1 -> x3, other arithmetic: 0.13 us -> 3.97 us  [the longest x2 3.84 us: body(): gathered = jnp.stack(got)]
  transfers between devices with their start and end apart: 5 -> 13, of which waited for: 3 -> 6; matrix products, arithmetic and copies ran while one was open for 1% -> 2% of each run, Pallas kernels for 3% -> 11%
where the time goes in v2:
time: 230 us; the launch traced here: 227 us
  starting transfers between devices  80.8 us (35%)
  Pallas kernels  53.1 us (23%)
  waiting for transfers between devices  46 us (20%)
  blocking collectives  32.7 us (14%)
  local copies, waits for them, and re-layouts  7.97 us (3%)
  other arithmetic  5.02 us (2%)
    ppermute x1, starting transfers between devices, body(): both = (keep + lax.ppermute(send, 'c', around(NC, 1))).astype(BF)  27.2 us
    pallas_call x4, Pallas kernels, lag_kernels(): pl.pallas_call(lag_kernel_body, grid=(G, SEG), in_specs=[pl.BlockSpec((1,...  25.1 us
    pallas_call x1, Pallas kernels, correlate(): pl.pallas_call(correlate_body, grid_spec=pltpu.PrefetchScalarGridSpec(num...  23 us
    all_to_all x1, blocking collectives, body(): parts = lax.all_to_all(both, 'x', 0, 0)  18 us
    all_to_all x1, blocking collectives, body(): return finish(lax.all_to_all(total, ('y', 'zl'), 0, 0))  14.7 us
    ppermute x1, waiting for transfers between devices, body(): lax.ppermute(low, ('y', 'zh', 'zl'), [(p, p - 1) for p in range(1, pairs)])  12.3 us
    ppermute x3, starting transfers between devices, body(): lax.ppermute(window, 'zl', around(G, d))  12 us
    ppermute x3, starting transfers between devices, body(): lax.ppermute(windows, 'y', around(NY, d))  11.2 us
  transfers between devices with their start and end apart: 13, of which 6 were waited for; matrix products, arithmetic and copies ran while one was open for 2% of the time, Pallas kernels for 11%

profile of v2, /device:TPU:1, one launch (start us, length us, event | category | flops | bytes accessed | tf_op | source)
XLA Modules:
  0.0 227.2 jit_solution(11816332058220967542)
XLA Ops:
  0.0 0.0 copy-start
  0.0 1.6 copy-done.1
  1.6 1.2 copy-done.2
  2.8 3.1 %whiten.1 = (bf16[16,2,8,1024]{3,2,1,0:T(8,128)(2,1)}, bf16[2,64,1024]{2,1,0:T(8,128)(2,1)S(1)}, bf16[2,64,1024]{2,1,0:T(8,128)(2,1)S(1)}) custom-call(bf16[2,2048,128]{2,1,0:T(8,128)(2,1)S(1)} %copy-done.2, bf16[2,512,1024]{2,1,0:T(8,128)(2,1)S(1)} %copy-done.1), custom_call_target="tpu_custom_call" | custom-call | tf_op jit(solution)/shard_map/whiten/pallas_call | solution.py:77
  6.0 9.3 %all-to-all-start = ((bf16[16,2,8,1024]{3,2,1,0:T(8,128)(2,1)}), bf16[16,2,8,1024]{3,2,1,0:T(8,128)(2,1)S(1)}, u32[]{:S(2)}, u32[]{:S(2)}) async-start(bf16[16,2,8,1024]{3,2,1,0:T(8,128)(2,1)} %get-tuple-element.15), calls=%async_computation | async-start | bytes 1048576 | tf_op jit(solution)/shard_map/all_to_all | solution.py:219
  15.3 1.3 collective-permute-start
  16.6 0.0 copy-done.7
  16.6 0.6 dynamic_slice.11
  18.5 12.3 %collective-permute-done = bf16[2,64,1024]{2,1,0:T(8,128)(2,1)S(1)} collective-permute-done((bf16[2,64,1024]{2,1,0:T(8,128)(2,1)S(1)}, bf16[2,64,1024]{2,1,0:T(8,128)(2,1)S(1)}, u32[]{:S(2)}, u32[]{:S(2)}) %collective-permute-start) | collective-permute-done | bytes 262176 | tf_op jit(solution)/shard_map/ppermute | solution.py:218
  30.9 0.2 fusion
  31.1 0.0 copy-start.8
  31.1 0.0 copy-start.3
  31.1 6.1 %collective-permute-start.1 = (bf16[2,64,1024]{2,1,0:T(8,128)(2,1)S(1)}, bf16[2,64,1024]{2,1,0:T(8,128)(2,1)S(1)}, u32[]{:S(2)}, u32[]{:S(2)}) collective-permute-start(bf16[2,64,1024]{2,1,0:T(8,128)(2,1)S(1)} %fusion), channel_id=1, source_target_pairs={{0,8},{8,16},{16,24},{24,0},{1,9},{9,17},{17,25},{25,1},{2,10},{10... | collective-permute-start | bytes 786440 | tf_op jit(solution)/shard_map/ppermute | solution.py:224
  37.2 1.9 collective-permute-start.2
  39.2 4.0 %collective-permute-start.3 = (bf16[2,64,1024]{2,1,0:T(8,128)(2,1)S(1)}, bf16[2,64,1024]{2,1,0:T(8,128)(2,1)S(1)}, u32[]{:S(2)}, u32[]{:S(2)}) collective-permute-start(bf16[2,64,1024]{2,1,0:T(8,128)(2,1)S(1)} %fusion), channel_id=1, source_target_pairs={{0,24},{8,0},{16,8},{24,16},{1,25},{9,1},{17,9},{25,17},{2,26},{10... | collective-permute-start | bytes 786440 | tf_op jit(solution)/shard_map/ppermute | solution.py:224
  43.2 0.1 broadcast_add_fusion
  43.2 0.1 add.129
  43.3 0.0 collective-permute-done.1
  43.3 11.0 %collective-permute-done.2 = bf16[2,64,1024]{2,1,0:T(8,128)(2,1)S(1)} collective-permute-done((bf16[2,64,1024]{2,1,0:T(8,128)(2,1)S(1)}, bf16[2,64,1024]{2,1,0:T(8,128)(2,1)S(1)}, u32[]{:S(2)}, u32[]{:S(2)}) %collective-permute-start.2) | collective-permute-done | bytes 262176 | tf_op jit(solution)/shard_map/ppermute | solution.py:224
  54.3 0.0 collective-permute-done.3
  54.3 0.1 pad_maximum_fusion.1.window_ref
  54.4 0.0 all-to-all-done
  54.4 0.0 copy-start.4
  54.5 4.1 %collective-permute-start.6 = (bf16[4,2,64,1024]{3,2,1,0:T(8,128)(2,1)S(1)}, bf16[4,2,64,1024]{3,2,1,0:T(8,128)(2,1)}, u32[]{:S(2)}, u32[]{:S(2)}) collective-permute-start(bf16[4,2,64,1024]{3,2,1,0:T(8,128)(2,1)S(1)} %pad_maximum_fusion.1.window_ref), channel_id=1, source_target_pairs={{0,128},{128,256},{256,384},{384,0},{1,129},{129,257},{257,385},{3... | collective-permute-start | bytes 3145736 | tf_op jit(solution)/shard_map/ppermute | solution.py:229
  58.5 0.0 copy-done.4
  58.5 3.3 %collective-permute-start.5 = (bf16[4,2,64,1024]{3,2,1,0:T(8,128)(2,1)S(1)}, bf16[4,2,64,1024]{3,2,1,0:T(8,128)(2,1)S(1)}, u32[]{:S(2)}, u32[]{:S(2)}) collective-permute-start(bf16[4,2,64,1024]{3,2,1,0:T(8,128)(2,1)S(1)} %pad_maximum_fusion.1.window_ref), channel_id=1, source_target_pairs={{0,384},{128,0},{256,128},{384,256},{1,385},{129,1},{257,129},{385... | collective-permute-start | bytes 3145736 | tf_op jit(solution)/shard_map/ppermute | solution.py:229
  61.9 3.8 %collective-permute-start.4 = (bf16[4,2,64,1024]{3,2,1,0:T(8,128)(2,1)S(1)}, bf16[4,2,64,1024]{3,2,1,0:T(8,128)(2,1)S(1)}, u32[]{:S(2)}, u32[]{:S(2)}) collective-permute-start(bf16[4,2,64,1024]{3,2,1,0:T(8,128)(2,1)S(1)} %pad_maximum_fusion.1.window_ref), channel_id=1, source_target_pairs={{0,256},{128,384},{256,0},{384,128},{1,257},{129,385},{257,1},{385... | collective-permute-start | bytes 3145736 | tf_op jit(solution)/shard_map/ppermute | solution.py:229
  65.7 0.1 tile.10
  65.8 0.1 broadcast_in_dim.20
  65.8 0.1 mul.52
  65.9 0.1 copy.12
  66.0 8.5 %collective-permute-start.9 = (bf16[16,2,8,1024]{3,2,1,0:T(8,128)(2,1)}, bf16[16,2,8,1024]{3,2,1,0:T(8,128)(2,1)}, u32[]{:S(2)}, u32[]{:S(2)}) collective-permute-start(bf16[16,2,8,1024]{3,2,1,0:T(8,128)(2,1)} %copy-done.4), channel_id=1, source_target_pairs={{0,96},{32,0},{64,32},{96,64},{1,97},{33,1},{65,33},{97,65},{2,98}... | collective-permute-start | bytes 1572872 | tf_op jit(solution)/shard_map/ppermute | solution.py:202
  74.5 1.9 collective-permute-start.7
  76.5 0.7 gather_fusion.1
  77.1 0.6 gather_fusion
  77.7 0.1 broadcast_select_fusion
  77.8 0.1 select_n.82
  77.9 7.1 %collective-permute-done.9 = bf16[16,2,8,1024]{3,2,1,0:T(8,128)(2,1)} collective-permute-done((bf16[16,2,8,1024]{3,2,1,0:T(8,128)(2,1)}, bf16[16,2,8,1024]{3,2,1,0:T(8,128)(2,1)}, u32[]{:S(2)}, u32[]{:S(2)}) %collective-permute-start.9) | collective-permute-done | bytes 524320 | tf_op jit(solution)/shard_map/ppermute | solution.py:202
  85.0 1.0 slice.13
  86.0 7.5 %collective-permute-start.10 = (bf16[8,2,8,1024]{3,2,1,0:T(8,128)(2,1)S(1)}, bf16[8,2,8,1024]{3,2,1,0:T(8,128)(2,1)}, u32[]{:S(2)}, u32[]{:S(2)}) collective-permute-start(bf16[8,2,8,1024]{3,2,1,0:T(8,128)(2,1)S(1)} %slice.13), channel_id=1, source_target_pairs={{0,96},{32,0},{64,32},{96,64},{1,97},{33,1},{65,33},{97,65},{2,98}... | collective-permute-start | bytes 786440 | tf_op jit(solution)/shard_map/ppermute | solution.py:205
  93.5 0.0 collective-permute-done.7
  93.5 1.7 slice.12
  95.1 1.9 collective-permute-start.8
  97.1 0.1 dynamic_slice.10
  97.2 0.1 concatenate.9.info_ref
  97.3 5.8 %lag_kernels.4.refs_0_ = bf16[16,2,8,64,1024]{4,3,2,1,0:T(8,128)(2,1)} custom-call(bf16[4,2,64,1024]{3,2,1,0:T(8,128)(2,1)S(1)} %pad_maximum_fusion.1.window_ref, f32[2,8,512]{2,1,0:T(8,128)S(1)} %copy-done.3), custom_call_target="tpu_custom_call" | custom-call | tf_op jit(solution)/shard_map/lag_kernels/pallas_call | solution.py:112
  103.1 0.0 collective-permute-done.6.window_ref
  103.1 7.6 %lag_kernels.5.refs_0_ = bf16[16,2,8,64,1024]{4,3,2,1,0:T(8,128)(2,1)} custom-call(bf16[4,2,64,1024]{3,2,1,0:T(8,128)(2,1)} %collective-permute-done.6.window_ref, f32[2,8,512]{2,1,0:T(8,128)S(1)} %copy-done.3, bf16[16,2,8,64,1024]{4,3,2,1,0:T(8,128)(2,1)} %lag_kernels.4.refs_0_), custom_call_target="tpu_custom_call", output_to_operand_aliasing={{}: (2, {})} | custom-call | tf_op jit(solution)/shard_map/lag_kernels/pallas_call | solution.py:112
  110.7 0.0 collective-permute-done.5.window_ref
  110.7 5.9 %lag_kernels.6.refs_0_ = bf16[16,2,8,64,1024]{4,3,2,1,0:T(8,128)(2,1)} custom-call(bf16[4,2,64,1024]{3,2,1,0:T(8,128)(2,1)S(1)} %collective-permute-done.5.window_ref, f32[2,8,512]{2,1,0:T(8,128)S(1)} %copy-done.3, bf16[16,2,8,64,1024]{4,3,2,1,0:T(8,128)(2,1)} %lag_kernels.5.refs_0_), custom_call_target="tpu_custom_call", output_to_operand_aliasing={{}: (2, {})} | custom-call | tf_op jit(solution)/shard_map/lag_kernels/pallas_call | solution.py:112
  116.6 0.0 collective-permute-done.4.window_ref
  116.6 5.8 %lag_kernels.7.kernel_ref = bf16[16,2,8,64,1024]{4,3,2,1,0:T(8,128)(2,1)} custom-call(bf16[4,2,64,1024]{3,2,1,0:T(8,128)(2,1)S(1)} %collective-permute-done.4.window_ref, f32[2,8,512]{2,1,0:T(8,128)S(1)} %copy-done.3, bf16[16,2,8,64,1024]{4,3,2,1,0:T(8,128)(2,1)} %lag_kernels.6.refs_0_), custom_call_target="tpu_custom_call", output_to_operand_aliasing={{}: (2, {})} | custom-call | tf_op jit(solution)/shard_map/lag_kernels/pallas_call | solution.py:112
  122.4 5.2 %collective-permute-done.10 = bf16[8,2,8,1024]{3,2,1,0:T(8,128)(2,1)} collective-permute-done((bf16[8,2,8,1024]{3,2,1,0:T(8,128)(2,1)S(1)}, bf16[8,2,8,1024]{3,2,1,0:T(8,128)(2,1)}, u32[]{:S(2)}, u32[]{:S(2)}) %collective-permute-start.10) | collective-permute-done | bytes 262176 | tf_op jit(solution)/shard_map/ppermute | solution.py:205
  127.6 6.6 %collective-permute-done.8 = bf16[8,2,8,1024]{3,2,1,0:T(8,128)(2,1)} collective-permute-done((bf16[8,2,8,1024]{3,2,1,0:T(8,128)(2,1)}, bf16[8,2,8,1024]{3,2,1,0:T(8,128)(2,1)}, u32[]{:S(2)}, u32[]{:S(2)}) %collective-permute-start.8) | collective-permute-done | bytes 262176 | tf_op jit(solution)/shard_map/ppermute | solution.py:204
  134.2 1.1 maximum_bitcast_fusion
  135.3 2.8 %pad_maximum_fusion.refs_0_.refs_1_.refs_2_.refs_3_.refs_4_.refs_5_.refs_6_.refs_7_ = bf16[4,16,2,8,1024]{4,3,2,1,0:T(8,128)(2,1)} fusion(bf16[1,16,2,8,1024]{4,3,2,1,0:T(8,128)(2,1)} %bitcast.11, bf16[1,16,2,8,1024]{4,3,2,1,0:T(8,128)(2,1)S(1)} %maximum_bitcast_fusion, bf16[1,16,2,8,1024]{4,3,2,1,0:T(8,128)(2,1)} %bitcast.9, ...), kind=kLoop, calls=%fused_computation.2 | loop fusion | flops 3145728 | bytes 4194304 | tf_op jit(solution)/shard_map/stack | solution.py:233
  138.0 23.0 %correlate.1 = (f32[4,16,64,128]{3,2,1,0:T(8,128)S(1)}, f32[4,16,64,128]{3,2,1,0:T(8,128)S(1)}) custom-call(s32[291]{0:T(512)S(1)} %concatenate.9.info_ref, bf16[16,2,8,64,1024]{4,3,2,1,0:T(8,128)(2,1)} %lag_kernels.7.kernel_ref, bf16[4,16,2,8,1024]{4,3,2,1,0:T(8,128)(2,1)} %pad_maximum_fusion.refs_0_.refs_1_.refs_2_.refs_3_.refs_4_.refs_5_.refs_6_.refs_7_, ...), custom_call_target="tpu_custom_call" | custom-call | tf_op jit(solution)/shard_map/correlate/pallas_call | solution.py:160
  161.1 27.2 %collective-permute-start.11 = (f32[4,16,64,128]{3,2,1,0:T(8,128)S(1)}, f32[4,16,64,128]{3,2,1,0:T(8,128)S(1)}, u32[]{:S(2)}, u32[]{:S(2)}) collective-permute-start(f32[4,16,64,128]{3,2,1,0:T(8,128)S(1)} %get-tuple-element.24), channel_id=1, source_target_pairs={{0,1},{1,0},{2,3},{3,2},{4,5},{5,4},{6,7},{7,6},{8,9},{9,8},{10,11... | collective-permute-start | bytes 6291464 | tf_op jit(solution)/shard_map/ppermute | solution.py:247
  188.3 3.8 %collective-permute-done.11 = f32[4,16,64,128]{3,2,1,0:T(8,128)S(1)} collective-permute-done((f32[4,16,64,128]{3,2,1,0:T(8,128)S(1)}, f32[4,16,64,128]{3,2,1,0:T(8,128)S(1)}, u32[]{:S(2)}, u32[]{:S(2)}) %collective-permute-start.11) | collective-permute-done | bytes 2097184 | tf_op jit(solution)/shard_map/ppermute | solution.py:247
  192.1 0.4 add_convert_fusion
  192.5 18.0 %all_to_all.15 = bf16[4,16,64,128]{3,2,1,0:T(8,128)(2,1)S(1)} all-to-all(bf16[4,16,64,128]{3,2,1,0:T(8,128)(2,1)S(1)} %add_convert_fusion), channel_id=1, replica_groups=mesh['y'=4,'zh'=4,'zl'=4,'x'=4,'c'=2] {'x'}, dimensions={0} | all-to-all | bytes 2097152 | tf_op jit(solution)/shard_map/all_to_all | solution.py:248
  210.6 0.2 reduce_sum.12
  210.8 14.7 %all_to_all.16.parts_ref = bf16[16,64,128]{2,1,0:T(8,128)(2,1)S(1)} all-to-all(bf16[16,64,128]{2,1,0:T(8,128)(2,1)S(1)} %reduce_sum.12), channel_id=1, replica_groups=mesh['y'=4,'zh'=4,'zl'=4,'x'=4,'c'=2] {'y','zl'}, dimensions={0} | all-to-all | bytes 524288 | tf_op jit(solution)/shard_map/all_to_all | solution.py:250
  225.5 1.8 finish.1
  (18 shorter events, 0.1 us)
Async XLA Ops:
  0.0 76.5 %copy-start = (s32[64]{0:T(128)S(1)}, s32[64]{0:T(128)}, u32[]{:S(2)}) copy-start(s32[64]{0:T(128)} %param.9) | copy-start | bytes 772
  0.0 1.6 copy-start.1
  1.6 1.2 copy-start.2
  2.8 13.8 %copy-start.7 = (s32[64]{0:T(128)S(1)}, s32[64]{0:T(128)}, u32[]{:S(2)}) copy-start(s32[64]{0:T(128)} %param.10) | copy-start | bytes 772
  6.0 59.9 %copy-start.6 = (s32[64,8]{0,1:T(8,128)S(1)}, s32[64,8]{0,1:T(8,128)}, u32[]{:S(2)}) copy-start(s32[64,8]{0,1:T(8,128)} %param.8) | copy-start | bytes 6148
  6.0 48.5 %all-to-all-start = ((bf16[16,2,8,1024]{3,2,1,0:T(8,128)(2,1)}), bf16[16,2,8,1024]{3,2,1,0:T(8,128)(2,1)S(1)}, u32[]{:S(2)}, u32[]{:S(2)}) async-start(bf16[16,2,8,1024]{3,2,1,0:T(8,128)(2,1)} %get-tuple-element.15), calls=%async_computation | async-start | bytes 1048576 | tf_op jit(solution)/shard_map/all_to_all | solution.py:219
  15.3 15.6 %collective-permute-start = (bf16[2,64,1024]{2,1,0:T(8,128)(2,1)S(1)}, bf16[2,64,1024]{2,1,0:T(8,128)(2,1)S(1)}, u32[]{:S(2)}, u32[]{:S(2)}) collective-permute-start(bf16[2,64,1024]{2,1,0:T(8,128)(2,1)S(1)} %get-tuple-element.17), channel_id=1, source_target_pairs={{8,0},{16,8},{24,16},{32,24},{40,32},{48,40},{56,48},{64,56},{72,6... | collective-permute-start | bytes 786440 | tf_op jit(solution)/shard_map/ppermute | solution.py:218
  31.1 66.0 %copy-start.8 = (s32[16]{0:T(128)S(1)}, s32[16]{0:T(128)}, u32[]{:S(2)}) copy-start(s32[16]{0:T(128)} %param.11) | copy-start | bytes 196
  31.1 66.2 %copy-start.3 = (f32[2,8,512]{2,1,0:T(8,128)S(1)}, f32[2,8,512]{2,1,0:T(8,128)}, u32[]{:S(2)}) copy-start(f32[2,8,512]{2,1,0:T(8,128)} %constant.135.clone.lag_ref) | copy-start | bytes 98308
  31.1 12.2 %collective-permute-start.1 = (bf16[2,64,1024]{2,1,0:T(8,128)(2,1)S(1)}, bf16[2,64,1024]{2,1,0:T(8,128)(2,1)S(1)}, u32[]{:S(2)}, u32[]{:S(2)}) collective-permute-start(bf16[2,64,1024]{2,1,0:T(8,128)(2,1)S(1)} %fusion), channel_id=1, source_target_pairs={{0,8},{8,16},{16,24},{24,0},{1,9},{9,17},{17,25},{25,1},{2,10},{10... | collective-permute-start | bytes 786440 | tf_op jit(solution)/shard_map/ppermute | solution.py:224
  37.2 17.1 %collective-permute-start.2 = (bf16[2,64,1024]{2,1,0:T(8,128)(2,1)S(1)}, bf16[2,64,1024]{2,1,0:T(8,128)(2,1)S(1)}, u32[]{:S(2)}, u32[]{:S(2)}) collective-permute-start(bf16[2,64,1024]{2,1,0:T(8,128)(2,1)S(1)} %fusion), channel_id=1, source_target_pairs={{0,16},{8,24},{16,0},{24,8},{1,17},{9,25},{17,1},{25,9},{2,18},{10... | collective-permute-start | bytes 786440 | tf_op jit(solution)/shard_map/ppermute | solution.py:224
  39.2 15.1 %collective-permute-start.3 = (bf16[2,64,1024]{2,1,0:T(8,128)(2,1)S(1)}, bf16[2,64,1024]{2,1,0:T(8,128)(2,1)S(1)}, u32[]{:S(2)}, u32[]{:S(2)}) collective-permute-start(bf16[2,64,1024]{2,1,0:T(8,128)(2,1)S(1)} %fusion), channel_id=1, source_target_pairs={{0,24},{8,0},{16,8},{24,16},{1,25},{9,1},{17,9},{25,17},{2,26},{10... | collective-permute-start | bytes 786440 | tf_op jit(solution)/shard_map/ppermute | solution.py:224
  54.4 4.1 %copy-start.4 = (bf16[16,2,8,1024]{3,2,1,0:T(8,128)(2,1)}, bf16[16,2,8,1024]{3,2,1,0:T(8,128)(2,1)S(1)}, u32[]{:S(2)}) copy-start(bf16[16,2,8,1024]{3,2,1,0:T(8,128)(2,1)S(1)} %all-to-all-done) | copy-start | bytes 1572868
  54.5 48.7 %collective-permute-start.6 = (bf16[4,2,64,1024]{3,2,1,0:T(8,128)(2,1)S(1)}, bf16[4,2,64,1024]{3,2,1,0:T(8,128)(2,1)}, u32[]{:S(2)}, u32[]{:S(2)}) collective-permute-start(bf16[4,2,64,1024]{3,2,1,0:T(8,128)(2,1)S(1)} %pad_maximum_fusion.1.window_ref), channel_id=1, source_target_pairs={{0,128},{128,256},{256,384},{384,0},{1,129},{129,257},{257,385},{3... | collective-permute-start | bytes 3145736 | tf_op jit(solution)/shard_map/ppermute | solution.py:229
  58.5 52.2 %collective-permute-start.5 = (bf16[4,2,64,1024]{3,2,1,0:T(8,128)(2,1)S(1)}, bf16[4,2,64,1024]{3,2,1,0:T(8,128)(2,1)S(1)}, u32[]{:S(2)}, u32[]{:S(2)}) collective-permute-start(bf16[4,2,64,1024]{3,2,1,0:T(8,128)(2,1)S(1)} %pad_maximum_fusion.1.window_ref), channel_id=1, source_target_pairs={{0,384},{128,0},{256,128},{384,256},{1,385},{129,1},{257,129},{385... | collective-permute-start | bytes 3145736 | tf_op jit(solution)/shard_map/ppermute | solution.py:229
  61.9 54.7 %collective-permute-start.4 = (bf16[4,2,64,1024]{3,2,1,0:T(8,128)(2,1)S(1)}, bf16[4,2,64,1024]{3,2,1,0:T(8,128)(2,1)S(1)}, u32[]{:S(2)}, u32[]{:S(2)}) collective-permute-start(bf16[4,2,64,1024]{3,2,1,0:T(8,128)(2,1)S(1)} %pad_maximum_fusion.1.window_ref), channel_id=1, source_target_pairs={{0,256},{128,384},{256,0},{384,128},{1,257},{129,385},{257,1},{385... | collective-permute-start | bytes 3145736 | tf_op jit(solution)/shard_map/ppermute | solution.py:229
  66.0 19.0 %collective-permute-start.9 = (bf16[16,2,8,1024]{3,2,1,0:T(8,128)(2,1)}, bf16[16,2,8,1024]{3,2,1,0:T(8,128)(2,1)}, u32[]{:S(2)}, u32[]{:S(2)}) collective-permute-start(bf16[16,2,8,1024]{3,2,1,0:T(8,128)(2,1)} %copy-done.4), channel_id=1, source_target_pairs={{0,96},{32,0},{64,32},{96,64},{1,97},{33,1},{65,33},{97,65},{2,98}... | collective-permute-start | bytes 1572872 | tf_op jit(solution)/shard_map/ppermute | solution.py:202
  74.5 19.0 %collective-permute-start.7 = (bf16[16,2,8,1024]{3,2,1,0:T(8,128)(2,1)}, bf16[16,2,8,1024]{3,2,1,0:T(8,128)(2,1)}, u32[]{:S(2)}, u32[]{:S(2)}) collective-permute-start(bf16[16,2,8,1024]{3,2,1,0:T(8,128)(2,1)} %copy-done.4), channel_id=1, source_target_pairs={{0,32},{32,64},{64,96},{96,0},{1,33},{33,65},{65,97},{97,1},{2,34}... | collective-permute-start | bytes 1572872 | tf_op jit(solution)/shard_map/ppermute | solution.py:201
  86.0 41.6 %collective-permute-start.10 = (bf16[8,2,8,1024]{3,2,1,0:T(8,128)(2,1)S(1)}, bf16[8,2,8,1024]{3,2,1,0:T(8,128)(2,1)}, u32[]{:S(2)}, u32[]{:S(2)}) collective-permute-start(bf16[8,2,8,1024]{3,2,1,0:T(8,128)(2,1)S(1)} %slice.13), channel_id=1, source_target_pairs={{0,96},{32,0},{64,32},{96,64},{1,97},{33,1},{65,33},{97,65},{2,98}... | collective-permute-start | bytes 786440 | tf_op jit(solution)/shard_map/ppermute | solution.py:205
  95.1 39.0 %collective-permute-start.8 = (bf16[8,2,8,1024]{3,2,1,0:T(8,128)(2,1)}, bf16[8,2,8,1024]{3,2,1,0:T(8,128)(2,1)}, u32[]{:S(2)}, u32[]{:S(2)}) collective-permute-start(bf16[8,2,8,1024]{3,2,1,0:T(8,128)(2,1)} %slice.12), channel_id=1, source_target_pairs={{0,32},{32,64},{64,96},{96,0},{1,33},{33,65},{65,97},{97,1},{2,34}... | collective-permute-start | bytes 786440 | tf_op jit(solution)/shard_map/ppermute | solution.py:204
  116.6 18.7 %copy-start.5 = (bf16[16,2,8,1024]{3,2,1,0:T(8,128)(2,1)S(1)}, bf16[16,2,8,1024]{3,2,1,0:T(8,128)(2,1)}, u32[]{:S(2)}) copy-start(bf16[16,2,8,1024]{3,2,1,0:T(8,128)(2,1)} %copy-done.4) | copy-start | bytes 1572868
  161.1 31.0 %collective-permute-start.11 = (f32[4,16,64,128]{3,2,1,0:T(8,128)S(1)}, f32[4,16,64,128]{3,2,1,0:T(8,128)S(1)}, u32[]{:S(2)}, u32[]{:S(2)}) collective-permute-start(f32[4,16,64,128]{3,2,1,0:T(8,128)S(1)} %get-tuple-element.24), channel_id=1, source_target_pairs={{0,1},{1,0},{2,3},{3,2},{4,5},{5,4},{6,7},{7,6},{8,9},{9,8},{10,11... | collective-permute-start | bytes 6291464 | tf_op jit(solution)/shard_map/ppermute | solution.py:247

commit v3 on v1

--- a/solution.py
+++ b/solution.py
@@ -26,7 +26,7 @@
 NORM = np.float32((2.0 * NF * SEGS / SLOTS) ** (-0.5))
 BF = jnp.bfloat16
 F32 = jnp.float32
-VMEM = 48 * 1024 * 1024
+MIB = 1024 * 1024
 
 
 def transform_table():
@@ -83,7 +83,7 @@
             half_spec,
         ],
         out_shape=[jax.ShapeDtypeStruct((NY, SEG, CQ, KF), BF), half, half],
-        compiler_params=pltpu.CompilerParams(vmem_limit_bytes=VMEM),
+        compiler_params=pltpu.CompilerParams(vmem_limit_bytes=448 * MIB),
         name="whiten",
     )(traces, table)
 
@@ -112,7 +112,7 @@
         ],
         out_specs=pl.BlockSpec((1, 1, LAGS, R_CH, KF), lambda o, s: (o, s, 0, 0, 0)),
         out_shape=jax.ShapeDtypeStruct((NY, SEG, LAGS, R_CH, KF), BF),
-        compiler_params=pltpu.CompilerParams(vmem_limit_bytes=VMEM),
+        compiler_params=pltpu.CompilerParams(vmem_limit_bytes=48 * MIB),
         name="lag_kernels",
     )(windows, lags)
 
@@ -120,22 +120,21 @@
 def correlate_body(info_ref, kernel_ref, *refs):
     sources, out_ref = refs[:K], refs[K]
     o = pl.program_id(0)
-    count = info_ref[64 + o]
     lane = lax.broadcasted_iota(jnp.int32, (1, K * CQ), 1)
-    live = (lane < count * CQ).astype(F32)
+    live = (lane < info_ref[64 + o] * CQ).astype(F32)
     sums = []
     for s in range(SEG):
-        left = kernel_ref[0, s].reshape(LAGS * R_CH, KF)
+        left = kernel_ref[0, s, :, 0].reshape(NX * R_CH, KF)
         right = jnp.concatenate([ref[0, 0, s] for ref in sources], axis=0)
         sums.append(lax.dot_general(left, right, (((1,), (1,)), ((), ())), preferred_element_type=F32))
     for q in range(SLOTS):
         total = 0.0
         for s in range(SEG):
             total = total + sums[s] * (live * (info_ref[68 + s] == q).astype(F32))
-        out_ref[0, :, q] = total.reshape(LAGS, R_CH, K * CQ).astype(BF)
-
-
-def correlate(info, kernels, gathered):
+        out_ref[0, :, q] = total.reshape(NX, R_CH, K * CQ)
+
+
+def correlate(info, kernels, gathered, name):
     def source_map(k):
         return lambda o, info: (info[o * K + k], info[32 + o * K + k], 0, 0, 0)
 
@@ -146,26 +145,25 @@
             grid=(NY,),
             in_specs=[
                 pl.BlockSpec(
-                    (1, SEG, LAGS, R_CH, KF),
-                    lambda o, info: (lax.rem(info[70] + NY - o, NY), 0, 0, 0, 0),
+                    (1, SEG, NX, 1, R_CH, KF),
+                    lambda o, info: (lax.rem(info[70] + NY - o, NY), 0, 0, info[71], 0, 0),
                 )
             ]
             + [pl.BlockSpec((1, 1, SEG, CQ, KF), source_map(k)) for k in range(K)],
-            out_specs=pl.BlockSpec((1, LAGS, SLOTS, R_CH, K * CQ), lambda o, info: (o, 0, 0, 0, 0)),
+            out_specs=pl.BlockSpec((1, NX, SLOTS, R_CH, K * CQ), lambda o, info: (o, 0, 0, 0, 0)),
         ),
-        out_shape=jax.ShapeDtypeStruct((NY, LAGS, SLOTS, R_CH, K * CQ), BF),
-        compiler_params=pltpu.CompilerParams(vmem_limit_bytes=VMEM),
-        name="correlate",
+        out_shape=jax.ShapeDtypeStruct((NY, NX, SLOTS, R_CH, K * CQ), F32),
+        compiler_params=pltpu.CompilerParams(vmem_limit_bytes=448 * MIB),
+        name=name,
     )(info, kernels, *([gathered] * K))
 
 
 def finish_body(parts_ref, out_ref):
-    n = NX * NC
     quarter = []
     for y in range(NY):
-        total = parts_ref[y * n, 0].astype(F32)
-        for t in range(1, n):
-            total = total + parts_ref[y * n + t, 0].astype(F32)
+        total = parts_ref[y * NX, 0].astype(F32)
+        for x in range(1, NX):
+            total = total + parts_ref[y * NX + x, 0].astype(F32)
         quarter.append(total)
     for k in range(K):
         row = jnp.concatenate([v[:, k * CQ : (k + 1) * CQ] for v in quarter], axis=1)
@@ -176,10 +174,10 @@
     return pl.pallas_call(
         finish_body,
         grid=(SLOTS,),
-        in_specs=[pl.BlockSpec((NY * NX * NC, 1, R_CH, K * CQ), lambda q: (0, q, 0, 0))],
+        in_specs=[pl.BlockSpec((NY * NX, 1, R_CH, K * CQ), lambda q: (0, q, 0, 0))],
         out_specs=pl.BlockSpec((1, 1, K, R_CH, CH), lambda q: (0, q, 0, 0, 0)),
         out_shape=jax.ShapeDtypeStruct((1, SLOTS, K, R_CH, CH), BF),
-        compiler_params=pltpu.CompilerParams(vmem_limit_bytes=VMEM),
+        compiler_params=pltpu.CompilerParams(vmem_limit_bytes=48 * MIB),
         name="finish",
     )(parts)
 
@@ -208,11 +206,14 @@
     lists = lax.dynamic_index_in_dim(source_list.reshape(NY, NZ, K), z, 1, keepdims=False).reshape(-1)
     counts = lax.dynamic_index_in_dim(source_count.reshape(NY, NZ), z, 1, keepdims=False)
     slots = lax.dynamic_slice_in_dim(segment_slot, t * SEG, SEG, 0)
-    info = jnp.concatenate([lists % NZ, lists // NZ, counts, slots, y[None].astype(jnp.int32)])
-    sums = correlate(info, kernels, gathered)
-    parts = sums.reshape(NY * LAGS, SLOTS, R_CH, K * CQ)
-    parts = lax.all_to_all(parts, ("y", "x", "c"), 0, 0)
-    return finish(parts)
+    core = lax.axis_index("c")[None].astype(jnp.int32)
+    common = [lists % NZ, lists // NZ, counts, slots, y[None].astype(jnp.int32)]
+    kernels = kernels.reshape(NY, SEG, NX, NC, R_CH, KF)
+    send = correlate(jnp.concatenate(common + [1 - core]), kernels, gathered, "correlate_other")
+    other = lax.ppermute(send, "c", [(0, 1), (1, 0)])
+    keep = correlate(jnp.concatenate(common + [core]), kernels, gathered, "correlate_own")
+    parts = (keep + other).astype(BF).reshape(NY * NX, SLOTS, R_CH, K * CQ)
+    return finish(lax.all_to_all(parts, ("y", "x"), 0, 0))
 
 
 def solution(mesh):

time: 187 us -> 187 us (level)
  blocking collectives: 47.6 us -> 34.9 us
  Pallas kernels: 17.5 us -> 25.4 us
  other arithmetic: 0.33 us -> 3.79 us
  starting transfers between devices: 19 us -> 21.9 us
  waiting for transfers between devices: 83.6 us -> 80.7 us
    all_to_all x1, blocking collectives: 35.8 us -> 22.7 us  [body(): return finish(lax.all_to_all(parts, ('y', 'x'), 0, 0))]
    pallas_call x1 -> x2, Pallas kernels: 7.77 us -> 13.4 us  [correlate(): pl.pallas_call(correlate_body, grid_spec=pltpu.PrefetchScalarGridSpec(num...]
    ppermute x0 -> x1, starting transfers between devices: none -> 2.83 us  [body(): other = lax.ppermute(send, 'c', [(0, 1), (1, 0)])]
    unnamed x15, local copies, waits for them, and re-layouts: 2.94 us -> 0.13 us
    convert_element_type x0 -> x1, other arithmetic: none -> 2.53 us  [body(): parts = (keep + other).astype(BF).reshape(NY * NX, SLOTS, R_CH, K * CQ)]
    pallas_call x1, Pallas kernels: 2.53 us -> 4.95 us  [whiten(): pl.pallas_call(whiten_kernel, grid=(NB,), in_specs=[pl.BlockSpec((SEG, SA...]
    concatenate x1 -> x2, local copies, waits for them, and re-layouts: 0.08 us -> 1.98 us  [the longest x1 1.36 us: body(): jnp.concatenate(common + [core])]
  transfers between devices with their start and end apart: 5 -> 6, of which waited for: 3 -> 3; matrix products, arithmetic and copies ran while one was open for 1% -> 3% of each run, Pallas kernels for 3% -> 7%
where the time goes in v3:
time: 187 us; the launch traced here: 186 us
  waiting for transfers between devices  80.7 us (43%)
  blocking collectives  34.9 us (19%)
  Pallas kernels  25.4 us (14%)
  starting transfers between devices  21.9 us (12%)
  between operations  14.6 us (8%)
  local copies, waits for them, and re-layouts  4.59 us (2%)
  other arithmetic  3.79 us (2%)
    all_gather x1, waiting for transfers between devices, body(): gathered = lax.all_gather(crossed, 'z', axis=0, tiled=False)  73.4 us
    all_to_all x1, blocking collectives, body(): return finish(lax.all_to_all(parts, ('y', 'x'), 0, 0))  22.7 us
    ppermute x3, starting transfers between devices, body(): lax.ppermute(window, 'y', [(i, (i + d) % NY) for i in range(NY)])  17.8 us
    pallas_call x2, Pallas kernels, correlate(): pl.pallas_call(correlate_body, grid_spec=pltpu.PrefetchScalarGridSpec(num...  13.4 us
    all_to_all x1, blocking collectives, body(): crossed = lax.all_to_all(split, 'y', 0, 0)  12.2 us
    pallas_call x1, Pallas kernels, lag_kernels(): pl.pallas_call(lag_kernel_body, grid=(NY, SEG), in_specs=[pl.BlockSpec((1...  5.88 us
    pallas_call x1, Pallas kernels, whiten(): pl.pallas_call(whiten_kernel, grid=(NB,), in_specs=[pl.BlockSpec((SEG, SA...  4.95 us
    ppermute x1, waiting for transfers between devices, body(): lax.ppermute(low, ('y', 'z'), [(p, p - 1) for p in range(1, pairs)])  4.75 us
  transfers between devices with their start and end apart: 6, of which 3 were waited for; matrix products, arithmetic and copies ran while one was open for 3% of the time, Pallas kernels for 7%

profile of v3, /device:TPU:1, one launch (start us, length us, event | category | flops | bytes accessed | tf_op | source)
XLA Modules:
  0.0 185.9 jit_solution(16137985947124200439)
XLA Ops:
  6.5 0.0 all-gather.3.cloned.1.call-start
  6.5 5.0 %whiten.1 = (bf16[4,2,32,1024]{3,2,1,0:T(8,128)(2,1)}, bf16[2,64,1024]{2,1,0:T(8,128)(2,1)}, bf16[2,64,1024]{2,1,0:T(8,128)(2,1)}) custom-call(bf16[2,2048,128]{2,1,0:T(8,128)(2,1)} %traces_ref.1, bf16[2,512,1024]{2,1,0:T(8,128)(2,1)} %constant.75.clone.table_ref), custom_call_target="tpu_custom_call" | custom-call | tf_op jit(solution)/shard_map/whiten/pallas_call | solution.py:73
  11.5 0.0 copy-start.5
  11.5 0.0 copy-start.6
  11.5 0.0 copy-start
  11.5 12.2 %all_to_all.10 = bf16[4,2,32,1024]{3,2,1,0:T(8,128)(2,1)} all-to-all(bf16[4,2,32,1024]{3,2,1,0:T(8,128)(2,1)} %get-tuple-element.12), channel_id=1, replica_groups=mesh['y'=4,'z'=16,'x'=4,'c'=2] {'y'}, dimensions={0} | all-to-all | bytes 1048576 | tf_op jit(solution)/shard_map/all_to_all | solution.py:192
  23.7 0.0 all-gather.3.cloned.1.call-update
  23.7 1.3 collective-permute-start
  25.0 1.2 dynamic_slice.21
  27.3 0.8 reshape.20
  28.1 4.8 %collective-permute-done = bf16[2,64,1024]{2,1,0:T(8,128)(2,1)S(1)} collective-permute-done((bf16[2,64,1024]{2,1,0:T(8,128)(2,1)}, bf16[2,64,1024]{2,1,0:T(8,128)(2,1)S(1)}, u32[]{:S(2)}, u32[]{:S(2)}) %collective-permute-start) | collective-permute-done | bytes 262176 | tf_op jit(solution)/shard_map/ppermute | solution.py:197
  32.9 1.1 fusion
  34.0 11.3 %collective-permute-start.2 = (bf16[2,64,1024]{2,1,0:T(8,128)(2,1)S(1)}, bf16[2,64,1024]{2,1,0:T(8,128)(2,1)S(1)}, u32[]{:S(2)}, u32[]{:S(2)}) collective-permute-start(bf16[2,64,1024]{2,1,0:T(8,128)(2,1)S(1)} %fusion), channel_id=1, source_target_pairs={{0,256},{128,384},{256,0},{384,128},{1,257},{129,385},{257,1},{385... | collective-permute-start | bytes 786440 | tf_op jit(solution)/shard_map/ppermute | solution.py:202
  45.3 1.9 %collective-permute-start.1 = (bf16[2,64,1024]{2,1,0:T(8,128)(2,1)S(1)}, bf16[2,64,1024]{2,1,0:T(8,128)(2,1)S(1)}, u32[]{:S(2)}, u32[]{:S(2)}) collective-permute-start(bf16[2,64,1024]{2,1,0:T(8,128)(2,1)S(1)} %fusion), channel_id=1, source_target_pairs={{0,128},{128,256},{256,384},{384,0},{1,129},{129,257},{257,385},{3... | collective-permute-start | bytes 786440 | tf_op jit(solution)/shard_map/ppermute | solution.py:202
  47.3 4.6 %collective-permute-start.3 = (bf16[2,64,1024]{2,1,0:T(8,128)(2,1)S(1)}, bf16[2,64,1024]{2,1,0:T(8,128)(2,1)S(1)}, u32[]{:S(2)}, u32[]{:S(2)}) collective-permute-start(bf16[2,64,1024]{2,1,0:T(8,128)(2,1)S(1)} %fusion), channel_id=1, source_target_pairs={{0,384},{128,0},{256,128},{384,256},{1,385},{129,1},{257,129},{385... | collective-permute-start | bytes 786440 | tf_op jit(solution)/shard_map/ppermute | solution.py:202
  51.8 0.1 constant_dynamic-slice_fusion
  51.9 0.0 copy-done.5
  51.9 0.1 reshape.22
  52.0 0.2 dynamic-slice_reduce_fusion
  52.2 0.0 copy-start.1
  52.2 0.1 copy.11
  52.3 0.1 reshape.21
  52.4 0.0 copy-done.6
  52.4 0.1 dynamic_slice.20
  52.5 0.0 copy-start.2
  52.5 0.0 copy-start.3
  52.5 0.0 copy-start.4
  52.5 0.6 concatenate.11.info_ref
  53.1 0.0 collective-permute-done.2
  53.1 2.5 %collective-permute-done.1 = bf16[2,64,1024]{2,1,0:T(8,128)(2,1)S(1)} collective-permute-done((bf16[2,64,1024]{2,1,0:T(8,128)(2,1)S(1)}, bf16[2,64,1024]{2,1,0:T(8,128)(2,1)S(1)}, u32[]{:S(2)}, u32[]{:S(2)}) %collective-permute-start.1) | collective-permute-done | bytes 262176 | tf_op jit(solution)/shard_map/ppermute | solution.py:202
  55.7 0.0 collective-permute-done.3
  55.7 0.1 pad_maximum_fusion.window_ref
  55.8 0.0 copy-done
  55.8 5.9 %lag_kernels.1 = bf16[4,2,8,64,1024]{4,3,2,1,0:T(8,128)(2,1)} custom-call(bf16[4,2,64,1024]{3,2,1,0:T(8,128)(2,1)S(1)} %pad_maximum_fusion.window_ref, f32[2,8,512]{2,1,0:T(8,128)S(1)} %copy-done), custom_call_target="tpu_custom_call" | custom-call | tf_op jit(solution)/shard_map/lag_kernels/pallas_call | solution.py:106
  61.7 0.0 copy-done.1
  61.7 0.0 copy-done.2
  61.7 0.0 copy-done.3
  61.7 0.0 copy-done.4
  61.7 73.4 %all-gather.3.cloned.1.call-done = bf16[64,2,32,1024]{3,2,1,0:T(8,128)(2,1)} async-done(((bf16[4,2,32,1024]{3,2,1,0:T(8,128)(2,1)}), bf16[64,2,32,1024]{3,2,1,0:T(8,128)(2,1)}) %all-gather.3.cloned.1.call-update) | async-done | bytes 8388624 | tf_op jit(solution)/shard_map/all_gather | solution.py:193
  135.1 6.5 %correlate_other.1 = f32[4,4,2,64,256]{4,3,2,1,0:T(8,128)} custom-call(s32[72]{0:T(128)} %concatenate.11.info_ref, bf16[4,2,4,2,64,1024]{5,4,3,2,1,0:T(8,128)(2,1)} %bitcast.31, bf16[16,4,2,32,1024]{4,3,2,1,0:T(8,128)(2,1)} %bitcast.15, bf16[16,4,2,32,1024]{4,3,2,1,0:T(8,128)(2,1)} %bitcast.16, bf16[16,4,2,32,1024]{4,3,2,1,0:T(8,128)(2,1)} %bitcast.17, ...), custom_call_target="tpu_custom_call" | custom-call | tf_op jit(solution)/shard_map/correlate_other/pallas_call | solution.py:141
  141.6 2.8 %collective-permute-start.4 = (f32[4,4,2,64,256]{4,3,2,1,0:T(8,128)}, f32[4,4,2,64,256]{4,3,2,1,0:T(8,128)}, u32[]{:S(2)}, u32[]{:S(2)}) collective-permute-start(f32[4,4,2,64,256]{4,3,2,1,0:T(8,128)} %correlate_other.1), channel_id=1, source_target_pairs={{0,1},{1,0},{2,3},{3,2},{4,5},{5,4},{6,7},{7,6},{8,9},{9,8},{10,11... | collective-permute-start | bytes 6291464 | tf_op jit(solution)/shard_map/ppermute | solution.py:213
  144.5 1.4 concatenate.9.info_ref
  145.8 6.8 %correlate_own.1 = f32[4,4,2,64,256]{4,3,2,1,0:T(8,128)} custom-call(s32[72]{0:T(128)} %concatenate.9.info_ref, bf16[4,2,4,2,64,1024]{5,4,3,2,1,0:T(8,128)(2,1)} %bitcast.32, bf16[16,4,2,32,1024]{4,3,2,1,0:T(8,128)(2,1)} %bitcast.23, bf16[16,4,2,32,1024]{4,3,2,1,0:T(8,128)(2,1)} %bitcast.24, bf16[16,4,2,32,1024]{4,3,2,1,0:T(8,128)(2,1)} %bitcast.25, ...), custom_call_target="tpu_custom_call" | custom-call | tf_op jit(solution)/shard_map/correlate_own/pallas_call | solution.py:141
  152.7 0.0 collective-permute-done.4
  152.7 2.5 %add_convert_fusion = bf16[4,4,2,64,256]{4,3,2,1,0:T(8,128)(2,1)S(1)} fusion(f32[4,4,2,64,256]{4,3,2,1,0:T(8,128)} %correlate_own.1, f32[4,4,2,64,256]{4,3,2,1,0:T(8,128)} %collective-permute-done.4), kind=kLoop, calls=%fused_computation | loop fusion | flops 1048576 | bytes 5242880 | tf_op jit(solution)/shard_map/convert_element_type | solution.py:215
  155.2 22.7 %all_to_all.11.parts_ref = bf16[16,2,64,256]{3,2,1,0:T(8,128)(2,1)S(1)} all-to-all(bf16[16,2,64,256]{3,2,1,0:T(8,128)(2,1)S(1)} %bitcast.33), channel_id=1, replica_groups=mesh['y'=4,'z'=16,'x'=4,'c'=2] {'y','x'}, dimensions={0} | all-to-all | bytes 2097152 | tf_op jit(solution)/shard_map/all_to_all | solution.py:216
  178.0 1.2 finish.1
  (1 shorter events, 0.0 us)
Async XLA Ops:
  6.5 128.6 %all-gather.3.cloned.1.call-start = ((), (), s32[]{:S(2)}) async-start(), calls=%async_computation.2 | async-start | bytes 8912896 | tf_op jit(solution)/shard_map/all_gather | solution.py:193
  11.5 40.4 %copy-start.5 = (s32[64]{0:T(128)S(1)}, s32[64]{0:T(128)}, u32[]{:S(2)}) copy-start(s32[64]{0:T(128)} %param.9) | copy-start | bytes 772
  11.5 40.9 %copy-start.6 = (s32[16]{0:T(128)S(1)}, s32[16]{0:T(128)}, u32[]{:S(2)}) copy-start(s32[16]{0:T(128)} %param.11) | copy-start | bytes 196
  11.5 44.3 %copy-start = (f32[2,8,512]{2,1,0:T(8,128)S(1)}, f32[2,8,512]{2,1,0:T(8,128)}, u32[]{:S(2)}) copy-start(f32[2,8,512]{2,1,0:T(8,128)} %constant.76.clone.lag_ref) | copy-start | bytes 98308
  23.7 9.1 %collective-permute-start = (bf16[2,64,1024]{2,1,0:T(8,128)(2,1)}, bf16[2,64,1024]{2,1,0:T(8,128)(2,1)S(1)}, u32[]{:S(2)}, u32[]{:S(2)}) collective-permute-start(bf16[2,64,1024]{2,1,0:T(8,128)(2,1)} %get-tuple-element.14), channel_id=1, source_target_pairs={{8,0},{16,8},{24,16},{32,24},{40,32},{48,40},{56,48},{64,56},{72,6... | collective-permute-start | bytes 786440 | tf_op jit(solution)/shard_map/ppermute | solution.py:197
  34.0 19.1 %collective-permute-start.2 = (bf16[2,64,1024]{2,1,0:T(8,128)(2,1)S(1)}, bf16[2,64,1024]{2,1,0:T(8,128)(2,1)S(1)}, u32[]{:S(2)}, u32[]{:S(2)}) collective-permute-start(bf16[2,64,1024]{2,1,0:T(8,128)(2,1)S(1)} %fusion), channel_id=1, source_target_pairs={{0,256},{128,384},{256,0},{384,128},{1,257},{129,385},{257,1},{385... | collective-permute-start | bytes 786440 | tf_op jit(solution)/shard_map/ppermute | solution.py:202
  45.3 10.3 %collective-permute-start.1 = (bf16[2,64,1024]{2,1,0:T(8,128)(2,1)S(1)}, bf16[2,64,1024]{2,1,0:T(8,128)(2,1)S(1)}, u32[]{:S(2)}, u32[]{:S(2)}) collective-permute-start(bf16[2,64,1024]{2,1,0:T(8,128)(2,1)S(1)} %fusion), channel_id=1, source_target_pairs={{0,128},{128,256},{256,384},{384,0},{1,129},{129,257},{257,385},{3... | collective-permute-start | bytes 786440 | tf_op jit(solution)/shard_map/ppermute | solution.py:202
  47.3 8.4 %collective-permute-start.3 = (bf16[2,64,1024]{2,1,0:T(8,128)(2,1)S(1)}, bf16[2,64,1024]{2,1,0:T(8,128)(2,1)S(1)}, u32[]{:S(2)}, u32[]{:S(2)}) collective-permute-start(bf16[2,64,1024]{2,1,0:T(8,128)(2,1)S(1)} %fusion), channel_id=1, source_target_pairs={{0,384},{128,0},{256,128},{384,256},{1,385},{129,1},{257,129},{385... | collective-permute-start | bytes 786440 | tf_op jit(solution)/shard_map/ppermute | solution.py:202
  52.2 9.5 %copy-start.1 = (s32[4]{0:T(128)}, s32[4]{0:T(128)S(1)}, u32[]{:S(2)}) copy-start(s32[4]{0:T(128)S(1)} %dynamic-slice_reduce_fusion) | copy-start | bytes 52
  52.5 9.2 %copy-start.2 = (s32[2]{0:T(128)}, s32[2]{0:T(128)S(1)}, u32[]{:S(2)}) copy-start(s32[2]{0:T(128)S(1)} %dynamic_slice.20) | copy-start | bytes 28
  52.5 9.2 %copy-start.3 = (s32[32]{0:T(128)}, s32[32]{0:T(128)S(1)}, u32[]{:S(2)}) copy-start(s32[32]{0:T(128)S(1)} %get-tuple-element.15) | copy-start | bytes 388
  52.5 9.2 %copy-start.4 = (s32[32]{0:T(128)}, s32[32]{0:T(128)S(1)}, u32[]{:S(2)}) copy-start(s32[32]{0:T(128)S(1)} %get-tuple-element.16) | copy-start | bytes 388
  141.6 11.0 %collective-permute-start.4 = (f32[4,4,2,64,256]{4,3,2,1,0:T(8,128)}, f32[4,4,2,64,256]{4,3,2,1,0:T(8,128)}, u32[]{:S(2)}, u32[]{:S(2)}) collective-permute-start(f32[4,4,2,64,256]{4,3,2,1,0:T(8,128)} %correlate_other.1), channel_id=1, source_target_pairs={{0,1},{1,0},{2,3},{3,2},{4,5},{5,4},{6,7},{7,6},{8,9},{9,8},{10,11... | collective-permute-start | bytes 6291464 | tf_op jit(solution)/shard_map/ppermute | solution.py:213
Sparse Core Ops, SparseCore 0:
  23.8 111.2 all-gather.2

commit v4 on v1

v4 whole, which is shorter than its diff:
```python
import jax
import jax.numpy as jnp
import numpy as np
from jax import lax
from jax.experimental import pallas as pl
from jax.experimental.pallas import tpu as pltpu
from jax.sharding import Mesh, PartitionSpec as P

CH = 128
SAMPLES = 2048
NF = 512
BAND = 32
K = 8
R_CH = 64
LAGS = 8
SLOTS = 2
F0 = 64
SEGS = 16
NY, NZ, NX, NC = 4, 16, 4, 2
SEG = 2
SEG_CHIP = SEG * NC
PIECES = NY * NC
CQ = CH // PIECES
FB = 128
NB = NF // FB
KF = 2 * NF
EPS = 1e-06
NORM = np.float32((2.0 * NF * SEGS / SLOTS) ** (-0.5))
BF = jnp.bfloat16
F32 = jnp.float32
VMEM = 48 * 1024 * 1024


def transform_table():
    bins = F0 + np.arange(NF, dtype=np.int64)
    phase = (bins[:, None] * np.arange(SAMPLES // 2, dtype=np.int64)[None, :]) % SAMPLES
    steps = np.arange(SAMPLES, dtype=np.float32) * np.float32(2.0 * np.pi / SAMPLES)
    cos = np.cos(steps)[phase]
    sin = -np.sin(steps)[phase]
    return np.stack([cos, sin], axis=0).astype(jnp.bfloat16)


def lag_tables():
    bins = F0 + np.arange(NF, dtype=np.int64)
    lags = np.arange(LAGS, dtype=np.int64) - LAGS // 2
    phase = (lags[:, None] * bins[None, :]) % SAMPLES
    angle = phase.astype(np.float32) * np.float32(2.0 * np.pi / SAMPLES)
    return np.stack([np.cos(angle), np.sin(angle)], axis=0).astype(np.float32)


def whiten_kernel(traces_ref, table_ref, split_ref, low_ref, high_ref):
    half = SAMPLES // 2
    table = table_ref[...].reshape(2 * FB, half)
    early = jnp.concatenate([traces_ref[s, :half] for s in range(SEG)], axis=1)
    late = jnp.concatenate([traces_ref[s, half:] for s in range(SEG)], axis=1)
    early = jnp.dot(table, early, preferred_element_type=F32)
    late = jnp.dot(table, late, preferred_element_type=F32)
    odd = lax.broadcasted_iota(jnp.int32, late.shape, 0) % 2 == 1
    spectra = early + jnp.where(odd, -late, late)
    grouped = spectra.reshape(2, FB // BAND, BAND, SEG * CH)
    power = jnp.sum(grouped * grouped, axis=(0, 2)) * (1.0 / (2 * BAND))
    scale = 1.0 / jnp.sqrt(power + EPS)
    whitened = grouped * scale[None, :, None, :]
    flipped = whitened.reshape(2 * FB, SEG * CH).T.astype(BF)
    for s in range(SEG):
        low_ref[s] = flipped[s * CH : s * CH + CH // 2]
        high_ref[s] = flipped[s * CH + CH // 2 : (s + 1) * CH]
        for r in range(PIECES):
            split_ref[r, s] = flipped[s * CH + r * CQ : s * CH + (r + 1) * CQ]


def whiten(traces, table):
    half = jax.ShapeDtypeStruct((SEG, CH // 2, KF), BF)
    half_spec = pl.BlockSpec((SEG, CH // 2, 2 * FB), lambda g: (0, 0, g))
    return pl.pallas_call(
        whiten_kernel,
        grid=(NB,),
        in_specs=[
            pl.BlockSpec((SEG, SAMPLES, CH), lambda g: (0, 0, 0)),
            pl.BlockSpec((2, FB, SAMPLES // 2), lambda g: (0, g, 0)),
        ],
        out_specs=[
            pl.BlockSpec((PIECES, SEG, CQ, 2 * FB), lambda g: (0, 0, 0, g)),
            half_spec,
            half_spec,
        ],
        out_shape=[jax.ShapeDtypeStruct((PIECES, SEG, CQ, KF), BF), half, half],
        compiler_params=pltpu.CompilerParams(vmem_limit_bytes=VMEM),
        name="whiten",
    )(traces, table)


def lag_kernel_body(core_ref, window_ref, lag_ref, out_ref):
    for b in range(NB):
        at = b * 2 * FB
        real = window_ref[0, 0, :, at : at + FB].astype(F32)
        imag = window_ref[0, 0, :, at + FB : at + 2 * FB].astype(F32)
        for l in range(0, LAGS, 2):
            reals, imags = [], []
            for m in (l, l + 1):
                cos = lag_ref[0, m : m + 1, b * FB : (b + 1) * FB]
                sin = lag_ref[1, m : m + 1, b * FB : (b + 1) * FB]
                reals.append((cos * real + sin * imag) * NORM)
                imags.append((cos * imag - sin * real) * NORM)
            lanes = slice(l * R_CH, (l + 2) * R_CH)
            out_ref[0, 0, at : at + FB, lanes] = jnp.concatenate(reals, axis=0).T.astype(BF)
            out_ref[0, 0, at + FB : at + 2 * FB, lanes] = jnp.concatenate(imags, axis=0).T.astype(BF)


def lag_kernels(core, windows, lags):
    return pl.pallas_call(
        lag_kernel_body,
        grid_spec=pltpu.PrefetchScalarGridSpec(
            num_scalar_prefetch=1,
            grid=(NY, SEG_CHIP),
            in_specs=[
                pl.BlockSpec((1, 1, R_CH, KF), lambda o, s, core: (o, s, 0, 0)),
                pl.BlockSpec((2, LAGS, NF), lambda o, s, core: (0, 0, 0)),
            ],
            out_specs=pl.BlockSpec(
                (1, 1, KF, LAGS * R_CH),
                lambda o, s, core: (o, lax.rem(s + SEG * core[0], SEG_CHIP), 0, 0),
            ),
        ),
        out_shape=jax.ShapeDtypeStruct((NY, SEG_CHIP, KF, LAGS * R_CH), BF),
        compiler_params=pltpu.CompilerParams(vmem_limit_bytes=VMEM),
        name="lag_kernels",
    )(core, windows, lags)


I_COUNT = 2 * NY * K
I_SLOT = I_COUNT + NY
I_Y = I_SLOT + SEG_CHIP


def correlate_body(info_ref, kernel_ref, *refs):
    sources, out_ref = refs[:K], refs[K]
    o = pl.program_id(0)
    row = lax.broadcasted_iota(jnp.int32, (K * CQ, 1), 0)
    live = (row < info_ref[I_COUNT + o] * CQ).astype(F32)
    totals = [0.0] * SLOTS
    for s in range(SEG_CHIP):
        left = jnp.concatenate([ref[0, 0, s] for ref in sources], axis=0)
        part = jnp.dot(left, kernel_ref[0, s], preferred_element_type=F32)
        for q in range(SLOTS):
            totals[q] = totals[q] + part * (live * (info_ref[I_SLOT + s] == q).astype(F32))
    for l in range(LAGS):
        both = jnp.concatenate([v[:, l * R_CH : (l + 1) * R_CH] for v in totals], axis=1)
        out_ref[0, l] = both.astype(BF)


def correlate(info, kernels, gathered):
    def source_map(k):
        return lambda o, info: (info[o * K + k], info[NY * K + o * K + k], 0, 0, 0)

    return pl.pallas_call(
        correlate_body,
        grid_spec=pltpu.PrefetchScalarGridSpec(
            num_scalar_prefetch=1,
            grid=(NY,),
            in_specs=[
                pl.BlockSpec(
                    (1, SEG_CHIP, KF, LAGS * R_CH),
                    lambda o, info: (lax.rem(info[I_Y] + NY - o, NY), 0, 0, 0),
                )
            ]
            + [pl.BlockSpec((1, 1, SEG_CHIP, CQ, KF), source_map(k)) for k in range(K)],
            out_specs=pl.BlockSpec((1, LAGS, K * CQ, SLOTS * R_CH), lambda o, info: (o, 0, 0, 0)),
        ),
        out_shape=jax.ShapeDtypeStruct((NY, LAGS, K * CQ, SLOTS * R_CH), BF),
        compiler_params=pltpu.CompilerParams(vmem_limit_bytes=VMEM),
        name="correlate",
    )(info, kernels, *([gathered] * K))


def finish_body(parts_ref, out_ref):
    pieces = []
    for y in range(NY):
        for c in range(NC):
            total = parts_ref[y * NX * NC + c].astype(F32)
            for x in range(1, NX):
                total = total + parts_ref[(y * NX + x) * NC + c].astype(F32)
            pieces.append(total)
    for k in range(K):
        rows = jnp.concatenate([v[k * CQ : (k + 1) * CQ] for v in pieces], axis=0).T.astype(BF)
        for q in range(SLOTS):
            out_ref[0, q, k] = rows[q * R_CH : (q + 1) * R_CH]


def finish(parts):
    return pl.pallas_call(
        finish_body,
        out_shape=jax.ShapeDtypeStruct((1, SLOTS, K, R_CH, CH), BF),
        compiler_params=pltpu.CompilerParams(vmem_limit_bytes=VMEM),
        name="finish",
    )(parts)


def body(traces, source_list, source_count, receiver_start, segment_slot):
    y = lax.axis_index("y")
    z = lax.axis_index("z")
    table = jnp.asarray(transform_table())
    lags = jnp.asarray(lag_tables())
    split, low, high = whiten(traces, table)
    crossed = lax.all_to_all(split, ("y", "c"), 0, 0).reshape(NY, SEG_CHIP, CQ, KF)
    gathered = lax.all_gather(crossed, "z", axis=0, tiled=False)

    low, high, _ = lax.optimization_barrier((low, high, crossed))
    pairs = NY * NZ
    following = lax.ppermute(low, ("y", "z"), [(p, p - 1) for p in range(1, pairs)])
    joined = jnp.concatenate([high, following], axis=1)
    offset = lax.dynamic_index_in_dim(receiver_start, y * NZ + z, keepdims=False) - CH // 2
    window = lax.dynamic_slice_in_dim(joined, offset, R_CH, 1)
    own = jnp.stack(
        [window] + [lax.ppermute(window, "y", [(i, (i + d) % NY) for i in range(NY)]) for d in range(1, NY)]
    )
    other = lax.ppermute(own, "c", [(0, 1), (1, 0)])
    core = lax.axis_index("c")[None].astype(jnp.int32)
    kernels = lag_kernels(core, jnp.concatenate([own, other], axis=1), lags)

    lists = lax.dynamic_index_in_dim(source_list.reshape(NY, NZ, K), z, 1, keepdims=False).reshape(-1)
    counts = lax.dynamic_index_in_dim(source_count.reshape(NY, NZ), z, 1, keepdims=False)
    slots = lax.dynamic_slice_in_dim(segment_slot, lax.axis_index("x") * SEG_CHIP, SEG_CHIP, 0)
    info = jnp.concatenate([lists % NZ, lists // NZ, counts, slots, y[None].astype(jnp.int32)])
    sums = correlate(info, kernels, gathered)
    parts = lax.all_to_all(sums.reshape(NY * LAGS, K * CQ, SLOTS * R_CH), ("y", "x", "c"), 0, 0)
    return finish(parts)


def solution(mesh):
    grid = Mesh(mesh.devices.reshape(NY, NZ, NX, NC), ("y", "z", "x", "c"))
    tm, pair = ("x", "c"), ("y", "z")
    return jax.shard_map(
        body,
        mesh=grid,
        in_specs=(P(tm, None, pair), P(), P(), P(), P()),
        out_specs=P(tm, None, pair, None, None),
        check_vma=False,
    )
```

time: 187 us -> 179 us (0.957)
  waiting for transfers between devices: 83.6 us -> 71.5 us
  Pallas kernels: 17.5 us -> 26.3 us
  blocking collectives: 47.6 us -> 43.8 us
    all_gather x1, waiting for transfers between devices: 74.6 us -> 57.8 us  [body(): gathered = lax.all_gather(crossed, 'z', axis=0, tiled=False)]
    pallas_call x2, Pallas kernels: 7.2 us -> 13.3 us  [the longest x1 12.4 us: lag_kernels(): pl.pallas_call(lag_kernel_body, grid_spec=pltpu.PrefetchScalarGridSpec(nu...]
    ppermute x3, starting transfers between devices: 17.7 us -> 12.5 us  [body(): lax.ppermute(window, 'y', [(i, (i + d) % NY) for i in range(NY)])]
    all_to_all x2, blocking collectives: 47.6 us -> 43.8 us  [the longest x1 24.3 us: body(): lax.all_to_all(sums.reshape(NY * LAGS, K * CQ, SLOTS * R_CH), ('y', 'x',...]
    ppermute x0 -> x1, starting transfers between devices: none -> 3.78 us  [body(): other = lax.ppermute(own, 'c', [(0, 1), (1, 0)])]
    ppermute x3, waiting for transfers between devices: 3.09 us -> 6.84 us  [body(): lax.ppermute(window, 'y', [(i, (i + d) % NY) for i in range(NY)])]
    pallas_call x1, Pallas kernels: 7.77 us -> 10.5 us  [correlate(): pl.pallas_call(correlate_body, grid_spec=pltpu.PrefetchScalarGridSpec(num...]
  transfers between devices with their start and end apart: 5 -> 6, of which waited for: 3 -> 5; matrix products, arithmetic and copies ran while one was open for 1% -> 1% of each run, Pallas kernels for 3% -> 7%
where the time goes in v4:
time: 179 us
  waiting for transfers between devices  71.5 us (40%)
  blocking collectives  43.8 us (24%)
  Pallas kernels  26.3 us (15%)
  starting transfers between devices  17.6 us (10%)
  between operations  14.8 us (8%)
  local copies, waits for them, and re-layouts  4.27 us (2%)
    all_gather x1, waiting for transfers between devices, body(): gathered = lax.all_gather(crossed, 'z', axis=0, tiled=False)  57.8 us
    all_to_all x1, blocking collectives, body(): lax.all_to_all(sums.reshape(NY * LAGS, K * CQ, SLOTS * R_CH), ('y', 'x',...  24.3 us
    all_to_all x1, blocking collectives, body(): lax.all_to_all(split, ('y', 'c'), 0, 0).reshape(NY, SEG_CHIP, CQ, KF)  19.4 us
    ppermute x3, starting transfers between devices, body(): lax.ppermute(window, 'y', [(i, (i + d) % NY) for i in range(NY)])  12.5 us
    pallas_call x1, Pallas kernels, lag_kernels(): pl.pallas_call(lag_kernel_body, grid_spec=pltpu.PrefetchScalarGridSpec(nu...  12.4 us
    pallas_call x1, Pallas kernels, correlate(): pl.pallas_call(correlate_body, grid_spec=pltpu.PrefetchScalarGridSpec(num...  10.5 us
    ppermute x3, waiting for transfers between devices, body(): lax.ppermute(window, 'y', [(i, (i + d) % NY) for i in range(NY)])  6.84 us
    ppermute x1, waiting for transfers between devices, body(): lax.ppermute(low, ('y', 'z'), [(p, p - 1) for p in range(1, pairs)])  5.43 us
  transfers between devices with their start and end apart: 6, of which 5 were waited for; matrix products, arithmetic and copies ran while one was open for 1% of the time, Pallas kernels for 7%

profile of v4, /device:TPU:1, one launch (start us, length us, event | category | flops | bytes accessed | tf_op | source)
XLA Modules:
  0.0 178.8 jit_solution(14769948165726696264)
XLA Ops:
  6.5 0.0 all-gather.2.cloned.1.call-start
  6.5 0.0 copy-start
  6.5 1.6 copy-done
  8.1 0.0 copy-start.1
  8.1 1.2 copy-done.1
  9.4 0.0 copy-start.5
  9.4 2.5 %whiten.1 = (bf16[8,2,16,1024]{3,2,1,0:T(8,128)(2,1)S(1)}, bf16[2,64,1024]{2,1,0:T(8,128)(2,1)S(1)}, bf16[2,64,1024]{2,1,0:T(8,128)(2,1)S(1)}) custom-call(bf16[2,2048,128]{2,1,0:T(8,128)(2,1)S(1)} %copy-done.1, bf16[2,512,1024]{2,1,0:T(8,128)(2,1)S(1)} %copy-done), custom_call_target="tpu_custom_call" | custom-call | tf_op jit(solution)/shard_map/whiten/pallas_call | solution.py:75
  11.9 0.0 copy-start.3
  11.9 0.0 copy-start.4
  11.9 0.0 copy-start.6
  11.9 19.4 %all_to_all.10 = bf16[8,2,16,1024]{3,2,1,0:T(8,128)(2,1)} all-to-all(bf16[8,2,16,1024]{3,2,1,0:T(8,128)(2,1)S(1)} %get-tuple-element.14), channel_id=1, replica_groups=mesh['y'=4,'z'=16,'x'=4,'c'=2] {'y','c'}, dimensions={0} | all-to-all | bytes 1048576 | tf_op jit(solution)/shard_map/all_to_all | solution.py:205
  31.4 0.0 all-gather.2.cloned.1.call-update
  31.4 1.3 collective-permute-start
  32.7 0.0 copy-done.5
  32.7 0.6 dynamic_slice.21
  34.6 5.4 %collective-permute-done = bf16[2,64,1024]{2,1,0:T(8,128)(2,1)S(1)} collective-permute-done((bf16[2,64,1024]{2,1,0:T(8,128)(2,1)S(1)}, bf16[2,64,1024]{2,1,0:T(8,128)(2,1)S(1)}, u32[]{:S(2)}, u32[]{:S(2)}) %collective-permute-start) | collective-permute-done | bytes 262176 | tf_op jit(solution)/shard_map/ppermute | solution.py:210
  40.0 0.2 fusion
  40.2 6.0 %collective-permute-start.1 = (bf16[2,64,1024]{2,1,0:T(8,128)(2,1)S(1)}, bf16[2,64,1024]{2,1,0:T(8,128)(2,1)S(1)}, u32[]{:S(2)}, u32[]{:S(2)}) collective-permute-start(bf16[2,64,1024]{2,1,0:T(8,128)(2,1)S(1)} %fusion), channel_id=1, source_target_pairs={{0,128},{128,256},{256,384},{384,0},{1,129},{129,257},{257,385},{3... | collective-permute-start | bytes 786440 | tf_op jit(solution)/shard_map/ppermute | solution.py:215
  46.2 3.0 %collective-permute-start.2 = (bf16[2,64,1024]{2,1,0:T(8,128)(2,1)S(1)}, bf16[2,64,1024]{2,1,0:T(8,128)(2,1)S(1)}, u32[]{:S(2)}, u32[]{:S(2)}) collective-permute-start(bf16[2,64,1024]{2,1,0:T(8,128)(2,1)S(1)} %fusion), channel_id=1, source_target_pairs={{0,256},{128,384},{256,0},{384,128},{1,257},{129,385},{257,1},{385... | collective-permute-start | bytes 786440 | tf_op jit(solution)/shard_map/ppermute | solution.py:215
  49.2 3.5 %collective-permute-start.3 = (bf16[2,64,1024]{2,1,0:T(8,128)(2,1)S(1)}, bf16[2,64,1024]{2,1,0:T(8,128)(2,1)S(1)}, u32[]{:S(2)}, u32[]{:S(2)}) collective-permute-start(bf16[2,64,1024]{2,1,0:T(8,128)(2,1)S(1)} %fusion), channel_id=1, source_target_pairs={{0,384},{128,0},{256,128},{384,256},{1,385},{129,1},{257,129},{385... | collective-permute-start | bytes 786440 | tf_op jit(solution)/shard_map/ppermute | solution.py:215
  52.8 0.0 collective-permute-done.1
  52.8 5.3 %collective-permute-done.2 = bf16[2,64,1024]{2,1,0:T(8,128)(2,1)S(1)} collective-permute-done((bf16[2,64,1024]{2,1,0:T(8,128)(2,1)S(1)}, bf16[2,64,1024]{2,1,0:T(8,128)(2,1)S(1)}, u32[]{:S(2)}, u32[]{:S(2)}) %collective-permute-start.2) | collective-permute-done | bytes 262176 | tf_op jit(solution)/shard_map/ppermute | solution.py:215
  58.0 1.6 collective-permute-done.3
  59.6 0.1 pad_maximum_fusion.1
  59.7 3.8 %collective-permute-start.4 = (bf16[4,2,64,1024]{3,2,1,0:T(8,128)(2,1)S(1)}, bf16[4,2,64,1024]{3,2,1,0:T(8,128)(2,1)S(1)}, u32[]{:S(2)}, u32[]{:S(2)}) collective-permute-start(bf16[4,2,64,1024]{3,2,1,0:T(8,128)(2,1)S(1)} %pad_maximum_fusion.1), channel_id=1, source_target_pairs={{0,1},{1,0},{2,3},{3,2},{4,5},{5,4},{6,7},{7,6},{8,9},{9,8},{10,11... | collective-permute-start | bytes 3145736 | tf_op jit(solution)/shard_map/ppermute | solution.py:217
  63.5 0.0 copy-done.3
  63.5 0.1 reshape.18
  63.6 0.1 constant_dynamic-slice_fusion
  63.7 0.1 copy.11
  63.8 0.1 reshape.19
  63.9 0.0 copy-done.4
  63.9 0.1 reshape.20
  64.0 0.2 dynamic-slice_reduce_fusion
  64.2 0.0 copy-done.6
  64.2 0.1 dynamic_slice.20
  64.3 0.1 concatenate.9.info_ref
  64.4 0.0 copy-start.2
  64.4 1.4 collective-permute-done.4
  65.8 0.2 pad_maximum_fusion.window_ref
  66.0 0.0 copy-done.2
  66.0 12.4 %lag_kernels.1.kernel_ref = bf16[4,4,1024,512]{3,2,1,0:T(8,128)(2,1)} custom-call(s32[1]{0:T(128)} %bitcast.1.core_ref, bf16[4,4,64,1024]{3,2,1,0:T(8,128)(2,1)S(1)} %pad_maximum_fusion.window_ref, f32[2,8,512]{2,1,0:T(8,128)S(1)} %copy-done.2), custom_call_target="tpu_custom_call" | custom-call | tf_op jit(solution)/shard_map/lag_kernels/pallas_call | solution.py:111
  78.4 57.8 %all-gather.2.cloned.1.call-done.refs_0_.refs_1_.refs_2_.refs_3_.refs_4_.refs_5_.refs_6_.refs_7_ = bf16[16,4,4,16,1024]{4,3,2,1,0:T(8,128)(2,1)} async-done(((bf16[1,4,4,16,1024]{4,3,2,1,0:T(8,128)(2,1)}), bf16[16,4,4,16,1024]{4,3,2,1,0:T(8,128)(2,1)}) %all-gather.2.cloned.1.call-update) | async-done | bytes 8388624 | tf_op jit(solution)/shard_map/all_gather | solution.py:206
  136.2 10.5 %correlate.1 = bf16[4,8,128,128]{3,2,1,0:T(8,128)(2,1)S(1)} custom-call(s32[73]{0:T(128)S(1)} %concatenate.9.info_ref, bf16[4,4,1024,512]{3,2,1,0:T(8,128)(2,1)} %lag_kernels.1.kernel_ref, bf16[16,4,4,16,1024]{4,3,2,1,0:T(8,128)(2,1)} %all-gather.2.cloned.1.call-done.refs_0_.refs_1_.refs_2_.refs_3_.refs_4_.refs_5_.refs_6_.refs_7_, ...), custom_call_target="tpu_custom_call" | custom-call | tf_op jit(solution)/shard_map/correlate/pallas_call | solution.py:156
  146.7 24.3 %all_to_all.11.parts_ref = bf16[32,128,128]{2,1,0:T(8,128)(2,1)S(1)} all-to-all(bf16[32,128,128]{2,1,0:T(8,128)(2,1)S(1)} %bitcast.14), channel_id=1, replica_groups=mesh['y'=4,'z'=16,'x'=4,'c'=2] {'y','x','c'}, dimensions={0} | all-to-all | bytes 2097152 | tf_op jit(solution)/shard_map/all_to_all | solution.py:226
  171.1 0.9 finish.1
  (1 shorter events, 0.0 us)
Async XLA Ops:
  6.5 129.7 %all-gather.2.cloned.1.call-start = ((), (), s32[]{:S(2)}) async-start(), calls=%async_computation.2 | async-start | bytes 8912896 | tf_op jit(solution)/shard_map/all_gather | solution.py:206
  6.5 1.6 copy-start
  8.1 1.2 copy-start.1
  9.4 23.3 %copy-start.5 = (s32[64]{0:T(128)S(1)}, s32[64]{0:T(128)}, u32[]{:S(2)}) copy-start(s32[64]{0:T(128)} %param.10) | copy-start | bytes 772
  11.9 51.7 %copy-start.3 = (s32[64,8]{0,1:T(8,128)S(1)}, s32[64,8]{0,1:T(8,128)}, u32[]{:S(2)}) copy-start(s32[64,8]{0,1:T(8,128)} %param.8) | copy-start | bytes 6148
  11.9 52.0 %copy-start.4 = (s32[64]{0:T(128)S(1)}, s32[64]{0:T(128)}, u32[]{:S(2)}) copy-start(s32[64]{0:T(128)} %param.9) | copy-start | bytes 772
  11.9 52.3 %copy-start.6 = (s32[16]{0:T(128)S(1)}, s32[16]{0:T(128)}, u32[]{:S(2)}) copy-start(s32[16]{0:T(128)} %param.11) | copy-start | bytes 196
  31.4 8.7 %collective-permute-start = (bf16[2,64,1024]{2,1,0:T(8,128)(2,1)S(1)}, bf16[2,64,1024]{2,1,0:T(8,128)(2,1)S(1)}, u32[]{:S(2)}, u32[]{:S(2)}) collective-permute-start(bf16[2,64,1024]{2,1,0:T(8,128)(2,1)S(1)} %get-tuple-element.13), channel_id=1, source_target_pairs={{8,0},{16,8},{24,16},{32,24},{40,32},{48,40},{56,48},{64,56},{72,6... | collective-permute-start | bytes 786440 | tf_op jit(solution)/shard_map/ppermute | solution.py:210
  40.2 12.5 %collective-permute-start.1 = (bf16[2,64,1024]{2,1,0:T(8,128)(2,1)S(1)}, bf16[2,64,1024]{2,1,0:T(8,128)(2,1)S(1)}, u32[]{:S(2)}, u32[]{:S(2)}) collective-permute-start(bf16[2,64,1024]{2,1,0:T(8,128)(2,1)S(1)} %fusion), channel_id=1, source_target_pairs={{0,128},{128,256},{256,384},{384,0},{1,129},{129,257},{257,385},{3... | collective-permute-start | bytes 786440 | tf_op jit(solution)/shard_map/ppermute | solution.py:215
  46.2 11.8 %collective-permute-start.2 = (bf16[2,64,1024]{2,1,0:T(8,128)(2,1)S(1)}, bf16[2,64,1024]{2,1,0:T(8,128)(2,1)S(1)}, u32[]{:S(2)}, u32[]{:S(2)}) collective-permute-start(bf16[2,64,1024]{2,1,0:T(8,128)(2,1)S(1)} %fusion), channel_id=1, source_target_pairs={{0,256},{128,384},{256,0},{384,128},{1,257},{129,385},{257,1},{385... | collective-permute-start | bytes 786440 | tf_op jit(solution)/shard_map/ppermute | solution.py:215
  49.2 10.4 %collective-permute-start.3 = (bf16[2,64,1024]{2,1,0:T(8,128)(2,1)S(1)}, bf16[2,64,1024]{2,1,0:T(8,128)(2,1)S(1)}, u32[]{:S(2)}, u32[]{:S(2)}) collective-permute-start(bf16[2,64,1024]{2,1,0:T(8,128)(2,1)S(1)} %fusion), channel_id=1, source_target_pairs={{0,384},{128,0},{256,128},{384,256},{1,385},{129,1},{257,129},{385... | collective-permute-start | bytes 786440 | tf_op jit(solution)/shard_map/ppermute | solution.py:215
  59.7 6.1 %collective-permute-start.4 = (bf16[4,2,64,1024]{3,2,1,0:T(8,128)(2,1)S(1)}, bf16[4,2,64,1024]{3,2,1,0:T(8,128)(2,1)S(1)}, u32[]{:S(2)}, u32[]{:S(2)}) collective-permute-start(bf16[4,2,64,1024]{3,2,1,0:T(8,128)(2,1)S(1)} %pad_maximum_fusion.1), channel_id=1, source_target_pairs={{0,1},{1,0},{2,3},{3,2},{4,5},{5,4},{6,7},{7,6},{8,9},{9,8},{10,11... | collective-permute-start | bytes 3145736 | tf_op jit(solution)/shard_map/ppermute | solution.py:217
  64.4 1.7 copy-start.2
Sparse Core Ops, SparseCore 0:
  31.5 104.6 all-gather.1

commit v5 on v4

--- a/solution.py
+++ b/solution.py
@@ -48,9 +48,30 @@
     return np.stack([np.cos(angle), np.sin(angle)], axis=0).astype(np.float32)
 
 
-def whiten_kernel(traces_ref, table_ref, split_ref, low_ref, high_ref):
+def whiten_kernel(traces_hbm, table_hbm, split_ref, low_ref, high_ref, traces_ref, table_ref, trace_sems, table_sems):
     half = SAMPLES // 2
-    table = table_ref[...].reshape(2 * FB, half)
+    g = pl.program_id(0)
+
+    def trace_copy(s, h):
+        part = pl.ds(h * half, half)
+        return pltpu.make_async_copy(traces_hbm.at[s, part], traces_ref.at[s, part], trace_sems.at[s, h])
+
+    def table_copy(b):
+        return pltpu.make_async_copy(table_hbm.at[:, pl.ds(b * FB, FB)], table_ref.at[b], table_sems.at[b])
+
+    @pl.when(g == 0)
+    def _():
+        for s in range(SEG):
+            for h in range(2):
+                trace_copy(s, h).start()
+        for b in range(NB):
+            table_copy(b).start()
+        for s in range(SEG):
+            for h in range(2):
+                trace_copy(s, h).wait()
+
+    table_copy(g).wait()
+    table = table_ref[g].reshape(2 * FB, half)
     early = jnp.concatenate([traces_ref[s, :half] for s in range(SEG)], axis=1)
     late = jnp.concatenate([traces_ref[s, half:] for s in range(SEG)], axis=1)
     early = jnp.dot(table, early, preferred_element_type=F32)
@@ -75,16 +96,19 @@
     return pl.pallas_call(
         whiten_kernel,
         grid=(NB,),
-        in_specs=[
-            pl.BlockSpec((SEG, SAMPLES, CH), lambda g: (0, 0, 0)),
-            pl.BlockSpec((2, FB, SAMPLES // 2), lambda g: (0, g, 0)),
-        ],
+        in_specs=[pl.BlockSpec(memory_space=pl.ANY), pl.BlockSpec(memory_space=pl.ANY)],
         out_specs=[
             pl.BlockSpec((PIECES, SEG, CQ, 2 * FB), lambda g: (0, 0, 0, g)),
             half_spec,
             half_spec,
         ],
         out_shape=[jax.ShapeDtypeStruct((PIECES, SEG, CQ, KF), BF), half, half],
+        scratch_shapes=[
+            pltpu.VMEM((SEG, SAMPLES, CH), BF),
+            pltpu.VMEM((NB, 2, FB, SAMPLES // 2), BF),
+            pltpu.SemaphoreType.DMA((SEG, 2)),
+            pltpu.SemaphoreType.DMA((NB,)),
+        ],
         compiler_params=pltpu.CompilerParams(vmem_limit_bytes=VMEM),
         name="whiten",
     )(traces, table)
@@ -133,15 +157,34 @@
 I_Y = I_SLOT + SEG_CHIP
 
 
-def correlate_body(info_ref, kernel_ref, *refs):
-    sources, out_ref = refs[:K], refs[K]
+def correlate_body(info_ref, kernel_ref, gathered_ref, out_ref, lagged_ref, source_ref, lag_sems, source_sems):
     o = pl.program_id(0)
+
+    def source_copy(n):
+        source = gathered_ref.at[info_ref[n], info_ref[NY * K + n]]
+        return pltpu.make_async_copy(source, source_ref.at[n], source_sems.at[n])
+
+    def lag_copy(n, s):
+        owner = lax.rem(info_ref[I_Y] + NY - n, NY)
+        return pltpu.make_async_copy(kernel_ref.at[owner, s], lagged_ref.at[n, s], lag_sems.at[n, s])
+
+    @pl.when(o == 0)
+    def _():
+        for n in range(NY):
+            for k in range(K):
+                source_copy(n * K + k).start()
+            for s in range(SEG_CHIP):
+                lag_copy(n, s).start()
+
+    for k in range(K):
+        source_copy(o * K + k).wait()
     row = lax.broadcasted_iota(jnp.int32, (K * CQ, 1), 0)
     live = (row < info_ref[I_COUNT + o] * CQ).astype(F32)
     totals = [0.0] * SLOTS
     for s in range(SEG_CHIP):
-        left = jnp.concatenate([ref[0, 0, s] for ref in sources], axis=0)
-        part = jnp.dot(left, kernel_ref[0, s], preferred_element_type=F32)
+        lag_copy(o, s).wait()
+        left = jnp.concatenate([source_ref[o * K + k, s] for k in range(K)], axis=0)
+        part = jnp.dot(left, lagged_ref[o, s], preferred_element_type=F32)
         for q in range(SLOTS):
             totals[q] = totals[q] + part * (live * (info_ref[I_SLOT + s] == q).astype(F32))
     for l in range(LAGS):
@@ -150,27 +193,24 @@
 
 
 def correlate(info, kernels, gathered):
-    def source_map(k):
-        return lambda o, info: (info[o * K + k], info[NY * K + o * K + k], 0, 0, 0)
-
     return pl.pallas_call(
         correlate_body,
         grid_spec=pltpu.PrefetchScalarGridSpec(
             num_scalar_prefetch=1,
             grid=(NY,),
-            in_specs=[
-                pl.BlockSpec(
-                    (1, SEG_CHIP, KF, LAGS * R_CH),
-                    lambda o, info: (lax.rem(info[I_Y] + NY - o, NY), 0, 0, 0),
-                )
-            ]
-            + [pl.BlockSpec((1, 1, SEG_CHIP, CQ, KF), source_map(k)) for k in range(K)],
+            in_specs=[pl.BlockSpec(memory_space=pl.ANY), pl.BlockSpec(memory_space=pl.ANY)],
             out_specs=pl.BlockSpec((1, LAGS, K * CQ, SLOTS * R_CH), lambda o, info: (o, 0, 0, 0)),
+            scratch_shapes=[
+                pltpu.VMEM((NY, SEG_CHIP, KF, LAGS * R_CH), BF),
+                pltpu.VMEM((NY * K, SEG_CHIP, CQ, KF), BF),
+                pltpu.SemaphoreType.DMA((NY, SEG_CHIP)),
+                pltpu.SemaphoreType.DMA((NY * K,)),
+            ],
         ),
         out_shape=jax.ShapeDtypeStruct((NY, LAGS, K * CQ, SLOTS * R_CH), BF),
         compiler_params=pltpu.CompilerParams(vmem_limit_bytes=VMEM),
         name="correlate",
-    )(info, kernels, *([gathered] * K))
+    )(info, kernels, gathered)
 
 
 def finish_body(parts_ref, out_ref):

time: 179 us -> 180 us (level)
  no operation moved by 1% of the time
where the time goes in v5:
time: 180 us; the launch traced here: 179 us
  waiting for transfers between devices  71.5 us (40%)
  blocking collectives  43.9 us (24%)
  Pallas kernels  26.8 us (15%)
  starting transfers between devices  17.6 us (10%)
  between operations  14.8 us (8%)
  local copies, waits for them, and re-layouts  4.27 us (2%)
    all_gather x1, waiting for transfers between devices, body(): gathered = lax.all_gather(crossed, 'z', axis=0, tiled=False)  57.8 us
    all_to_all x1, blocking collectives, body(): lax.all_to_all(sums.reshape(NY * LAGS, K * CQ, SLOTS * R_CH), ('y', 'x',...  24.5 us
    all_to_all x1, blocking collectives, body(): lax.all_to_all(split, ('y', 'c'), 0, 0).reshape(NY, SEG_CHIP, CQ, KF)  19.4 us
    ppermute x3, starting transfers between devices, body(): lax.ppermute(window, 'y', [(i, (i + d) % NY) for i in range(NY)])  12.5 us
    pallas_call x1, Pallas kernels, lag_kernels(): pl.pallas_call(lag_kernel_body, grid_spec=pltpu.PrefetchScalarGridSpec(nu...  12.4 us
    pallas_call x1, Pallas kernels, correlate(): pl.pallas_call(correlate_body, grid_spec=pltpu.PrefetchScalarGridSpec(num...  10.8 us
    ppermute x3, waiting for transfers between devices, body(): lax.ppermute(window, 'y', [(i, (i + d) % NY) for i in range(NY)])  6.84 us
    ppermute x1, waiting for transfers between devices, body(): lax.ppermute(low, ('y', 'z'), [(p, p - 1) for p in range(1, pairs)])  5.43 us
  transfers between devices with their start and end apart: 6, of which 5 were waited for; matrix products, arithmetic and copies ran while one was open for 1% of the time, Pallas kernels for 7%

profile of v5, /device:TPU:1, one launch (start us, length us, event | category | flops | bytes accessed | tf_op | source)
XLA Modules:
  0.0 179.4 jit_solution(9939007821567022634)
XLA Ops:
  6.5 0.0 all-gather.2.cloned.1.call-start
  6.5 0.0 copy-start
  6.5 1.6 copy-done
  8.1 0.0 copy-start.1
  8.1 1.2 copy-done.1
  9.4 0.0 copy-start.5
  9.4 2.6 %whiten.1 = (bf16[8,2,16,1024]{3,2,1,0:T(8,128)(2,1)S(1)}, bf16[2,64,1024]{2,1,0:T(8,128)(2,1)S(1)}, bf16[2,64,1024]{2,1,0:T(8,128)(2,1)S(1)}) custom-call(bf16[2,2048,128]{2,1,0:T(8,128)(2,1)S(1)} %copy-done.1, bf16[2,512,1024]{2,1,0:T(8,128)(2,1)S(1)} %copy-done), custom_call_target="tpu_custom_call" | custom-call | tf_op jit(solution)/shard_map/whiten/pallas_call | solution.py:96
  12.0 0.0 copy-start.3
  12.0 0.0 copy-start.4
  12.0 0.0 copy-start.6
  12.0 19.4 %all_to_all.10 = bf16[8,2,16,1024]{3,2,1,0:T(8,128)(2,1)} all-to-all(bf16[8,2,16,1024]{3,2,1,0:T(8,128)(2,1)S(1)} %get-tuple-element.14), channel_id=1, replica_groups=mesh['y'=4,'z'=16,'x'=4,'c'=2] {'y','c'}, dimensions={0} | all-to-all | bytes 1048576 | tf_op jit(solution)/shard_map/all_to_all | solution.py:245
  31.5 0.0 all-gather.2.cloned.1.call-update
  31.5 1.3 collective-permute-start
  32.8 0.0 copy-done.5
  32.8 0.6 dynamic_slice.21
  34.7 5.4 %collective-permute-done = bf16[2,64,1024]{2,1,0:T(8,128)(2,1)S(1)} collective-permute-done((bf16[2,64,1024]{2,1,0:T(8,128)(2,1)S(1)}, bf16[2,64,1024]{2,1,0:T(8,128)(2,1)S(1)}, u32[]{:S(2)}, u32[]{:S(2)}) %collective-permute-start) | collective-permute-done | bytes 262176 | tf_op jit(solution)/shard_map/ppermute | solution.py:250
  40.2 0.2 fusion
  40.4 6.0 %collective-permute-start.1 = (bf16[2,64,1024]{2,1,0:T(8,128)(2,1)S(1)}, bf16[2,64,1024]{2,1,0:T(8,128)(2,1)S(1)}, u32[]{:S(2)}, u32[]{:S(2)}) collective-permute-start(bf16[2,64,1024]{2,1,0:T(8,128)(2,1)S(1)} %fusion), channel_id=1, source_target_pairs={{0,128},{128,256},{256,384},{384,0},{1,129},{129,257},{257,385},{3... | collective-permute-start | bytes 786440 | tf_op jit(solution)/shard_map/ppermute | solution.py:255
  46.4 3.0 %collective-permute-start.2 = (bf16[2,64,1024]{2,1,0:T(8,128)(2,1)S(1)}, bf16[2,64,1024]{2,1,0:T(8,128)(2,1)S(1)}, u32[]{:S(2)}, u32[]{:S(2)}) collective-permute-start(bf16[2,64,1024]{2,1,0:T(8,128)(2,1)S(1)} %fusion), channel_id=1, source_target_pairs={{0,256},{128,384},{256,0},{384,128},{1,257},{129,385},{257,1},{385... | collective-permute-start | bytes 786440 | tf_op jit(solution)/shard_map/ppermute | solution.py:255
  49.4 3.5 %collective-permute-start.3 = (bf16[2,64,1024]{2,1,0:T(8,128)(2,1)S(1)}, bf16[2,64,1024]{2,1,0:T(8,128)(2,1)S(1)}, u32[]{:S(2)}, u32[]{:S(2)}) collective-permute-start(bf16[2,64,1024]{2,1,0:T(8,128)(2,1)S(1)} %fusion), channel_id=1, source_target_pairs={{0,384},{128,0},{256,128},{384,256},{1,385},{129,1},{257,129},{385... | collective-permute-start | bytes 786440 | tf_op jit(solution)/shard_map/ppermute | solution.py:255
  52.9 0.0 collective-permute-done.1
  52.9 5.3 %collective-permute-done.2 = bf16[2,64,1024]{2,1,0:T(8,128)(2,1)S(1)} collective-permute-done((bf16[2,64,1024]{2,1,0:T(8,128)(2,1)S(1)}, bf16[2,64,1024]{2,1,0:T(8,128)(2,1)S(1)}, u32[]{:S(2)}, u32[]{:S(2)}) %collective-permute-start.2) | collective-permute-done | bytes 262176 | tf_op jit(solution)/shard_map/ppermute | solution.py:255
  58.2 1.6 collective-permute-done.3
  59.7 0.1 pad_maximum_fusion.1
  59.9 3.8 %collective-permute-start.4 = (bf16[4,2,64,1024]{3,2,1,0:T(8,128)(2,1)S(1)}, bf16[4,2,64,1024]{3,2,1,0:T(8,128)(2,1)S(1)}, u32[]{:S(2)}, u32[]{:S(2)}) collective-permute-start(bf16[4,2,64,1024]{3,2,1,0:T(8,128)(2,1)S(1)} %pad_maximum_fusion.1), channel_id=1, source_target_pairs={{0,1},{1,0},{2,3},{3,2},{4,5},{5,4},{6,7},{7,6},{8,9},{9,8},{10,11... | collective-permute-start | bytes 3145736 | tf_op jit(solution)/shard_map/ppermute | solution.py:257
  63.7 0.0 copy-done.3
  63.7 0.1 reshape.18
  63.8 0.1 constant_dynamic-slice_fusion
  63.8 0.1 copy.11
  63.9 0.1 reshape.19
  64.0 0.0 copy-done.4
  64.0 0.1 reshape.20
  64.1 0.2 dynamic-slice_reduce_fusion
  64.3 0.0 copy-done.6
  64.3 0.1 dynamic_slice.20
  64.4 0.1 concatenate.9.info_ref
  64.5 0.0 copy-start.2
  64.5 1.4 collective-permute-done.4
  65.9 0.2 pad_maximum_fusion.window_ref
  66.2 0.0 copy-done.2
  66.2 12.4 %lag_kernels.1.kernel_ref = bf16[4,4,1024,512]{3,2,1,0:T(8,128)(2,1)} custom-call(s32[1]{0:T(128)} %bitcast.1.core_ref, bf16[4,4,64,1024]{3,2,1,0:T(8,128)(2,1)S(1)} %pad_maximum_fusion.window_ref, f32[2,8,512]{2,1,0:T(8,128)S(1)} %copy-done.2), custom_call_target="tpu_custom_call" | custom-call | tf_op jit(solution)/shard_map/lag_kernels/pallas_call | solution.py:135
  78.6 57.8 %all-gather.2.cloned.1.call-done.gathered_ref = bf16[16,4,4,16,1024]{4,3,2,1,0:T(8,128)(2,1)} async-done(((bf16[1,4,4,16,1024]{4,3,2,1,0:T(8,128)(2,1)}), bf16[16,4,4,16,1024]{4,3,2,1,0:T(8,128)(2,1)}) %all-gather.2.cloned.1.call-update) | async-done | bytes 8388624 | tf_op jit(solution)/shard_map/all_gather | solution.py:246
  136.3 10.8 %correlate.1 = bf16[4,8,128,128]{3,2,1,0:T(8,128)(2,1)S(1)} custom-call(s32[73]{0:T(128)S(1)} %concatenate.9.info_ref, bf16[4,4,1024,512]{3,2,1,0:T(8,128)(2,1)} %lag_kernels.1.kernel_ref, bf16[16,4,4,16,1024]{4,3,2,1,0:T(8,128)(2,1)} %all-gather.2.cloned.1.call-done.gathered_ref), custom_call_target="tpu_custom_call" | custom-call | tf_op jit(solution)/shard_map/correlate/pallas_call | solution.py:196
  147.2 24.5 %all_to_all.11.parts_ref = bf16[32,128,128]{2,1,0:T(8,128)(2,1)S(1)} all-to-all(bf16[32,128,128]{2,1,0:T(8,128)(2,1)S(1)} %bitcast.14), channel_id=1, replica_groups=mesh['y'=4,'z'=16,'x'=4,'c'=2] {'y','x','c'}, dimensions={0} | all-to-all | bytes 2097152 | tf_op jit(solution)/shard_map/all_to_all | solution.py:266
  171.6 0.9 finish.1
  (1 shorter events, 0.0 us)
Async XLA Ops:
  6.5 129.8 %all-gather.2.cloned.1.call-start = ((), (), s32[]{:S(2)}) async-start(), calls=%async_computation.2 | async-start | bytes 8912896 | tf_op jit(solution)/shard_map/all_gather | solution.py:246
  6.5 1.6 copy-start
  8.1 1.2 copy-start.1
  9.4 23.5 %copy-start.5 = (s32[64]{0:T(128)S(1)}, s32[64]{0:T(128)}, u32[]{:S(2)}) copy-start(s32[64]{0:T(128)} %param.10) | copy-start | bytes 772
  12.0 51.7 %copy-start.3 = (s32[64,8]{0,1:T(8,128)S(1)}, s32[64,8]{0,1:T(8,128)}, u32[]{:S(2)}) copy-start(s32[64,8]{0,1:T(8,128)} %param.8) | copy-start | bytes 6148
  12.0 52.0 %copy-start.4 = (s32[64]{0:T(128)S(1)}, s32[64]{0:T(128)}, u32[]{:S(2)}) copy-start(s32[64]{0:T(128)} %param.9) | copy-start | bytes 772
  12.0 52.3 %copy-start.6 = (s32[16]{0:T(128)S(1)}, s32[16]{0:T(128)}, u32[]{:S(2)}) copy-start(s32[16]{0:T(128)} %param.11) | copy-start | bytes 196
  31.5 8.7 %collective-permute-start = (bf16[2,64,1024]{2,1,0:T(8,128)(2,1)S(1)}, bf16[2,64,1024]{2,1,0:T(8,128)(2,1)S(1)}, u32[]{:S(2)}, u32[]{:S(2)}) collective-permute-start(bf16[2,64,1024]{2,1,0:T(8,128)(2,1)S(1)} %get-tuple-element.13), channel_id=1, source_target_pairs={{8,0},{16,8},{24,16},{32,24},{40,32},{48,40},{56,48},{64,56},{72,6... | collective-permute-start | bytes 786440 | tf_op jit(solution)/shard_map/ppermute | solution.py:250
  40.4 12.5 %collective-permute-start.1 = (bf16[2,64,1024]{2,1,0:T(8,128)(2,1)S(1)}, bf16[2,64,1024]{2,1,0:T(8,128)(2,1)S(1)}, u32[]{:S(2)}, u32[]{:S(2)}) collective-permute-start(bf16[2,64,1024]{2,1,0:T(8,128)(2,1)S(1)} %fusion), channel_id=1, source_target_pairs={{0,128},{128,256},{256,384},{384,0},{1,129},{129,257},{257,385},{3... | collective-permute-start | bytes 786440 | tf_op jit(solution)/shard_map/ppermute | solution.py:255
  46.4 11.8 %collective-permute-start.2 = (bf16[2,64,1024]{2,1,0:T(8,128)(2,1)S(1)}, bf16[2,64,1024]{2,1,0:T(8,128)(2,1)S(1)}, u32[]{:S(2)}, u32[]{:S(2)}) collective-permute-start(bf16[2,64,1024]{2,1,0:T(8,128)(2,1)S(1)} %fusion), channel_id=1, source_target_pairs={{0,256},{128,384},{256,0},{384,128},{1,257},{129,385},{257,1},{385... | collective-permute-start | bytes 786440 | tf_op jit(solution)/shard_map/ppermute | solution.py:255
  49.4 10.4 %collective-permute-start.3 = (bf16[2,64,1024]{2,1,0:T(8,128)(2,1)S(1)}, bf16[2,64,1024]{2,1,0:T(8,128)(2,1)S(1)}, u32[]{:S(2)}, u32[]{:S(2)}) collective-permute-start(bf16[2,64,1024]{2,1,0:T(8,128)(2,1)S(1)} %fusion), channel_id=1, source_target_pairs={{0,384},{128,0},{256,128},{384,256},{1,385},{129,1},{257,129},{385... | collective-permute-start | bytes 786440 | tf_op jit(solution)/shard_map/ppermute | solution.py:255
  59.9 6.1 %collective-permute-start.4 = (bf16[4,2,64,1024]{3,2,1,0:T(8,128)(2,1)S(1)}, bf16[4,2,64,1024]{3,2,1,0:T(8,128)(2,1)S(1)}, u32[]{:S(2)}, u32[]{:S(2)}) collective-permute-start(bf16[4,2,64,1024]{3,2,1,0:T(8,128)(2,1)S(1)} %pad_maximum_fusion.1), channel_id=1, source_target_pairs={{0,1},{1,0},{2,3},{3,2},{4,5},{5,4},{6,7},{7,6},{8,9},{9,8},{10,11... | collective-permute-start | bytes 3145736 | tf_op jit(solution)/shard_map/ppermute | solution.py:257
  64.5 1.7 copy-start.2
Sparse Core Ops, SparseCore 0:
  31.6 104.6 all-gather.1

commit v6 on v5

--- a/solution.py
+++ b/solution.py
@@ -19,6 +19,8 @@
 NY, NZ, NX, NC = 4, 16, 4, 2
 SEG = 2
 SEG_CHIP = SEG * NC
+MOST = 3
+SCALE = 4096.0
 PIECES = NY * NC
 CQ = CH // PIECES
 FB = 128
@@ -45,7 +47,7 @@
     lags = np.arange(LAGS, dtype=np.int64) - LAGS // 2
     phase = (lags[:, None] * bins[None, :]) % SAMPLES
     angle = phase.astype(np.float32) * np.float32(2.0 * np.pi / SAMPLES)
-    return np.stack([np.cos(angle), np.sin(angle)], axis=0).astype(np.float32)
+    return (np.stack([np.cos(angle), np.sin(angle)], axis=0) * NORM).astype(np.float32)
 
 
 def whiten_kernel(traces_hbm, table_hbm, split_ref, low_ref, high_ref, traces_ref, table_ref, trace_sems, table_sems):
@@ -114,21 +116,26 @@
     )(traces, table)
 
 
-def lag_kernel_body(core_ref, window_ref, lag_ref, out_ref):
+def lag_kernel_body(core_ref, window_ref, lag_ref, out_ref, wide_ref):
+    @pl.when((pl.program_id(0) == 0) & (pl.program_id(1) == 0))
+    def _():
+        for part in range(2):
+            columns = lag_ref[part].T
+            for l in range(0, LAGS, 2):
+                both = [jnp.broadcast_to(columns[:, m : m + 1], (NF, R_CH)) for m in (l, l + 1)]
+                wide_ref[part, :, l * R_CH : (l + 2) * R_CH] = jnp.concatenate(both, axis=1)
+
     for b in range(NB):
         at = b * 2 * FB
-        real = window_ref[0, 0, :, at : at + FB].astype(F32)
-        imag = window_ref[0, 0, :, at + FB : at + 2 * FB].astype(F32)
+        bins = slice(b * FB, (b + 1) * FB)
+        window = window_ref[0, 0, :, at : at + 2 * FB].astype(F32).T
+        window = jnp.concatenate([window, window], axis=1)
+        real, imag = window[:FB], window[FB:]
         for l in range(0, LAGS, 2):
-            reals, imags = [], []
-            for m in (l, l + 1):
-                cos = lag_ref[0, m : m + 1, b * FB : (b + 1) * FB]
-                sin = lag_ref[1, m : m + 1, b * FB : (b + 1) * FB]
-                reals.append((cos * real + sin * imag) * NORM)
-                imags.append((cos * imag - sin * real) * NORM)
             lanes = slice(l * R_CH, (l + 2) * R_CH)
-            out_ref[0, 0, at : at + FB, lanes] = jnp.concatenate(reals, axis=0).T.astype(BF)
-            out_ref[0, 0, at + FB : at + 2 * FB, lanes] = jnp.concatenate(imags, axis=0).T.astype(BF)
+            cos, sin = wide_ref[0, bins, lanes], wide_ref[1, bins, lanes]
+            out_ref[0, 0, at : at + FB, lanes] = (cos * real + sin * imag).astype(BF)
+            out_ref[0, 0, at + FB : at + 2 * FB, lanes] = (cos * imag - sin * real).astype(BF)
 
 
 def lag_kernels(core, windows, lags):
@@ -145,6 +152,7 @@
                 (1, 1, KF, LAGS * R_CH),
                 lambda o, s, core: (o, lax.rem(s + SEG * core[0], SEG_CHIP), 0, 0),
             ),
+            scratch_shapes=[pltpu.VMEM((2, NF, LAGS * R_CH), F32)],
         ),
         out_shape=jax.ShapeDtypeStruct((NY, SEG_CHIP, KF, LAGS * R_CH), BF),
         compiler_params=pltpu.CompilerParams(vmem_limit_bytes=VMEM),
@@ -157,12 +165,17 @@
 I_Y = I_SLOT + SEG_CHIP
 
 
-def correlate_body(info_ref, kernel_ref, gathered_ref, out_ref, lagged_ref, source_ref, lag_sems, source_sems):
+def correlate_body(info_ref, kernel_ref, most_ref, last_ref, out_ref, lagged_ref, source_ref, lag_sems, source_sems):
     o = pl.program_id(0)
 
-    def source_copy(n):
-        source = gathered_ref.at[info_ref[n], info_ref[NY * K + n]]
-        return pltpu.make_async_copy(source, source_ref.at[n], source_sems.at[n])
+    def source_copies(n):
+        most = most_ref.at[info_ref[n], info_ref[NY * K + n]]
+        last = last_ref.at[info_ref[n], info_ref[NY * K + n]]
+        into = source_ref.at[n]
+        return (
+            pltpu.make_async_copy(most, into.at[pl.ds(0, MOST)], source_sems.at[0, n]),
+            pltpu.make_async_copy(last, into.at[pl.ds(MOST, SEG_CHIP - MOST)], source_sems.at[1, n]),
+        )
 
     def lag_copy(n, s):
         owner = lax.rem(info_ref[I_Y] + NY - n, NY)
@@ -172,12 +185,14 @@
     def _():
         for n in range(NY):
             for k in range(K):
-                source_copy(n * K + k).start()
+                for copy in source_copies(n * K + k):
+                    copy.start()
             for s in range(SEG_CHIP):
                 lag_copy(n, s).start()
 
     for k in range(K):
-        source_copy(o * K + k).wait()
+        for copy in source_copies(o * K + k):
+            copy.wait()
     row = lax.broadcasted_iota(jnp.int32, (K * CQ, 1), 0)
     live = (row < info_ref[I_COUNT + o] * CQ).astype(F32)
     totals = [0.0] * SLOTS
@@ -192,25 +207,25 @@
         out_ref[0, l] = both.astype(BF)
 
 
-def correlate(info, kernels, gathered):
+def correlate(info, kernels, most, last):
     return pl.pallas_call(
         correlate_body,
         grid_spec=pltpu.PrefetchScalarGridSpec(
             num_scalar_prefetch=1,
             grid=(NY,),
-            in_specs=[pl.BlockSpec(memory_space=pl.ANY), pl.BlockSpec(memory_space=pl.ANY)],
+            in_specs=[pl.BlockSpec(memory_space=pl.ANY)] * 3,
             out_specs=pl.BlockSpec((1, LAGS, K * CQ, SLOTS * R_CH), lambda o, info: (o, 0, 0, 0)),
             scratch_shapes=[
                 pltpu.VMEM((NY, SEG_CHIP, KF, LAGS * R_CH), BF),
                 pltpu.VMEM((NY * K, SEG_CHIP, CQ, KF), BF),
                 pltpu.SemaphoreType.DMA((NY, SEG_CHIP)),
-                pltpu.SemaphoreType.DMA((NY * K,)),
+                pltpu.SemaphoreType.DMA((2, NY * K)),
             ],
         ),
         out_shape=jax.ShapeDtypeStruct((NY, LAGS, K * CQ, SLOTS * R_CH), BF),
         compiler_params=pltpu.CompilerParams(vmem_limit_bytes=VMEM),
         name="correlate",
-    )(info, kernels, gathered)
+    )(info, kernels, most, last)
 
 
 def finish_body(parts_ref, out_ref):
@@ -243,11 +258,15 @@
     lags = jnp.asarray(lag_tables())
     split, low, high = whiten(traces, table)
     crossed = lax.all_to_all(split, ("y", "c"), 0, 0).reshape(NY, SEG_CHIP, CQ, KF)
-    gathered = lax.all_gather(crossed, "z", axis=0, tiled=False)
+    most = lax.all_gather(crossed[:, :MOST], "z", axis=0, tiled=False)
+    last = (crossed[:, MOST:] * jnp.bfloat16(SCALE)).astype(jnp.float16)
+    last = lax.all_gather(last, "z", axis=0, tiled=False)
 
     low, high, _ = lax.optimization_barrier((low, high, crossed))
     pairs = NY * NZ
     following = lax.ppermute(low, ("y", "z"), [(p, p - 1) for p in range(1, pairs)])
+    following, last = lax.optimization_barrier((following, last))
+    last = (last.astype(F32) * (1.0 / SCALE)).astype(BF)
     joined = jnp.concatenate([high, following], axis=1)
     offset = lax.dynamic_index_in_dim(receiver_start, y * NZ + z, keepdims=False) - CH // 2
     window = lax.dynamic_slice_in_dim(joined, offset, R_CH, 1)
@@ -262,7 +281,7 @@
     counts = lax.dynamic_index_in_dim(source_count.reshape(NY, NZ), z, 1, keepdims=False)
     slots = lax.dynamic_slice_in_dim(segment_slot, lax.axis_index("x") * SEG_CHIP, SEG_CHIP, 0)
     info = jnp.concatenate([lists % NZ, lists // NZ, counts, slots, y[None].astype(jnp.int32)])
-    sums = correlate(info, kernels, gathered)
+    sums = correlate(info, kernels, most, last)
     parts = lax.all_to_all(sums.reshape(NY * LAGS, K * CQ, SLOTS * R_CH), ("y", "x", "c"), 0, 0)
     return finish(parts)
 

time: 180 us -> 193 us (1.072)
  waiting for transfers between devices: 71.5 us -> 3.3 us
  blocking collectives: 43.9 us -> 111 us
  starting transfers between devices: 17.6 us -> 25.3 us
  other arithmetic: 0.56 us -> 4.08 us
    all_gather x0 -> x1, blocking collectives: none -> 67.7 us  [body(): last = lax.all_gather(last, 'z', axis=0, tiled=False)]
    all_gather x1, waiting for transfers between devices: 57.8 us -> 0.01 us  [body(): most = lax.all_gather(crossed[:, :MOST], 'z', axis=0, tiled=False)]
    ppermute x1, starting transfers between devices: 3.78 us -> 11.2 us  [body(): other = lax.ppermute(own, 'c', [(0, 1), (1, 0)])]
    ppermute x1, waiting for transfers between devices: 5.43 us -> 0.01 us  [body(): lax.ppermute(low, ('y', 'z'), [(p, p - 1) for p in range(1, pairs)])]
    ppermute x3, waiting for transfers between devices: 6.84 us -> 3.27 us  [body(): lax.ppermute(window, 'y', [(i, (i + d) % NY) for i in range(NY)])]
    convert_element_type x0 -> x2, other arithmetic: none -> 2.28 us  [the longest x1 2.25 us: body(): last = (last.astype(F32) * (1.0 / SCALE)).astype(BF)]
  transfers between devices with their start and end apart: 6 -> 6, of which waited for: 5 -> 2; matrix products, arithmetic and copies ran while one was open for 1% -> 3% of each run, Pallas kernels for 7% -> 7%
where the time goes in v6:
time: 193 us; the launch traced here: 192 us
  blocking collectives  111 us (58%)
  Pallas kernels  27.9 us (14%)
  starting transfers between devices  25.3 us (13%)
  between operations  14.9 us (8%)
  local copies, waits for them, and re-layouts  5.59 us (3%)
  other arithmetic  4.08 us (2%)
  waiting for transfers between devices  3.3 us (2%)
    all_gather x1, blocking collectives, body(): last = lax.all_gather(last, 'z', axis=0, tiled=False)  67.7 us
    all_to_all x1, blocking collectives, body(): lax.all_to_all(sums.reshape(NY * LAGS, K * CQ, SLOTS * R_CH), ('y', 'x',...  24.7 us
    all_to_all x1, blocking collectives, body(): lax.all_to_all(split, ('y', 'c'), 0, 0).reshape(NY, SEG_CHIP, CQ, KF)  18.6 us
    pallas_call x1, Pallas kernels, lag_kernels(): pl.pallas_call(lag_kernel_body, grid_spec=pltpu.PrefetchScalarGridSpec(nu...  14.2 us
    ppermute x3, starting transfers between devices, body(): lax.ppermute(window, 'y', [(i, (i + d) % NY) for i in range(NY)])  12.8 us
    ppermute x1, starting transfers between devices, body(): other = lax.ppermute(own, 'c', [(0, 1), (1, 0)])  11.2 us
    pallas_call x1, Pallas kernels, correlate(): pl.pallas_call(correlate_body, grid_spec=pltpu.PrefetchScalarGridSpec(num...  10.2 us
  transfers between devices with their start and end apart: 6, of which 2 were waited for; matrix products, arithmetic and copies ran while one was open for 3% of the time, Pallas kernels for 7%

profile of v6, /device:TPU:1, one launch (start us, length us, event | category | flops | bytes accessed | tf_op | source)
XLA Modules:
  0.0 192.1 jit_solution(15772568161276629900)
XLA Ops:
  6.5 0.0 all-gather.5.cloned.1.call-start
  6.5 0.0 copy-start
  6.5 1.6 copy-done
  8.1 0.0 copy-start.1
  8.1 1.2 copy-done.1
  9.4 0.0 copy-start.11
  9.4 2.6 %whiten.1 = (bf16[8,2,16,1024]{3,2,1,0:T(8,128)(2,1)S(1)}, bf16[2,64,1024]{2,1,0:T(8,128)(2,1)S(1)}, bf16[2,64,1024]{2,1,0:T(8,128)(2,1)S(1)}) custom-call(bf16[2,2048,128]{2,1,0:T(8,128)(2,1)S(1)} %copy-done.1, bf16[2,512,1024]{2,1,0:T(8,128)(2,1)S(1)} %copy-done), custom_call_target="tpu_custom_call" | custom-call | tf_op jit(solution)/shard_map/whiten/pallas_call | solution.py:98
  12.0 18.6 %all_to_all.10 = bf16[8,2,16,1024]{3,2,1,0:T(8,128)(2,1)S(1)} all-to-all(bf16[8,2,16,1024]{3,2,1,0:T(8,128)(2,1)S(1)} %get-tuple-element.14), channel_id=1, replica_groups=mesh['y'=4,'z'=16,'x'=4,'c'=2] {'y','c'}, dimensions={0} | all-to-all | bytes 1048576 | tf_op jit(solution)/shard_map/all_to_all | solution.py:260
  30.6 0.8 slice.9
  31.4 0.0 all-gather.5.cloned.1.call-update
  31.5 0.0 copy-done.11
  31.5 0.6 dynamic_slice.21
  33.4 1.3 collective-permute-start
  34.7 0.0 copy-start.9
  34.7 0.0 copy-start.10
  34.7 0.0 copy-start.12
  34.7 67.7 %all-gather.6 = f16[64,1,16,1024]{3,2,1,0:T(8,128)(2,1)} all-gather(f16[4,1,16,1024]{3,2,1,0:T(8,128)(2,1)S(1)} %fusion.1), channel_id=2, replica_groups=mesh['y'=4,'z'=16,'x'=4,'c'=2] {'z'}, dimensions={0}, use_global_device_ids=true | all-gather | bytes 2228224 | tf_op jit(solution)/shard_map/all_gather | solution.py:263
  102.5 0.0 collective-permute-done
  102.5 0.2 fusion
  102.7 6.6 %collective-permute-start.1 = (bf16[2,64,1024]{2,1,0:T(8,128)(2,1)S(1)}, bf16[2,64,1024]{2,1,0:T(8,128)(2,1)S(1)}, u32[]{:S(2)}, u32[]{:S(2)}) collective-permute-start(bf16[2,64,1024]{2,1,0:T(8,128)(2,1)S(1)} %fusion), channel_id=1, source_target_pairs={{0,128},{128,256},{256,384},{384,0},{1,129},{129,257},{257,385},{3... | collective-permute-start | bytes 786440 | tf_op jit(solution)/shard_map/ppermute | solution.py:274
  109.3 1.9 collective-permute-start.2
  111.2 4.3 %collective-permute-start.3 = (bf16[2,64,1024]{2,1,0:T(8,128)(2,1)S(1)}, bf16[2,64,1024]{2,1,0:T(8,128)(2,1)S(1)}, u32[]{:S(2)}, u32[]{:S(2)}) collective-permute-start(bf16[2,64,1024]{2,1,0:T(8,128)(2,1)S(1)} %fusion), channel_id=1, source_target_pairs={{0,384},{128,0},{256,128},{384,256},{1,385},{129,1},{257,129},{385... | collective-permute-start | bytes 786440 | tf_op jit(solution)/shard_map/ppermute | solution.py:274
  115.5 0.0 collective-permute-done.1
  115.5 0.0 copy-start.3
  115.5 2.6 %collective-permute-done.2 = bf16[2,64,1024]{2,1,0:T(8,128)(2,1)S(1)} collective-permute-done((bf16[2,64,1024]{2,1,0:T(8,128)(2,1)S(1)}, bf16[2,64,1024]{2,1,0:T(8,128)(2,1)S(1)}, u32[]{:S(2)}, u32[]{:S(2)}) %collective-permute-start.2) | collective-permute-done | bytes 262176 | tf_op jit(solution)/shard_map/ppermute | solution.py:274
  118.2 0.0 copy-start.5
  118.2 0.6 collective-permute-done.3
  118.8 0.0 copy-start.7
  118.8 0.0 copy-done.3
  118.8 0.1 pad_maximum_fusion.1
  119.0 0.0 copy-done.5
  119.0 0.6 copy-done.7
  119.5 11.2 %collective-permute-start.4 = (bf16[4,2,64,1024]{3,2,1,0:T(8,128)(2,1)S(1)}, bf16[4,2,64,1024]{3,2,1,0:T(8,128)(2,1)}, u32[]{:S(2)}, u32[]{:S(2)}) collective-permute-start(bf16[4,2,64,1024]{3,2,1,0:T(8,128)(2,1)S(1)} %pad_maximum_fusion.1), channel_id=1, source_target_pairs={{0,1},{1,0},{2,3},{3,2},{4,5},{5,4},{6,7},{7,6},{8,9},{9,8},{10,11... | collective-permute-start | bytes 3145736 | tf_op jit(solution)/shard_map/ppermute | solution.py:276
  130.7 0.0 copy-done.9
  130.7 0.1 reshape.20
  130.8 0.1 constant_dynamic-slice_fusion
  130.9 0.1 copy.13
  131.0 0.1 reshape.21
  131.0 0.0 copy-done.10
  131.0 0.1 reshape.22
  131.1 0.2 dynamic-slice_reduce_fusion
  131.3 0.0 copy-done.12
  131.3 0.1 dynamic_slice.20
  131.4 0.1 concatenate.9.info_ref
  131.5 0.0 copy-start.4
  131.5 0.0 copy-start.6
  131.5 0.0 copy-start.8
  131.5 2.3 %multiply_convert_fusion.last_ref = bf16[16,4,1,16,1024]{4,3,2,1,0:T(8,128)(2,1)S(1)} fusion(f16[16,4,1,16,1024]{4,3,2,1,0:T(8,128)(2,1)} %bitcast.17), kind=kLoop, calls=%fused_computation | loop fusion | flops 3145728 | bytes 4194304 | tf_op jit(solution)/shard_map/convert_element_type | solution.py:269
  133.8 0.0 copy-start.2
  133.8 0.0 collective-permute-done.4
  133.8 0.0 copy-done.4
  133.8 0.0 copy-done.6
  133.8 0.0 copy-done.8
  133.8 1.5 pad_maximum_fusion.window_ref
  135.3 0.0 copy-done.2
  135.3 14.2 %lag_kernels.1.kernel_ref = bf16[4,4,1024,512]{3,2,1,0:T(8,128)(2,1)} custom-call(s32[1]{0:T(128)} %bitcast.1.core_ref, bf16[4,4,64,1024]{3,2,1,0:T(8,128)(2,1)S(1)} %pad_maximum_fusion.window_ref, f32[2,8,512]{2,1,0:T(8,128)S(1)} %copy-done.2), custom_call_target="tpu_custom_call" | custom-call | tf_op jit(solution)/shard_map/lag_kernels/pallas_call | solution.py:142
  149.5 0.0 all-gather.5.cloned.1.call-done
  149.5 10.2 %correlate.1 = bf16[4,8,128,128]{3,2,1,0:T(8,128)(2,1)S(1)} custom-call(s32[73]{0:T(128)S(1)} %concatenate.9.info_ref, bf16[4,4,1024,512]{3,2,1,0:T(8,128)(2,1)} %lag_kernels.1.kernel_ref, bf16[16,4,3,16,1024]{4,3,2,1,0:T(8,128)(2,1)} %bitcast.18, bf16[16,4,1,16,1024]{4,3,2,1,0:T(8,128)(2,1)S(1)} %multiply_convert_fusion.last_ref), custom_call_target="tpu_custom_call" | custom-call | tf_op jit(solution)/shard_map/correlate/pallas_call | solution.py:211
  159.7 24.7 %all_to_all.11.parts_ref = bf16[32,128,128]{2,1,0:T(8,128)(2,1)S(1)} all-to-all(bf16[32,128,128]{2,1,0:T(8,128)(2,1)S(1)} %bitcast.16), channel_id=1, replica_groups=mesh['y'=4,'z'=16,'x'=4,'c'=2] {'y','x','c'}, dimensions={0} | all-to-all | bytes 2097152 | tf_op jit(solution)/shard_map/all_to_all | solution.py:285
  184.3 0.9 finish.1
  (2 shorter events, 0.0 us)
Async XLA Ops:
  6.5 143.0 %all-gather.5.cloned.1.call-start = ((), (), s32[]{:S(2)}) async-start(), calls=%async_computation.2 | async-start | bytes 6684672 | tf_op jit(solution)/shard_map/all_gather | solution.py:261
  6.5 1.6 copy-start
  8.1 1.2 copy-start.1
  9.4 22.1 %copy-start.11 = (s32[64]{0:T(128)S(1)}, s32[64]{0:T(128)}, u32[]{:S(2)}) copy-start(s32[64]{0:T(128)} %param.10) | copy-start | bytes 772
  33.4 69.1 %collective-permute-start = (bf16[2,64,1024]{2,1,0:T(8,128)(2,1)S(1)}, bf16[2,64,1024]{2,1,0:T(8,128)(2,1)S(1)}, u32[]{:S(2)}, u32[]{:S(2)}) collective-permute-start(bf16[2,64,1024]{2,1,0:T(8,128)(2,1)S(1)} %get-tuple-element.16), channel_id=1, source_target_pairs={{8,0},{16,8},{24,16},{32,24},{40,32},{48,40},{56,48},{64,56},{72,6... | collective-permute-start | bytes 786440 | tf_op jit(solution)/shard_map/ppermute | solution.py:267
  34.7 96.0 %copy-start.9 = (s32[64,8]{0,1:T(8,128)S(1)}, s32[64,8]{0,1:T(8,128)}, u32[]{:S(2)}) copy-start(s32[64,8]{0,1:T(8,128)} %param.8) | copy-start | bytes 6148
  34.7 96.3 %copy-start.10 = (s32[64]{0:T(128)S(1)}, s32[64]{0:T(128)}, u32[]{:S(2)}) copy-start(s32[64]{0:T(128)} %param.9) | copy-start | bytes 772
  34.7 96.6 %copy-start.12 = (s32[16]{0:T(128)S(1)}, s32[16]{0:T(128)}, u32[]{:S(2)}) copy-start(s32[16]{0:T(128)} %param.11) | copy-start | bytes 196
  102.7 12.9 %collective-permute-start.1 = (bf16[2,64,1024]{2,1,0:T(8,128)(2,1)S(1)}, bf16[2,64,1024]{2,1,0:T(8,128)(2,1)S(1)}, u32[]{:S(2)}, u32[]{:S(2)}) collective-permute-start(bf16[2,64,1024]{2,1,0:T(8,128)(2,1)S(1)} %fusion), channel_id=1, source_target_pairs={{0,128},{128,256},{256,384},{384,0},{1,129},{129,257},{257,385},{3... | collective-permute-start | bytes 786440 | tf_op jit(solution)/shard_map/ppermute | solution.py:274
  109.3 8.9 %collective-permute-start.2 = (bf16[2,64,1024]{2,1,0:T(8,128)(2,1)S(1)}, bf16[2,64,1024]{2,1,0:T(8,128)(2,1)S(1)}, u32[]{:S(2)}, u32[]{:S(2)}) collective-permute-start(bf16[2,64,1024]{2,1,0:T(8,128)(2,1)S(1)} %fusion), channel_id=1, source_target_pairs={{0,256},{128,384},{256,0},{384,128},{1,257},{129,385},{257,1},{385... | collective-permute-start | bytes 786440 | tf_op jit(solution)/shard_map/ppermute | solution.py:274
  111.2 7.6 %collective-permute-start.3 = (bf16[2,64,1024]{2,1,0:T(8,128)(2,1)S(1)}, bf16[2,64,1024]{2,1,0:T(8,128)(2,1)S(1)}, u32[]{:S(2)}, u32[]{:S(2)}) collective-permute-start(bf16[2,64,1024]{2,1,0:T(8,128)(2,1)S(1)} %fusion), channel_id=1, source_target_pairs={{0,384},{128,0},{256,128},{384,256},{1,385},{129,1},{257,129},{385... | collective-permute-start | bytes 786440 | tf_op jit(solution)/shard_map/ppermute | solution.py:274
  115.5 3.3 %copy-start.3 = (bf16[2,64,1024]{2,1,0:T(8,128)(2,1)}, bf16[2,64,1024]{2,1,0:T(8,128)(2,1)S(1)}, u32[]{:S(2)}) copy-start(bf16[2,64,1024]{2,1,0:T(8,128)(2,1)S(1)} %collective-permute-done.1) | copy-start | bytes 786436
  118.2 0.8 copy-start.5
  118.8 0.7 copy-start.7
  119.5 14.3 %collective-permute-start.4 = (bf16[4,2,64,1024]{3,2,1,0:T(8,128)(2,1)S(1)}, bf16[4,2,64,1024]{3,2,1,0:T(8,128)(2,1)}, u32[]{:S(2)}, u32[]{:S(2)}) collective-permute-start(bf16[4,2,64,1024]{3,2,1,0:T(8,128)(2,1)S(1)} %pad_maximum_fusion.1), channel_id=1, source_target_pairs={{0,1},{1,0},{2,3},{3,2},{4,5},{5,4},{6,7},{7,6},{8,9},{9,8},{10,11... | collective-permute-start | bytes 3145736 | tf_op jit(solution)/shard_map/ppermute | solution.py:276
  131.5 2.3 %copy-start.4 = (bf16[2,64,1024]{2,1,0:T(8,128)(2,1)S(1)}, bf16[2,64,1024]{2,1,0:T(8,128)(2,1)}, u32[]{:S(2)}) copy-start(bf16[2,64,1024]{2,1,0:T(8,128)(2,1)} %copy-done.3) | copy-start | bytes 786436
  131.5 2.3 %copy-start.6 = (bf16[2,64,1024]{2,1,0:T(8,128)(2,1)S(1)}, bf16[2,64,1024]{2,1,0:T(8,128)(2,1)}, u32[]{:S(2)}) copy-start(bf16[2,64,1024]{2,1,0:T(8,128)(2,1)} %copy-done.5) | copy-start | bytes 786436
  131.5 2.3 %copy-start.8 = (bf16[2,64,1024]{2,1,0:T(8,128)(2,1)S(1)}, bf16[2,64,1024]{2,1,0:T(8,128)(2,1)}, u32[]{:S(2)}) copy-start(bf16[2,64,1024]{2,1,0:T(8,128)(2,1)} %copy-done.7) | copy-start | bytes 786436
  133.8 1.5 copy-start.2
Sparse Core Ops, SparseCore 0:
  31.6 102.7 all-gather.4

commit v7 on v4

--- a/solution.py
+++ b/solution.py
@@ -48,9 +48,30 @@
     return np.stack([np.cos(angle), np.sin(angle)], axis=0).astype(np.float32)
 
 
-def whiten_kernel(traces_ref, table_ref, split_ref, low_ref, high_ref):
+def whiten_kernel(traces_hbm, table_hbm, split_ref, low_ref, high_ref, traces_ref, table_ref, trace_sems, table_sems):
     half = SAMPLES // 2
-    table = table_ref[...].reshape(2 * FB, half)
+    g = pl.program_id(0)
+
+    def trace_copy(s, h):
+        part = pl.ds(h * half, half)
+        return pltpu.make_async_copy(traces_hbm.at[s, part], traces_ref.at[s, part], trace_sems.at[s, h])
+
+    def table_copy(b):
+        return pltpu.make_async_copy(table_hbm.at[:, pl.ds(b * FB, FB)], table_ref.at[b], table_sems.at[b])
+
+    @pl.when(g == 0)
+    def _():
+        for s in range(SEG):
+            for h in range(2):
+                trace_copy(s, h).start()
+        for b in range(NB):
+            table_copy(b).start()
+        for s in range(SEG):
+            for h in range(2):
+                trace_copy(s, h).wait()
+
+    table_copy(g).wait()
+    table = table_ref[g].reshape(2 * FB, half)
     early = jnp.concatenate([traces_ref[s, :half] for s in range(SEG)], axis=1)
     late = jnp.concatenate([traces_ref[s, half:] for s in range(SEG)], axis=1)
     early = jnp.dot(table, early, preferred_element_type=F32)
@@ -75,17 +96,20 @@
     return pl.pallas_call(
         whiten_kernel,
         grid=(NB,),
-        in_specs=[
-            pl.BlockSpec((SEG, SAMPLES, CH), lambda g: (0, 0, 0)),
-            pl.BlockSpec((2, FB, SAMPLES // 2), lambda g: (0, g, 0)),
-        ],
+        in_specs=[pl.BlockSpec(memory_space=pl.ANY), pl.BlockSpec(memory_space=pl.ANY)],
         out_specs=[
             pl.BlockSpec((PIECES, SEG, CQ, 2 * FB), lambda g: (0, 0, 0, g)),
             half_spec,
             half_spec,
         ],
         out_shape=[jax.ShapeDtypeStruct((PIECES, SEG, CQ, KF), BF), half, half],
-        compiler_params=pltpu.CompilerParams(vmem_limit_bytes=VMEM),
+        scratch_shapes=[
+            pltpu.VMEM((SEG, SAMPLES, CH), BF),
+            pltpu.VMEM((NB, 2, FB, SAMPLES // 2), BF),
+            pltpu.SemaphoreType.DMA((SEG, 2)),
+            pltpu.SemaphoreType.DMA((NB,)),
+        ],
+        compiler_params=pltpu.CompilerParams(vmem_limit_bytes=61 * 1024 * 1024),
         name="whiten",
     )(traces, table)
 

time: 179 us -> 179 us (level)
  local copies, waits for them, and re-layouts: 4.27 us -> 1.42 us
  Pallas kernels: 26.3 us -> 28.5 us
    unnamed x15 -> x11, local copies, waits for them, and re-layouts: 2.95 us -> 0.13 us
    pallas_call x1, Pallas kernels: 2.5 us -> 4.78 us  [whiten(): pl.pallas_call(whiten_kernel, grid=(NB,), in_specs=[pl.BlockSpec(memory_s...]
  transfers between devices with their start and end apart: 6 -> 6, of which waited for: 5 -> 5; matrix products, arithmetic and copies ran while one was open for 1% -> 2% of each run, Pallas kernels for 7% -> 7%
where the time goes in v7:
time: 179 us
  waiting for transfers between devices  70.5 us (39%)
  blocking collectives  45 us (25%)
  Pallas kernels  28.5 us (16%)
  starting transfers between devices  16.8 us (9%)
  between operations  14.8 us (8%)
    all_gather x1, waiting for transfers between devices, body(): gathered = lax.all_gather(crossed, 'z', axis=0, tiled=False)  56.6 us
    all_to_all x1, blocking collectives, body(): lax.all_to_all(sums.reshape(NY * LAGS, K * CQ, SLOTS * R_CH), ('y', 'x',...  24.5 us
    all_to_all x1, blocking collectives, body(): lax.all_to_all(split, ('y', 'c'), 0, 0).reshape(NY, SEG_CHIP, CQ, KF)  20.5 us
    pallas_call x1, Pallas kernels, lag_kernels(): pl.pallas_call(lag_kernel_body, grid_spec=pltpu.PrefetchScalarGridSpec(nu...  12.4 us
    ppermute x3, starting transfers between devices, body(): lax.ppermute(window, 'y', [(i, (i + d) % NY) for i in range(NY)])  11.8 us
    pallas_call x1, Pallas kernels, correlate(): pl.pallas_call(correlate_body, grid_spec=pltpu.PrefetchScalarGridSpec(num...  10.5 us
    ppermute x3, waiting for transfers between devices, body(): lax.ppermute(window, 'y', [(i, (i + d) % NY) for i in range(NY)])  6.84 us
    ppermute x1, waiting for transfers between devices, body(): lax.ppermute(low, ('y', 'z'), [(p, p - 1) for p in range(1, pairs)])  5.65 us
  transfers between devices with their start and end apart: 6, of which 5 were waited for; matrix products, arithmetic and copies ran while one was open for 2% of the time, Pallas kernels for 7%

profile of v7, /device:TPU:1, one launch (start us, length us, event | category | flops | bytes accessed | tf_op | source)
XLA Modules:
  0.0 178.6 jit_solution(13494582761243438618)
XLA Ops:
  6.5 0.0 copy-start.3
  6.5 0.0 all-gather.2.cloned.1.call-start
  6.5 4.8 %whiten.1 = (bf16[8,2,16,1024]{3,2,1,0:T(8,128)(2,1)}, bf16[2,64,1024]{2,1,0:T(8,128)(2,1)}, bf16[2,64,1024]{2,1,0:T(8,128)(2,1)}) custom-call(bf16[2,2048,128]{2,1,0:T(8,128)(2,1)} %traces_hbm.1, bf16[2,512,1024]{2,1,0:T(8,128)(2,1)} %constant.72.clone.table_hbm), custom_call_target="tpu_custom_call" | custom-call | tf_op jit(solution)/shard_map/whiten/pallas_call | solution.py:96
  11.3 0.0 copy-start.1
  11.3 0.0 copy-start.2
  11.3 0.0 copy-start.4
  11.4 20.5 %all_to_all.10 = bf16[8,2,16,1024]{3,2,1,0:T(8,128)(2,1)} all-to-all(bf16[8,2,16,1024]{3,2,1,0:T(8,128)(2,1)} %get-tuple-element.14), channel_id=1, replica_groups=mesh['y'=4,'z'=16,'x'=4,'c'=2] {'y','c'}, dimensions={0} | all-to-all | bytes 1048576 | tf_op jit(solution)/shard_map/all_to_all | solution.py:229
  31.9 0.0 all-gather.2.cloned.1.call-update
  31.9 1.3 collective-permute-start
  33.2 0.0 copy-done.3
  33.2 0.6 dynamic_slice.21
  35.1 5.7 %collective-permute-done = bf16[2,64,1024]{2,1,0:T(8,128)(2,1)S(1)} collective-permute-done((bf16[2,64,1024]{2,1,0:T(8,128)(2,1)}, bf16[2,64,1024]{2,1,0:T(8,128)(2,1)S(1)}, u32[]{:S(2)}, u32[]{:S(2)}) %collective-permute-start) | collective-permute-done | bytes 262176 | tf_op jit(solution)/shard_map/ppermute | solution.py:234
  40.7 1.1 fusion
  41.9 5.2 %collective-permute-start.1 = (bf16[2,64,1024]{2,1,0:T(8,128)(2,1)S(1)}, bf16[2,64,1024]{2,1,0:T(8,128)(2,1)S(1)}, u32[]{:S(2)}, u32[]{:S(2)}) collective-permute-start(bf16[2,64,1024]{2,1,0:T(8,128)(2,1)S(1)} %fusion), channel_id=1, source_target_pairs={{0,128},{128,256},{256,384},{384,0},{1,129},{129,257},{257,385},{3... | collective-permute-start | bytes 786440 | tf_op jit(solution)/shard_map/ppermute | solution.py:239
  47.1 3.0 %collective-permute-start.2 = (bf16[2,64,1024]{2,1,0:T(8,128)(2,1)S(1)}, bf16[2,64,1024]{2,1,0:T(8,128)(2,1)S(1)}, u32[]{:S(2)}, u32[]{:S(2)}) collective-permute-start(bf16[2,64,1024]{2,1,0:T(8,128)(2,1)S(1)} %fusion), channel_id=1, source_target_pairs={{0,256},{128,384},{256,0},{384,128},{1,257},{129,385},{257,1},{385... | collective-permute-start | bytes 786440 | tf_op jit(solution)/shard_map/ppermute | solution.py:239
  50.1 3.5 %collective-permute-start.3 = (bf16[2,64,1024]{2,1,0:T(8,128)(2,1)S(1)}, bf16[2,64,1024]{2,1,0:T(8,128)(2,1)S(1)}, u32[]{:S(2)}, u32[]{:S(2)}) collective-permute-start(bf16[2,64,1024]{2,1,0:T(8,128)(2,1)S(1)} %fusion), channel_id=1, source_target_pairs={{0,384},{128,0},{256,128},{384,256},{1,385},{129,1},{257,129},{385... | collective-permute-start | bytes 786440 | tf_op jit(solution)/shard_map/ppermute | solution.py:239
  53.7 0.0 collective-permute-done.1
  53.7 5.2 %collective-permute-done.2 = bf16[2,64,1024]{2,1,0:T(8,128)(2,1)S(1)} collective-permute-done((bf16[2,64,1024]{2,1,0:T(8,128)(2,1)S(1)}, bf16[2,64,1024]{2,1,0:T(8,128)(2,1)S(1)}, u32[]{:S(2)}, u32[]{:S(2)}) %collective-permute-start.2) | collective-permute-done | bytes 262176 | tf_op jit(solution)/shard_map/ppermute | solution.py:239
  58.9 1.6 collective-permute-done.3
  60.5 0.1 pad_maximum_fusion.1
  60.6 3.8 %collective-permute-start.4 = (bf16[4,2,64,1024]{3,2,1,0:T(8,128)(2,1)S(1)}, bf16[4,2,64,1024]{3,2,1,0:T(8,128)(2,1)S(1)}, u32[]{:S(2)}, u32[]{:S(2)}) collective-permute-start(bf16[4,2,64,1024]{3,2,1,0:T(8,128)(2,1)S(1)} %pad_maximum_fusion.1), channel_id=1, source_target_pairs={{0,1},{1,0},{2,3},{3,2},{4,5},{5,4},{6,7},{7,6},{8,9},{9,8},{10,11... | collective-permute-start | bytes 3145736 | tf_op jit(solution)/shard_map/ppermute | solution.py:241
  64.4 0.0 copy-done.1
  64.4 0.1 reshape.18
  64.5 0.1 constant_dynamic-slice_fusion
  64.6 0.1 copy.11
  64.7 0.1 reshape.19
  64.8 0.0 copy-done.2
  64.8 0.1 reshape.20
  64.9 0.2 dynamic-slice_reduce_fusion
  65.1 0.0 copy-done.4
  65.1 0.1 dynamic_slice.20
  65.2 0.1 concatenate.9.info_ref
  65.3 0.0 copy-start
  65.3 1.4 collective-permute-done.4
  66.7 0.2 pad_maximum_fusion.window_ref
  66.9 0.0 copy-done
  66.9 12.4 %lag_kernels.1.kernel_ref = bf16[4,4,1024,512]{3,2,1,0:T(8,128)(2,1)} custom-call(s32[1]{0:T(128)} %bitcast.1.core_ref, bf16[4,4,64,1024]{3,2,1,0:T(8,128)(2,1)S(1)} %pad_maximum_fusion.window_ref, f32[2,8,512]{2,1,0:T(8,128)S(1)} %copy-done), custom_call_target="tpu_custom_call" | custom-call | tf_op jit(solution)/shard_map/lag_kernels/pallas_call | solution.py:135
  79.3 56.6 %all-gather.2.cloned.1.call-done.refs_0_.refs_1_.refs_2_.refs_3_.refs_4_.refs_5_.refs_6_.refs_7_ = bf16[16,4,4,16,1024]{4,3,2,1,0:T(8,128)(2,1)} async-done(((bf16[1,4,4,16,1024]{4,3,2,1,0:T(8,128)(2,1)}), bf16[16,4,4,16,1024]{4,3,2,1,0:T(8,128)(2,1)}) %all-gather.2.cloned.1.call-update) | async-done | bytes 8388624 | tf_op jit(solution)/shard_map/all_gather | solution.py:230
  135.9 10.5 %correlate.1 = bf16[4,8,128,128]{3,2,1,0:T(8,128)(2,1)S(1)} custom-call(s32[73]{0:T(128)S(1)} %concatenate.9.info_ref, bf16[4,4,1024,512]{3,2,1,0:T(8,128)(2,1)} %lag_kernels.1.kernel_ref, bf16[16,4,4,16,1024]{4,3,2,1,0:T(8,128)(2,1)} %all-gather.2.cloned.1.call-done.refs_0_.refs_1_.refs_2_.refs_3_.refs_4_.refs_5_.refs_6_.refs_7_, ...), custom_call_target="tpu_custom_call" | custom-call | tf_op jit(solution)/shard_map/correlate/pallas_call | solution.py:180
  146.4 24.5 %all_to_all.11.parts_ref = bf16[32,128,128]{2,1,0:T(8,128)(2,1)S(1)} all-to-all(bf16[32,128,128]{2,1,0:T(8,128)(2,1)S(1)} %bitcast.14), channel_id=1, replica_groups=mesh['y'=4,'z'=16,'x'=4,'c'=2] {'y','x','c'}, dimensions={0} | all-to-all | bytes 2097152 | tf_op jit(solution)/shard_map/all_to_all | solution.py:250
  170.8 0.9 finish.1
  (1 shorter events, 0.0 us)
Async XLA Ops:
  6.5 26.7 %copy-start.3 = (s32[64]{0:T(128)S(1)}, s32[64]{0:T(128)}, u32[]{:S(2)}) copy-start(s32[64]{0:T(128)} %param.10) | copy-start | bytes 772
  6.5 129.3 %all-gather.2.cloned.1.call-start = ((), (), s32[]{:S(2)}) async-start(), calls=%async_computation.2 | async-start | bytes 8912896 | tf_op jit(solution)/shard_map/all_gather | solution.py:230
  11.3 53.1 %copy-start.1 = (s32[64,8]{0,1:T(8,128)S(1)}, s32[64,8]{0,1:T(8,128)}, u32[]{:S(2)}) copy-start(s32[64,8]{0,1:T(8,128)} %param.8) | copy-start | bytes 6148
  11.3 53.5 %copy-start.2 = (s32[64]{0:T(128)S(1)}, s32[64]{0:T(128)}, u32[]{:S(2)}) copy-start(s32[64]{0:T(128)} %param.9) | copy-start | bytes 772
  11.3 53.7 %copy-start.4 = (s32[16]{0:T(128)S(1)}, s32[16]{0:T(128)}, u32[]{:S(2)}) copy-start(s32[16]{0:T(128)} %param.11) | copy-start | bytes 196
  31.9 8.9 %collective-permute-start = (bf16[2,64,1024]{2,1,0:T(8,128)(2,1)}, bf16[2,64,1024]{2,1,0:T(8,128)(2,1)S(1)}, u32[]{:S(2)}, u32[]{:S(2)}) collective-permute-start(bf16[2,64,1024]{2,1,0:T(8,128)(2,1)} %get-tuple-element.13), channel_id=1, source_target_pairs={{8,0},{16,8},{24,16},{32,24},{40,32},{48,40},{56,48},{64,56},{72,6... | collective-permute-start | bytes 786440 | tf_op jit(solution)/shard_map/ppermute | solution.py:234
  41.9 11.8 %collective-permute-start.1 = (bf16[2,64,1024]{2,1,0:T(8,128)(2,1)S(1)}, bf16[2,64,1024]{2,1,0:T(8,128)(2,1)S(1)}, u32[]{:S(2)}, u32[]{:S(2)}) collective-permute-start(bf16[2,64,1024]{2,1,0:T(8,128)(2,1)S(1)} %fusion), channel_id=1, source_target_pairs={{0,128},{128,256},{256,384},{384,0},{1,129},{129,257},{257,385},{3... | collective-permute-start | bytes 786440 | tf_op jit(solution)/shard_map/ppermute | solution.py:239
  47.1 11.8 %collective-permute-start.2 = (bf16[2,64,1024]{2,1,0:T(8,128)(2,1)S(1)}, bf16[2,64,1024]{2,1,0:T(8,128)(2,1)S(1)}, u32[]{:S(2)}, u32[]{:S(2)}) collective-permute-start(bf16[2,64,1024]{2,1,0:T(8,128)(2,1)S(1)} %fusion), channel_id=1, source_target_pairs={{0,256},{128,384},{256,0},{384,128},{1,257},{129,385},{257,1},{385... | collective-permute-start | bytes 786440 | tf_op jit(solution)/shard_map/ppermute | solution.py:239
  50.1 10.4 %collective-permute-start.3 = (bf16[2,64,1024]{2,1,0:T(8,128)(2,1)S(1)}, bf16[2,64,1024]{2,1,0:T(8,128)(2,1)S(1)}, u32[]{:S(2)}, u32[]{:S(2)}) collective-permute-start(bf16[2,64,1024]{2,1,0:T(8,128)(2,1)S(1)} %fusion), channel_id=1, source_target_pairs={{0,384},{128,0},{256,128},{384,256},{1,385},{129,1},{257,129},{385... | collective-permute-start | bytes 786440 | tf_op jit(solution)/shard_map/ppermute | solution.py:239
  60.6 6.1 %collective-permute-start.4 = (bf16[4,2,64,1024]{3,2,1,0:T(8,128)(2,1)S(1)}, bf16[4,2,64,1024]{3,2,1,0:T(8,128)(2,1)S(1)}, u32[]{:S(2)}, u32[]{:S(2)}) collective-permute-start(bf16[4,2,64,1024]{3,2,1,0:T(8,128)(2,1)S(1)} %pad_maximum_fusion.1), channel_id=1, source_target_pairs={{0,1},{1,0},{2,3},{3,2},{4,5},{5,4},{6,7},{7,6},{8,9},{9,8},{10,11... | collective-permute-start | bytes 3145736 | tf_op jit(solution)/shard_map/ppermute | solution.py:241
  65.3 1.7 copy-start
Sparse Core Ops, SparseCore 0:
  32.0 103.8 all-gather.1

commit v8 on v7

--- a/solution.py
+++ b/solution.py
@@ -164,18 +164,18 @@
     live = (row < info_ref[I_COUNT + o] * CQ).astype(F32)
     totals = [0.0] * SLOTS
     for s in range(SEG_CHIP):
-        left = jnp.concatenate([ref[0, 0, s] for ref in sources], axis=0)
+        left = jnp.concatenate([ref[0, s // SEG, 0, s % SEG] for ref in sources], axis=0)
         part = jnp.dot(left, kernel_ref[0, s], preferred_element_type=F32)
         for q in range(SLOTS):
             totals[q] = totals[q] + part * (live * (info_ref[I_SLOT + s] == q).astype(F32))
     for l in range(LAGS):
         both = jnp.concatenate([v[:, l * R_CH : (l + 1) * R_CH] for v in totals], axis=1)
-        out_ref[0, l] = both.astype(BF)
+        out_ref[l // NC, 0, l % NC] = both.astype(BF)
 
 
 def correlate(info, kernels, gathered):
     def source_map(k):
-        return lambda o, info: (info[o * K + k], info[NY * K + o * K + k], 0, 0, 0)
+        return lambda o, info: (info[o * K + k], 0, info[NY * K + o * K + k], 0, 0, 0)
 
     return pl.pallas_call(
         correlate_body,
@@ -188,10 +188,10 @@
                     lambda o, info: (lax.rem(info[I_Y] + NY - o, NY), 0, 0, 0),
                 )
             ]
-            + [pl.BlockSpec((1, 1, SEG_CHIP, CQ, KF), source_map(k)) for k in range(K)],
-            out_specs=pl.BlockSpec((1, LAGS, K * CQ, SLOTS * R_CH), lambda o, info: (o, 0, 0, 0)),
+            + [pl.BlockSpec((1, NC, 1, SEG, CQ, KF), source_map(k)) for k in range(K)],
+            out_specs=pl.BlockSpec((NX, 1, NC, K * CQ, SLOTS * R_CH), lambda o, info: (0, o, 0, 0, 0)),
         ),
-        out_shape=jax.ShapeDtypeStruct((NY, LAGS, K * CQ, SLOTS * R_CH), BF),
+        out_shape=jax.ShapeDtypeStruct((NX, NY, NC, K * CQ, SLOTS * R_CH), BF),
         compiler_params=pltpu.CompilerParams(vmem_limit_bytes=VMEM),
         name="correlate",
     )(info, kernels, *([gathered] * K))
@@ -199,11 +199,11 @@
 
 def finish_body(parts_ref, out_ref):
     pieces = []
-    for y in range(NY):
-        for c in range(NC):
-            total = parts_ref[y * NX * NC + c].astype(F32)
+    for c in range(NC):
+        for y in range(NY):
+            total = parts_ref[y * NC + c].astype(F32)
             for x in range(1, NX):
-                total = total + parts_ref[(y * NX + x) * NC + c].astype(F32)
+                total = total + parts_ref[(x * NY + y) * NC + c].astype(F32)
             pieces.append(total)
     for k in range(K):
         rows = jnp.concatenate([v[k * CQ : (k + 1) * CQ] for v in pieces], axis=0).T.astype(BF)
@@ -226,7 +226,7 @@
     table = jnp.asarray(transform_table())
     lags = jnp.asarray(lag_tables())
     split, low, high = whiten(traces, table)
-    crossed = lax.all_to_all(split, ("y", "c"), 0, 0).reshape(NY, SEG_CHIP, CQ, KF)
+    crossed = lax.all_to_all(split, ("c", "y"), 0, 0).reshape(NC, NY, SEG, CQ, KF)
     gathered = lax.all_gather(crossed, "z", axis=0, tiled=False)
 
     low, high, _ = lax.optimization_barrier((low, high, crossed))
@@ -247,7 +247,7 @@
     slots = lax.dynamic_slice_in_dim(segment_slot, lax.axis_index("x") * SEG_CHIP, SEG_CHIP, 0)
     info = jnp.concatenate([lists % NZ, lists // NZ, counts, slots, y[None].astype(jnp.int32)])
     sums = correlate(info, kernels, gathered)
-    parts = lax.all_to_all(sums.reshape(NY * LAGS, K * CQ, SLOTS * R_CH), ("y", "x", "c"), 0, 0)
+    parts = lax.all_to_all(sums.reshape(NY * LAGS, K * CQ, SLOTS * R_CH), ("x", "y", "c"), 0, 0)
     return finish(parts)
 
 

time: 179 us -> 177 us (0.989)
  no operation moved by 1% of the time
where the time goes in v8:
time: 177 us
  waiting for transfers between devices  70.1 us (40%)
  blocking collectives  44.8 us (25%)
  Pallas kernels  27.2 us (15%)
  starting transfers between devices  17.3 us (10%)
  between operations  14.8 us (8%)
    all_gather x1, waiting for transfers between devices, body(): gathered = lax.all_gather(crossed, 'z', axis=0, tiled=False)  55.6 us
    all_to_all x1, blocking collectives, body(): lax.all_to_all(sums.reshape(NY * LAGS, K * CQ, SLOTS * R_CH), ('x', 'y',...  24.3 us
    all_to_all x1, blocking collectives, body(): lax.all_to_all(split, ('c', 'y'), 0, 0).reshape(NC, NY, SEG, CQ, KF)  20.5 us
    pallas_call x1, Pallas kernels, lag_kernels(): pl.pallas_call(lag_kernel_body, grid_spec=pltpu.PrefetchScalarGridSpec(nu...  12.4 us
    ppermute x3, starting transfers between devices, body(): lax.ppermute(window, 'y', [(i, (i + d) % NY) for i in range(NY)])  12.1 us
    pallas_call x1, Pallas kernels, correlate(): pl.pallas_call(correlate_body, grid_spec=pltpu.PrefetchScalarGridSpec(num...  9.14 us
    ppermute x3, waiting for transfers between devices, body(): lax.ppermute(window, 'y', [(i, (i + d) % NY) for i in range(NY)])  6.57 us
    ppermute x1, waiting for transfers between devices, body(): lax.ppermute(low, ('y', 'z'), [(p, p - 1) for p in range(1, pairs)])  6.42 us
  transfers between devices with their start and end apart: 6, of which 5 were waited for; matrix products, arithmetic and copies ran while one was open for 2% of the time, Pallas kernels for 7%

profile of v8, /device:TPU:1, one launch (start us, length us, event | category | flops | bytes accessed | tf_op | source)
XLA Modules:
  0.0 177.0 jit_solution(10654371970877700123)
XLA Ops:
  6.5 0.0 copy-start.3
  6.5 0.0 all-gather.2.cloned.1.call-start
  6.5 4.8 %whiten.1 = (bf16[8,2,16,1024]{3,2,1,0:T(8,128)(2,1)}, bf16[2,64,1024]{2,1,0:T(8,128)(2,1)}, bf16[2,64,1024]{2,1,0:T(8,128)(2,1)}) custom-call(bf16[2,2048,128]{2,1,0:T(8,128)(2,1)} %traces_hbm.1, bf16[2,512,1024]{2,1,0:T(8,128)(2,1)} %constant.72.clone.table_hbm), custom_call_target="tpu_custom_call" | custom-call | tf_op jit(solution)/shard_map/whiten/pallas_call | solution.py:96
  11.3 0.0 copy-start.1
  11.3 0.0 copy-start.2
  11.3 0.0 copy-start.4
  11.4 20.5 %all_to_all.10 = bf16[8,2,16,1024]{3,2,1,0:T(8,128)(2,1)} all-to-all(bf16[8,2,16,1024]{3,2,1,0:T(8,128)(2,1)} %get-tuple-element.14), channel_id=1, replica_groups=mesh['y'=4,'z'=16,'x'=4,'c'=2] {'c','y'}, dimensions={0} | all-to-all | bytes 1048576 | tf_op jit(solution)/shard_map/all_to_all | solution.py:229
  31.9 0.0 all-gather.2.cloned.1.call-update
  31.9 1.3 collective-permute-start
  33.2 0.0 copy-done.3
  33.2 0.6 dynamic_slice.21
  35.1 6.4 %collective-permute-done = bf16[2,64,1024]{2,1,0:T(8,128)(2,1)S(1)} collective-permute-done((bf16[2,64,1024]{2,1,0:T(8,128)(2,1)}, bf16[2,64,1024]{2,1,0:T(8,128)(2,1)S(1)}, u32[]{:S(2)}, u32[]{:S(2)}) %collective-permute-start) | collective-permute-done | bytes 262176 | tf_op jit(solution)/shard_map/ppermute | solution.py:234
  41.5 1.1 fusion
  42.6 5.3 %collective-permute-start.1 = (bf16[2,64,1024]{2,1,0:T(8,128)(2,1)S(1)}, bf16[2,64,1024]{2,1,0:T(8,128)(2,1)S(1)}, u32[]{:S(2)}, u32[]{:S(2)}) collective-permute-start(bf16[2,64,1024]{2,1,0:T(8,128)(2,1)S(1)} %fusion), channel_id=1, source_target_pairs={{0,128},{128,256},{256,384},{384,0},{1,129},{129,257},{257,385},{3... | collective-permute-start | bytes 786440 | tf_op jit(solution)/shard_map/ppermute | solution.py:239
  47.9 2.8 %collective-permute-start.2 = (bf16[2,64,1024]{2,1,0:T(8,128)(2,1)S(1)}, bf16[2,64,1024]{2,1,0:T(8,128)(2,1)S(1)}, u32[]{:S(2)}, u32[]{:S(2)}) collective-permute-start(bf16[2,64,1024]{2,1,0:T(8,128)(2,1)S(1)} %fusion), channel_id=1, source_target_pairs={{0,256},{128,384},{256,0},{384,128},{1,257},{129,385},{257,1},{385... | collective-permute-start | bytes 786440 | tf_op jit(solution)/shard_map/ppermute | solution.py:239
  50.7 4.0 %collective-permute-start.3 = (bf16[2,64,1024]{2,1,0:T(8,128)(2,1)S(1)}, bf16[2,64,1024]{2,1,0:T(8,128)(2,1)S(1)}, u32[]{:S(2)}, u32[]{:S(2)}) collective-permute-start(bf16[2,64,1024]{2,1,0:T(8,128)(2,1)S(1)} %fusion), channel_id=1, source_target_pairs={{0,384},{128,0},{256,128},{384,256},{1,385},{129,1},{257,129},{385... | collective-permute-start | bytes 786440 | tf_op jit(solution)/shard_map/ppermute | solution.py:239
  54.7 0.0 collective-permute-done.1
  54.7 5.1 %collective-permute-done.2 = bf16[2,64,1024]{2,1,0:T(8,128)(2,1)S(1)} collective-permute-done((bf16[2,64,1024]{2,1,0:T(8,128)(2,1)S(1)}, bf16[2,64,1024]{2,1,0:T(8,128)(2,1)S(1)}, u32[]{:S(2)}, u32[]{:S(2)}) %collective-permute-start.2) | collective-permute-done | bytes 262176 | tf_op jit(solution)/shard_map/ppermute | solution.py:239
  59.8 1.5 collective-permute-done.3
  61.3 0.1 pad_maximum_fusion.1
  61.4 3.9 %collective-permute-start.4 = (bf16[4,2,64,1024]{3,2,1,0:T(8,128)(2,1)S(1)}, bf16[4,2,64,1024]{3,2,1,0:T(8,128)(2,1)S(1)}, u32[]{:S(2)}, u32[]{:S(2)}) collective-permute-start(bf16[4,2,64,1024]{3,2,1,0:T(8,128)(2,1)S(1)} %pad_maximum_fusion.1), channel_id=1, source_target_pairs={{0,1},{1,0},{2,3},{3,2},{4,5},{5,4},{6,7},{7,6},{8,9},{9,8},{10,11... | collective-permute-start | bytes 3145736 | tf_op jit(solution)/shard_map/ppermute | solution.py:241
  65.3 0.0 copy-done.1
  65.3 0.1 reshape.18
  65.4 0.1 constant_dynamic-slice_fusion
  65.5 0.1 copy.11
  65.6 0.1 reshape.19
  65.7 0.0 copy-done.2
  65.7 0.1 reshape.20
  65.8 0.2 dynamic-slice_reduce_fusion
  66.0 0.0 copy-done.4
  66.0 0.1 dynamic_slice.20
  66.1 0.1 concatenate.9.info_ref
  66.2 0.0 copy-start
  66.2 1.4 collective-permute-done.4
  67.6 0.2 pad_maximum_fusion.window_ref
  67.8 0.0 copy-done
  67.8 12.4 %lag_kernels.1.kernel_ref = bf16[4,4,1024,512]{3,2,1,0:T(8,128)(2,1)} custom-call(s32[1]{0:T(128)} %bitcast.1.core_ref, bf16[4,4,64,1024]{3,2,1,0:T(8,128)(2,1)S(1)} %pad_maximum_fusion.window_ref, f32[2,8,512]{2,1,0:T(8,128)S(1)} %copy-done), custom_call_target="tpu_custom_call" | custom-call | tf_op jit(solution)/shard_map/lag_kernels/pallas_call | solution.py:135
  80.2 55.6 %all-gather.2.cloned.1.call-done.refs_0_.refs_1_.refs_2_.refs_3_.refs_4_.refs_5_.refs_6_.refs_7_ = bf16[16,2,4,2,16,1024]{5,4,3,2,1,0:T(8,128)(2,1)} async-done(((bf16[1,2,4,2,16,1024]{5,4,3,2,1,0:T(8,128)(2,1)}), bf16[16,2,4,2,16,1024]{5,4,3,2,1,0:T(8,128)(2,1)}) %all-gather.2.cloned.1.call-update) | async-done | bytes 8388624 | tf_op jit(solution)/shard_map/all_gather | solution.py:230
  135.8 9.1 %correlate.1 = bf16[4,4,2,128,128]{4,3,2,1,0:T(8,128)(2,1)S(1)} custom-call(s32[73]{0:T(128)S(1)} %concatenate.9.info_ref, bf16[4,4,1024,512]{3,2,1,0:T(8,128)(2,1)} %lag_kernels.1.kernel_ref, bf16[16,2,4,2,16,1024]{5,4,3,2,1,0:T(8,128)(2,1)} %all-gather.2.cloned.1.call-done.refs_0_.refs_1_.refs_2_.refs_3_.refs_4_.refs_5_.refs_6_.refs_7_, ...), custom_call_target="tpu_custom_call" | custom-call | tf_op jit(solution)/shard_map/correlate/pallas_call | solution.py:180
  145.0 24.3 %all_to_all.11.parts_ref = bf16[32,128,128]{2,1,0:T(8,128)(2,1)S(1)} all-to-all(bf16[32,128,128]{2,1,0:T(8,128)(2,1)S(1)} %bitcast.14), channel_id=1, replica_groups=mesh['y'=4,'z'=16,'x'=4,'c'=2] {'x','y','c'}, dimensions={0} | all-to-all | bytes 2097152 | tf_op jit(solution)/shard_map/all_to_all | solution.py:250
  169.2 0.9 finish.1
  (1 shorter events, 0.0 us)
Async XLA Ops:
  6.5 26.7 %copy-start.3 = (s32[64]{0:T(128)S(1)}, s32[64]{0:T(128)}, u32[]{:S(2)}) copy-start(s32[64]{0:T(128)} %param.10) | copy-start | bytes 772
  6.5 129.3 %all-gather.2.cloned.1.call-start = ((), (), s32[]{:S(2)}) async-start(), calls=%async_computation.2 | async-start | bytes 8912896 | tf_op jit(solution)/shard_map/all_gather | solution.py:230
  11.3 54.0 %copy-start.1 = (s32[64,8]{0,1:T(8,128)S(1)}, s32[64,8]{0,1:T(8,128)}, u32[]{:S(2)}) copy-start(s32[64,8]{0,1:T(8,128)} %param.8) | copy-start | bytes 6148
  11.3 54.4 %copy-start.2 = (s32[64]{0:T(128)S(1)}, s32[64]{0:T(128)}, u32[]{:S(2)}) copy-start(s32[64]{0:T(128)} %param.9) | copy-start | bytes 772
  11.3 54.6 %copy-start.4 = (s32[16]{0:T(128)S(1)}, s32[16]{0:T(128)}, u32[]{:S(2)}) copy-start(s32[16]{0:T(128)} %param.11) | copy-start | bytes 196
  31.9 9.6 %collective-permute-start = (bf16[2,64,1024]{2,1,0:T(8,128)(2,1)}, bf16[2,64,1024]{2,1,0:T(8,128)(2,1)S(1)}, u32[]{:S(2)}, u32[]{:S(2)}) collective-permute-start(bf16[2,64,1024]{2,1,0:T(8,128)(2,1)} %get-tuple-element.13), channel_id=1, source_target_pairs={{8,0},{16,8},{24,16},{32,24},{40,32},{48,40},{56,48},{64,56},{72,6... | collective-permute-start | bytes 786440 | tf_op jit(solution)/shard_map/ppermute | solution.py:234
  42.6 12.1 %collective-permute-start.1 = (bf16[2,64,1024]{2,1,0:T(8,128)(2,1)S(1)}, bf16[2,64,1024]{2,1,0:T(8,128)(2,1)S(1)}, u32[]{:S(2)}, u32[]{:S(2)}) collective-permute-start(bf16[2,64,1024]{2,1,0:T(8,128)(2,1)S(1)} %fusion), channel_id=1, source_target_pairs={{0,128},{128,256},{256,384},{384,0},{1,129},{129,257},{257,385},{3... | collective-permute-start | bytes 786440 | tf_op jit(solution)/shard_map/ppermute | solution.py:239
  47.9 11.9 %collective-permute-start.2 = (bf16[2,64,1024]{2,1,0:T(8,128)(2,1)S(1)}, bf16[2,64,1024]{2,1,0:T(8,128)(2,1)S(1)}, u32[]{:S(2)}, u32[]{:S(2)}) collective-permute-start(bf16[2,64,1024]{2,1,0:T(8,128)(2,1)S(1)} %fusion), channel_id=1, source_target_pairs={{0,256},{128,384},{256,0},{384,128},{1,257},{129,385},{257,1},{385... | collective-permute-start | bytes 786440 | tf_op jit(solution)/shard_map/ppermute | solution.py:239
  50.7 10.5 %collective-permute-start.3 = (bf16[2,64,1024]{2,1,0:T(8,128)(2,1)S(1)}, bf16[2,64,1024]{2,1,0:T(8,128)(2,1)S(1)}, u32[]{:S(2)}, u32[]{:S(2)}) collective-permute-start(bf16[2,64,1024]{2,1,0:T(8,128)(2,1)S(1)} %fusion), channel_id=1, source_target_pairs={{0,384},{128,0},{256,128},{384,256},{1,385},{129,1},{257,129},{385... | collective-permute-start | bytes 786440 | tf_op jit(solution)/shard_map/ppermute | solution.py:239
  61.4 6.2 %collective-permute-start.4 = (bf16[4,2,64,1024]{3,2,1,0:T(8,128)(2,1)S(1)}, bf16[4,2,64,1024]{3,2,1,0:T(8,128)(2,1)S(1)}, u32[]{:S(2)}, u32[]{:S(2)}) collective-permute-start(bf16[4,2,64,1024]{3,2,1,0:T(8,128)(2,1)S(1)} %pad_maximum_fusion.1), channel_id=1, source_target_pairs={{0,1},{1,0},{2,3},{3,2},{4,5},{5,4},{6,7},{7,6},{8,9},{9,8},{10,11... | collective-permute-start | bytes 3145736 | tf_op jit(solution)/shard_map/ppermute | solution.py:241
  66.2 1.7 copy-start
Sparse Core Ops, SparseCore 0:
  32.0 103.7 all-gather.1

commit v9 on v8

--- a/solution.py
+++ b/solution.py
@@ -19,6 +19,7 @@
 NY, NZ, NX, NC = 4, 16, 4, 2
 SEG = 2
 SEG_CHIP = SEG * NC
+EVEN = LAGS // NC
 PIECES = NY * NC
 CQ = CH // PIECES
 FB = 128
@@ -119,14 +120,14 @@
         at = b * 2 * FB
         real = window_ref[0, 0, :, at : at + FB].astype(F32)
         imag = window_ref[0, 0, :, at + FB : at + 2 * FB].astype(F32)
-        for l in range(0, LAGS, 2):
+        for a in range(0, EVEN, 2):
             reals, imags = [], []
-            for m in (l, l + 1):
+            for m in (NC * a, NC * a + NC):
                 cos = lag_ref[0, m : m + 1, b * FB : (b + 1) * FB]
                 sin = lag_ref[1, m : m + 1, b * FB : (b + 1) * FB]
                 reals.append((cos * real + sin * imag) * NORM)
                 imags.append((cos * imag - sin * real) * NORM)
-            lanes = slice(l * R_CH, (l + 2) * R_CH)
+            lanes = slice(a * R_CH, (a + 2) * R_CH)
             out_ref[0, 0, at : at + FB, lanes] = jnp.concatenate(reals, axis=0).T.astype(BF)
             out_ref[0, 0, at + FB : at + 2 * FB, lanes] = jnp.concatenate(imags, axis=0).T.astype(BF)
 
@@ -142,11 +143,11 @@
                 pl.BlockSpec((2, LAGS, NF), lambda o, s, core: (0, 0, 0)),
             ],
             out_specs=pl.BlockSpec(
-                (1, 1, KF, LAGS * R_CH),
+                (1, 1, KF, EVEN * R_CH),
                 lambda o, s, core: (o, lax.rem(s + SEG * core[0], SEG_CHIP), 0, 0),
             ),
         ),
-        out_shape=jax.ShapeDtypeStruct((NY, SEG_CHIP, KF, LAGS * R_CH), BF),
+        out_shape=jax.ShapeDtypeStruct((NY, SEG_CHIP, KF, EVEN * R_CH), BF),
         compiler_params=pltpu.CompilerParams(vmem_limit_bytes=VMEM),
         name="lag_kernels",
     )(core, windows, lags)
@@ -157,23 +158,39 @@
 I_Y = I_SLOT + SEG_CHIP
 
 
-def correlate_body(info_ref, kernel_ref, *refs):
+def turned(rows, lag_ref):
+    one = LAGS // 2 + 1
+    blocks = []
+    for b in range(NB):
+        at = b * 2 * FB
+        real = rows[:, at : at + FB].astype(F32)
+        imag = rows[:, at + FB : at + 2 * FB].astype(F32)
+        cos = lag_ref[0, one : one + 1, b * FB : (b + 1) * FB]
+        sin = lag_ref[1, one : one + 1, b * FB : (b + 1) * FB]
+        blocks.append((real * cos - imag * sin).astype(BF))
+        blocks.append((real * sin + imag * cos).astype(BF))
+    return jnp.concatenate(blocks, axis=1)
+
+
+def correlate_body(info_ref, kernel_ref, lag_ref, *refs):
     sources, out_ref = refs[:K], refs[K]
     o = pl.program_id(0)
-    row = lax.broadcasted_iota(jnp.int32, (K * CQ, 1), 0)
+    row = lax.broadcasted_iota(jnp.int32, (NC * K * CQ, 1), 0) % (K * CQ)
     live = (row < info_ref[I_COUNT + o] * CQ).astype(F32)
     totals = [0.0] * SLOTS
     for s in range(SEG_CHIP):
-        left = jnp.concatenate([ref[0, s // SEG, 0, s % SEG] for ref in sources], axis=0)
+        rows = jnp.concatenate([ref[0, s // SEG, 0, s % SEG] for ref in sources], axis=0)
+        left = jnp.concatenate([rows, turned(rows, lag_ref)], axis=0)
         part = jnp.dot(left, kernel_ref[0, s], preferred_element_type=F32)
         for q in range(SLOTS):
             totals[q] = totals[q] + part * (live * (info_ref[I_SLOT + s] == q).astype(F32))
-    for l in range(LAGS):
-        both = jnp.concatenate([v[:, l * R_CH : (l + 1) * R_CH] for v in totals], axis=1)
-        out_ref[l // NC, 0, l % NC] = both.astype(BF)
-
-
-def correlate(info, kernels, gathered):
+    for a in range(EVEN):
+        for b in range(NC):
+            block = [v[b * K * CQ : (b + 1) * K * CQ, a * R_CH : (a + 1) * R_CH] for v in totals]
+            out_ref[a, 0, b] = jnp.concatenate(block, axis=1).astype(BF)
+
+
+def correlate(info, kernels, lags, gathered):
     def source_map(k):
         return lambda o, info: (info[o * K + k], 0, info[NY * K + o * K + k], 0, 0, 0)
 
@@ -184,9 +201,10 @@
             grid=(NY,),
             in_specs=[
                 pl.BlockSpec(
-                    (1, SEG_CHIP, KF, LAGS * R_CH),
+                    (1, SEG_CHIP, KF, EVEN * R_CH),
                     lambda o, info: (lax.rem(info[I_Y] + NY - o, NY), 0, 0, 0),
-                )
+                ),
+                pl.BlockSpec((2, LAGS, NF), lambda o, info: (0, 0, 0)),
             ]
             + [pl.BlockSpec((1, NC, 1, SEG, CQ, KF), source_map(k)) for k in range(K)],
             out_specs=pl.BlockSpec((NX, 1, NC, K * CQ, SLOTS * R_CH), lambda o, info: (0, o, 0, 0, 0)),
@@ -194,7 +212,7 @@
         out_shape=jax.ShapeDtypeStruct((NX, NY, NC, K * CQ, SLOTS * R_CH), BF),
         compiler_params=pltpu.CompilerParams(vmem_limit_bytes=VMEM),
         name="correlate",
-    )(info, kernels, *([gathered] * K))
+    )(info, kernels, lags, *([gathered] * K))
 
 
 def finish_body(parts_ref, out_ref):
@@ -246,7 +264,7 @@
     counts = lax.dynamic_index_in_dim(source_count.reshape(NY, NZ), z, 1, keepdims=False)
     slots = lax.dynamic_slice_in_dim(segment_slot, lax.axis_index("x") * SEG_CHIP, SEG_CHIP, 0)
     info = jnp.concatenate([lists % NZ, lists // NZ, counts, slots, y[None].astype(jnp.int32)])
-    sums = correlate(info, kernels, gathered)
+    sums = correlate(info, kernels, lags, gathered)
     parts = lax.all_to_all(sums.reshape(NY * LAGS, K * CQ, SLOTS * R_CH), ("x", "y", "c"), 0, 0)
     return finish(parts)
 

time: 177 us -> 176 us (level)
  Pallas kernels: 27.2 us -> 22.2 us
  waiting for transfers between devices: 70.1 us -> 73.7 us
    all_gather x1, waiting for transfers between devices: 55.6 us -> 59 us  [body(): gathered = lax.all_gather(crossed, 'z', axis=0, tiled=False)]
    pallas_call x1, Pallas kernels: 12.4 us -> 8.98 us  [lag_kernels(): pl.pallas_call(lag_kernel_body, grid_spec=pltpu.PrefetchScalarGridSpec(nu...]
  transfers between devices with their start and end apart: 6 -> 6, of which waited for: 5 -> 5; matrix products, arithmetic and copies ran while one was open for 2% -> 2% of each run, Pallas kernels for 7% -> 5%
where the time goes in v9:
time: 176 us; the launch traced here: 175 us
  waiting for transfers between devices  73.7 us (42%)
  blocking collectives  44.8 us (25%)
  Pallas kernels  22.2 us (13%)
  starting transfers between devices  17.2 us (10%)
  between operations  14.7 us (8%)
    all_gather x1, waiting for transfers between devices, body(): gathered = lax.all_gather(crossed, 'z', axis=0, tiled=False)  59 us
    all_to_all x1, blocking collectives, body(): lax.all_to_all(sums.reshape(NY * LAGS, K * CQ, SLOTS * R_CH), ('x', 'y',...  24.3 us
    all_to_all x1, blocking collectives, body(): lax.all_to_all(split, ('c', 'y'), 0, 0).reshape(NC, NY, SEG, CQ, KF)  20.5 us
    ppermute x3, starting transfers between devices, body(): lax.ppermute(window, 'y', [(i, (i + d) % NY) for i in range(NY)])  12 us
    pallas_call x1, Pallas kernels, lag_kernels(): pl.pallas_call(lag_kernel_body, grid_spec=pltpu.PrefetchScalarGridSpec(nu...  8.98 us
    pallas_call x1, Pallas kernels, correlate(): pl.pallas_call(correlate_body, grid_spec=pltpu.PrefetchScalarGridSpec(num...  7.47 us
    ppermute x1, waiting for transfers between devices, body(): lax.ppermute(low, ('y', 'z'), [(p, p - 1) for p in range(1, pairs)])  6.65 us
    ppermute x3, waiting for transfers between devices, body(): lax.ppermute(window, 'y', [(i, (i + d) % NY) for i in range(NY)])  6.57 us
  transfers between devices with their start and end apart: 6, of which 5 were waited for; matrix products, arithmetic and copies ran while one was open for 2% of the time, Pallas kernels for 5%

profile of v9, /device:TPU:1, one launch (start us, length us, event | category | flops | bytes accessed | tf_op | source)
XLA Modules:
  0.0 175.3 jit_solution(10112392678784338930)
XLA Ops:
  6.5 0.0 copy-start.3
  6.5 0.0 all-gather.2.cloned.1.call-start
  6.5 4.8 %whiten.1 = (bf16[8,2,16,1024]{3,2,1,0:T(8,128)(2,1)}, bf16[2,64,1024]{2,1,0:T(8,128)(2,1)}, bf16[2,64,1024]{2,1,0:T(8,128)(2,1)}) custom-call(bf16[2,2048,128]{2,1,0:T(8,128)(2,1)} %traces_hbm.1, bf16[2,512,1024]{2,1,0:T(8,128)(2,1)} %constant.72.clone.table_hbm), custom_call_target="tpu_custom_call" | custom-call | tf_op jit(solution)/shard_map/whiten/pallas_call | solution.py:97
  11.4 0.0 copy-start.1
  11.4 0.0 copy-start.2
  11.4 0.0 copy-start.4
  11.4 20.5 %all_to_all.10 = bf16[8,2,16,1024]{3,2,1,0:T(8,128)(2,1)} all-to-all(bf16[8,2,16,1024]{3,2,1,0:T(8,128)(2,1)} %get-tuple-element.14), channel_id=1, replica_groups=mesh['y'=4,'z'=16,'x'=4,'c'=2] {'c','y'}, dimensions={0} | all-to-all | bytes 1048576 | tf_op jit(solution)/shard_map/all_to_all | solution.py:247
  31.9 0.0 all-gather.2.cloned.1.call-update
  31.9 1.3 collective-permute-start
  33.2 0.0 copy-done.3
  33.2 0.6 dynamic_slice.21
  34.9 6.6 %collective-permute-done = bf16[2,64,1024]{2,1,0:T(8,128)(2,1)S(1)} collective-permute-done((bf16[2,64,1024]{2,1,0:T(8,128)(2,1)}, bf16[2,64,1024]{2,1,0:T(8,128)(2,1)S(1)}, u32[]{:S(2)}, u32[]{:S(2)}) %collective-permute-start) | collective-permute-done | bytes 262176 | tf_op jit(solution)/shard_map/ppermute | solution.py:252
  41.6 1.1 fusion
  42.7 5.1 %collective-permute-start.1 = (bf16[2,64,1024]{2,1,0:T(8,128)(2,1)S(1)}, bf16[2,64,1024]{2,1,0:T(8,128)(2,1)S(1)}, u32[]{:S(2)}, u32[]{:S(2)}) collective-permute-start(bf16[2,64,1024]{2,1,0:T(8,128)(2,1)S(1)} %fusion), channel_id=1, source_target_pairs={{0,128},{128,256},{256,384},{384,0},{1,129},{129,257},{257,385},{3... | collective-permute-start | bytes 786440 | tf_op jit(solution)/shard_map/ppermute | solution.py:257
  47.8 2.9 %collective-permute-start.2 = (bf16[2,64,1024]{2,1,0:T(8,128)(2,1)S(1)}, bf16[2,64,1024]{2,1,0:T(8,128)(2,1)S(1)}, u32[]{:S(2)}, u32[]{:S(2)}) collective-permute-start(bf16[2,64,1024]{2,1,0:T(8,128)(2,1)S(1)} %fusion), channel_id=1, source_target_pairs={{0,256},{128,384},{256,0},{384,128},{1,257},{129,385},{257,1},{385... | collective-permute-start | bytes 786440 | tf_op jit(solution)/shard_map/ppermute | solution.py:257
  50.7 4.0 %collective-permute-start.3 = (bf16[2,64,1024]{2,1,0:T(8,128)(2,1)S(1)}, bf16[2,64,1024]{2,1,0:T(8,128)(2,1)S(1)}, u32[]{:S(2)}, u32[]{:S(2)}) collective-permute-start(bf16[2,64,1024]{2,1,0:T(8,128)(2,1)S(1)} %fusion), channel_id=1, source_target_pairs={{0,384},{128,0},{256,128},{384,256},{1,385},{129,1},{257,129},{385... | collective-permute-start | bytes 786440 | tf_op jit(solution)/shard_map/ppermute | solution.py:257
  54.7 0.0 collective-permute-done.1
  54.7 5.2 %collective-permute-done.2 = bf16[2,64,1024]{2,1,0:T(8,128)(2,1)S(1)} collective-permute-done((bf16[2,64,1024]{2,1,0:T(8,128)(2,1)S(1)}, bf16[2,64,1024]{2,1,0:T(8,128)(2,1)S(1)}, u32[]{:S(2)}, u32[]{:S(2)}) %collective-permute-start.2) | collective-permute-done | bytes 262176 | tf_op jit(solution)/shard_map/ppermute | solution.py:257
  59.9 1.4 collective-permute-done.3
  61.3 0.1 pad_maximum_fusion.1
  61.4 3.9 %collective-permute-start.4 = (bf16[4,2,64,1024]{3,2,1,0:T(8,128)(2,1)S(1)}, bf16[4,2,64,1024]{3,2,1,0:T(8,128)(2,1)S(1)}, u32[]{:S(2)}, u32[]{:S(2)}) collective-permute-start(bf16[4,2,64,1024]{3,2,1,0:T(8,128)(2,1)S(1)} %pad_maximum_fusion.1), channel_id=1, source_target_pairs={{0,1},{1,0},{2,3},{3,2},{4,5},{5,4},{6,7},{7,6},{8,9},{9,8},{10,11... | collective-permute-start | bytes 3145736 | tf_op jit(solution)/shard_map/ppermute | solution.py:259
  65.3 0.0 copy-done.1
  65.3 0.1 reshape.18
  65.4 0.1 constant_dynamic-slice_fusion
  65.5 0.1 copy.11
  65.6 0.1 reshape.19
  65.7 0.0 copy-done.2
  65.7 0.1 reshape.20
  65.8 0.2 dynamic-slice_reduce_fusion
  65.9 0.0 copy-done.4
  66.0 0.1 dynamic_slice.20
  66.1 0.1 concatenate.9.info_ref
  66.1 0.0 copy-start
  66.1 1.4 collective-permute-done.4
  67.6 0.2 pad_maximum_fusion.window_ref
  67.8 0.0 copy-done
  67.8 9.0 %lag_kernels.1.kernel_ref = bf16[4,4,1024,256]{3,2,1,0:T(8,128)(2,1)} custom-call(s32[1]{0:T(128)} %bitcast.1.core_ref, bf16[4,4,64,1024]{3,2,1,0:T(8,128)(2,1)S(1)} %pad_maximum_fusion.window_ref, f32[2,8,512]{2,1,0:T(8,128)S(1)} %copy-done), custom_call_target="tpu_custom_call" | custom-call | tf_op jit(solution)/shard_map/lag_kernels/pallas_call | solution.py:136
  76.8 59.0 %all-gather.2.cloned.1.call-done.refs_0_.refs_1_.refs_2_.refs_3_.refs_4_.refs_5_.refs_6_.refs_7_ = bf16[16,2,4,2,16,1024]{5,4,3,2,1,0:T(8,128)(2,1)} async-done(((bf16[1,2,4,2,16,1024]{5,4,3,2,1,0:T(8,128)(2,1)}), bf16[16,2,4,2,16,1024]{5,4,3,2,1,0:T(8,128)(2,1)}) %all-gather.2.cloned.1.call-update) | async-done | bytes 8388624 | tf_op jit(solution)/shard_map/all_gather | solution.py:248
  135.9 7.5 %correlate.1 = bf16[4,4,2,128,128]{4,3,2,1,0:T(8,128)(2,1)S(1)} custom-call(s32[73]{0:T(128)S(1)} %concatenate.9.info_ref, bf16[4,4,1024,256]{3,2,1,0:T(8,128)(2,1)} %lag_kernels.1.kernel_ref, f32[2,8,512]{2,1,0:T(8,128)S(1)} %copy-done, ...), custom_call_target="tpu_custom_call" | custom-call | tf_op jit(solution)/shard_map/correlate/pallas_call | solution.py:197
  143.3 24.3 %all_to_all.11.parts_ref = bf16[32,128,128]{2,1,0:T(8,128)(2,1)S(1)} all-to-all(bf16[32,128,128]{2,1,0:T(8,128)(2,1)S(1)} %bitcast.14), channel_id=1, replica_groups=mesh['y'=4,'z'=16,'x'=4,'c'=2] {'x','y','c'}, dimensions={0} | all-to-all | bytes 2097152 | tf_op jit(solution)/shard_map/all_to_all | solution.py:268
  167.6 0.9 finish.1
  (1 shorter events, 0.0 us)
Async XLA Ops:
  6.5 26.7 %copy-start.3 = (s32[64]{0:T(128)S(1)}, s32[64]{0:T(128)}, u32[]{:S(2)}) copy-start(s32[64]{0:T(128)} %param.10) | copy-start | bytes 772
  6.5 129.3 %all-gather.2.cloned.1.call-start = ((), (), s32[]{:S(2)}) async-start(), calls=%async_computation.2 | async-start | bytes 8912896 | tf_op jit(solution)/shard_map/all_gather | solution.py:248
  11.4 54.0 %copy-start.1 = (s32[64,8]{0,1:T(8,128)S(1)}, s32[64,8]{0,1:T(8,128)}, u32[]{:S(2)}) copy-start(s32[64,8]{0,1:T(8,128)} %param.8) | copy-start | bytes 6148
  11.4 54.3 %copy-start.2 = (s32[64]{0:T(128)S(1)}, s32[64]{0:T(128)}, u32[]{:S(2)}) copy-start(s32[64]{0:T(128)} %param.9) | copy-start | bytes 772
  11.4 54.6 %copy-start.4 = (s32[16]{0:T(128)S(1)}, s32[16]{0:T(128)}, u32[]{:S(2)}) copy-start(s32[16]{0:T(128)} %param.11) | copy-start | bytes 196
  31.9 9.6 %collective-permute-start = (bf16[2,64,1024]{2,1,0:T(8,128)(2,1)}, bf16[2,64,1024]{2,1,0:T(8,128)(2,1)S(1)}, u32[]{:S(2)}, u32[]{:S(2)}) collective-permute-start(bf16[2,64,1024]{2,1,0:T(8,128)(2,1)} %get-tuple-element.13), channel_id=1, source_target_pairs={{8,0},{16,8},{24,16},{32,24},{40,32},{48,40},{56,48},{64,56},{72,6... | collective-permute-start | bytes 786440 | tf_op jit(solution)/shard_map/ppermute | solution.py:252
  42.7 12.0 %collective-permute-start.1 = (bf16[2,64,1024]{2,1,0:T(8,128)(2,1)S(1)}, bf16[2,64,1024]{2,1,0:T(8,128)(2,1)S(1)}, u32[]{:S(2)}, u32[]{:S(2)}) collective-permute-start(bf16[2,64,1024]{2,1,0:T(8,128)(2,1)S(1)} %fusion), channel_id=1, source_target_pairs={{0,128},{128,256},{256,384},{384,0},{1,129},{129,257},{257,385},{3... | collective-permute-start | bytes 786440 | tf_op jit(solution)/shard_map/ppermute | solution.py:257
  47.8 12.1 %collective-permute-start.2 = (bf16[2,64,1024]{2,1,0:T(8,128)(2,1)S(1)}, bf16[2,64,1024]{2,1,0:T(8,128)(2,1)S(1)}, u32[]{:S(2)}, u32[]{:S(2)}) collective-permute-start(bf16[2,64,1024]{2,1,0:T(8,128)(2,1)S(1)} %fusion), channel_id=1, source_target_pairs={{0,256},{128,384},{256,0},{384,128},{1,257},{129,385},{257,1},{385... | collective-permute-start | bytes 786440 | tf_op jit(solution)/shard_map/ppermute | solution.py:257
  50.7 10.5 %collective-permute-start.3 = (bf16[2,64,1024]{2,1,0:T(8,128)(2,1)S(1)}, bf16[2,64,1024]{2,1,0:T(8,128)(2,1)S(1)}, u32[]{:S(2)}, u32[]{:S(2)}) collective-permute-start(bf16[2,64,1024]{2,1,0:T(8,128)(2,1)S(1)} %fusion), channel_id=1, source_target_pairs={{0,384},{128,0},{256,128},{384,256},{1,385},{129,1},{257,129},{385... | collective-permute-start | bytes 786440 | tf_op jit(solution)/shard_map/ppermute | solution.py:257
  61.4 6.2 %collective-permute-start.4 = (bf16[4,2,64,1024]{3,2,1,0:T(8,128)(2,1)S(1)}, bf16[4,2,64,1024]{3,2,1,0:T(8,128)(2,1)S(1)}, u32[]{:S(2)}, u32[]{:S(2)}) collective-permute-start(bf16[4,2,64,1024]{3,2,1,0:T(8,128)(2,1)S(1)} %pad_maximum_fusion.1), channel_id=1, source_target_pairs={{0,1},{1,0},{2,3},{3,2},{4,5},{5,4},{6,7},{7,6},{8,9},{9,8},{10,11... | collective-permute-start | bytes 3145736 | tf_op jit(solution)/shard_map/ppermute | solution.py:259
  66.1 1.7 copy-start
Sparse Core Ops, SparseCore 0:
  32.0 103.7 all-gather.1

commit v10 on v9

--- a/solution.py
+++ b/solution.py
@@ -17,10 +17,12 @@
 F0 = 64
 SEGS = 16
 NY, NZ, NX, NC = 4, 16, 4, 2
+NP = 2
+NO = NX // NP
 SEG = 2
-SEG_CHIP = SEG * NC
+SEG_PAIR = SEG * NC * NP
 EVEN = LAGS // NC
-PIECES = NY * NC
+PIECES = NY * NC * NP
 CQ = CH // PIECES
 FB = 128
 NB = NF // FB
@@ -83,12 +85,12 @@
     power = jnp.sum(grouped * grouped, axis=(0, 2)) * (1.0 / (2 * BAND))
     scale = 1.0 / jnp.sqrt(power + EPS)
     whitened = grouped * scale[None, :, None, :]
-    flipped = whitened.reshape(2 * FB, SEG * CH).T.astype(BF)
+    flipped = whitened.reshape(2 * FB, SEG * CH).T
     for s in range(SEG):
-        low_ref[s] = flipped[s * CH : s * CH + CH // 2]
-        high_ref[s] = flipped[s * CH + CH // 2 : (s + 1) * CH]
+        low_ref[s] = flipped[s * CH : s * CH + CH // 2].astype(BF)
+        high_ref[s] = flipped[s * CH + CH // 2 : (s + 1) * CH].astype(BF)
         for r in range(PIECES):
-            split_ref[r, s] = flipped[s * CH + r * CQ : s * CH + (r + 1) * CQ]
+            split_ref[r, s] = flipped[s * CH + r * CQ : s * CH + (r + 1) * CQ].astype(BF)
 
 
 def whiten(traces, table):
@@ -132,22 +134,28 @@
             out_ref[0, 0, at + FB : at + 2 * FB, lanes] = jnp.concatenate(imags, axis=0).T.astype(BF)
 
 
+def segment_place(s, core):
+    half = SEG * NC
+    chip = lax.rem(s // half + core[1], NP)
+    return chip * half + lax.rem(lax.rem(s, half) + SEG * core[0], half)
+
+
 def lag_kernels(core, windows, lags):
     return pl.pallas_call(
         lag_kernel_body,
         grid_spec=pltpu.PrefetchScalarGridSpec(
             num_scalar_prefetch=1,
-            grid=(NY, SEG_CHIP),
+            grid=(NY, SEG_PAIR),
             in_specs=[
                 pl.BlockSpec((1, 1, R_CH, KF), lambda o, s, core: (o, s, 0, 0)),
                 pl.BlockSpec((2, LAGS, NF), lambda o, s, core: (0, 0, 0)),
             ],
             out_specs=pl.BlockSpec(
                 (1, 1, KF, EVEN * R_CH),
-                lambda o, s, core: (o, lax.rem(s + SEG * core[0], SEG_CHIP), 0, 0),
+                lambda o, s, core: (o, segment_place(s, core), 0, 0),
             ),
         ),
-        out_shape=jax.ShapeDtypeStruct((NY, SEG_CHIP, KF, EVEN * R_CH), BF),
+        out_shape=jax.ShapeDtypeStruct((NY, SEG_PAIR, KF, EVEN * R_CH), BF),
         compiler_params=pltpu.CompilerParams(vmem_limit_bytes=VMEM),
         name="lag_kernels",
     )(core, windows, lags)
@@ -155,7 +163,7 @@
 
 I_COUNT = 2 * NY * K
 I_SLOT = I_COUNT + NY
-I_Y = I_SLOT + SEG_CHIP
+I_Y = I_SLOT + SEG_PAIR
 
 
 def turned(rows, lag_ref):
@@ -178,8 +186,9 @@
     row = lax.broadcasted_iota(jnp.int32, (NC * K * CQ, 1), 0) % (K * CQ)
     live = (row < info_ref[I_COUNT + o] * CQ).astype(F32)
     totals = [0.0] * SLOTS
-    for s in range(SEG_CHIP):
-        rows = jnp.concatenate([ref[0, s // SEG, 0, s % SEG] for ref in sources], axis=0)
+    for s in range(SEG_PAIR):
+        at = (0, s // (SEG * NC), s // SEG % NC, 0, s % SEG)
+        rows = jnp.concatenate([ref[at].astype(F32) for ref in sources], axis=0).astype(BF)
         left = jnp.concatenate([rows, turned(rows, lag_ref)], axis=0)
         part = jnp.dot(left, kernel_ref[0, s], preferred_element_type=F32)
         for q in range(SLOTS):
@@ -192,7 +201,7 @@
 
 def correlate(info, kernels, lags, gathered):
     def source_map(k):
-        return lambda o, info: (info[o * K + k], 0, info[NY * K + o * K + k], 0, 0, 0)
+        return lambda o, info: (info[o * K + k], 0, 0, info[NY * K + o * K + k], 0, 0, 0)
 
     return pl.pallas_call(
         correlate_body,
@@ -201,12 +210,12 @@
             grid=(NY,),
             in_specs=[
                 pl.BlockSpec(
-                    (1, SEG_CHIP, KF, EVEN * R_CH),
+                    (1, SEG_PAIR, KF, EVEN * R_CH),
                     lambda o, info: (lax.rem(info[I_Y] + NY - o, NY), 0, 0, 0),
                 ),
                 pl.BlockSpec((2, LAGS, NF), lambda o, info: (0, 0, 0)),
             ]
-            + [pl.BlockSpec((1, NC, 1, SEG, CQ, KF), source_map(k)) for k in range(K)],
+            + [pl.BlockSpec((1, NP, NC, 1, SEG, CQ, KF), source_map(k)) for k in range(K)],
             out_specs=pl.BlockSpec((NX, 1, NC, K * CQ, SLOTS * R_CH), lambda o, info: (0, o, 0, 0, 0)),
         ),
         out_shape=jax.ShapeDtypeStruct((NX, NY, NC, K * CQ, SLOTS * R_CH), BF),
@@ -217,12 +226,13 @@
 
 def finish_body(parts_ref, out_ref):
     pieces = []
-    for c in range(NC):
-        for y in range(NY):
-            total = parts_ref[y * NC + c].astype(F32)
-            for x in range(1, NX):
-                total = total + parts_ref[(x * NY + y) * NC + c].astype(F32)
-            pieces.append(total)
+    for p in range(NP):
+        for c in range(NC):
+            for y in range(NY):
+                total = parts_ref[(p * NY + y) * NC + c].astype(F32)
+                for x in range(1, NO):
+                    total = total + parts_ref[((x * NP + p) * NY + y) * NC + c].astype(F32)
+                pieces.append(total)
     for k in range(K):
         rows = jnp.concatenate([v[k * CQ : (k + 1) * CQ] for v in pieces], axis=0).T.astype(BF)
         for q in range(SLOTS):
@@ -244,7 +254,7 @@
     table = jnp.asarray(transform_table())
     lags = jnp.asarray(lag_tables())
     split, low, high = whiten(traces, table)
-    crossed = lax.all_to_all(split, ("c", "y"), 0, 0).reshape(NC, NY, SEG, CQ, KF)
+    crossed = lax.all_to_all(split, ("xl", "c", "y"), 0, 0).reshape(NP, NC, NY, SEG, CQ, KF)
     gathered = lax.all_gather(crossed, "z", axis=0, tiled=False)
 
     low, high, _ = lax.optimization_barrier((low, high, crossed))
@@ -257,21 +267,23 @@
         [window] + [lax.ppermute(window, "y", [(i, (i + d) % NY) for i in range(NY)]) for d in range(1, NY)]
     )
     other = lax.ppermute(own, "c", [(0, 1), (1, 0)])
-    core = lax.axis_index("c")[None].astype(jnp.int32)
-    kernels = lag_kernels(core, jnp.concatenate([own, other], axis=1), lags)
+    chip = jnp.concatenate([own, other], axis=1)
+    beside = lax.ppermute(chip, "xl", [(0, 1), (1, 0)])
+    core = jnp.stack([lax.axis_index("c"), lax.axis_index("xl")]).astype(jnp.int32)
+    kernels = lag_kernels(core, jnp.concatenate([chip, beside], axis=1), lags)
 
     lists = lax.dynamic_index_in_dim(source_list.reshape(NY, NZ, K), z, 1, keepdims=False).reshape(-1)
     counts = lax.dynamic_index_in_dim(source_count.reshape(NY, NZ), z, 1, keepdims=False)
-    slots = lax.dynamic_slice_in_dim(segment_slot, lax.axis_index("x") * SEG_CHIP, SEG_CHIP, 0)
+    slots = lax.dynamic_slice_in_dim(segment_slot, lax.axis_index("xh") * SEG_PAIR, SEG_PAIR, 0)
     info = jnp.concatenate([lists % NZ, lists // NZ, counts, slots, y[None].astype(jnp.int32)])
     sums = correlate(info, kernels, lags, gathered)
-    parts = lax.all_to_all(sums.reshape(NY * LAGS, K * CQ, SLOTS * R_CH), ("x", "y", "c"), 0, 0)
+    parts = lax.all_to_all(sums.reshape(NY * LAGS, K * CQ, SLOTS * R_CH), ("xh", "xl", "y", "c"), 0, 0)
     return finish(parts)
 
 
 def solution(mesh):
-    grid = Mesh(mesh.devices.reshape(NY, NZ, NX, NC), ("y", "z", "x", "c"))
-    tm, pair = ("x", "c"), ("y", "z")
+    grid = Mesh(mesh.devices.reshape(NY, NZ, NO, NP, NC), ("y", "z", "xh", "xl", "c"))
+    tm, pair = ("xh", "xl", "c"), ("y", "z")
     return jax.shard_map(
         body,
         mesh=grid,

time: 176 us -> 177 us (level)
  Pallas kernels: 22.2 us -> 33 us
  waiting for transfers between devices: 73.7 us -> 63.4 us
  blocking collectives: 44.8 us -> 40.2 us
  other arithmetic: 1.5 us -> 4.67 us
    all_gather x1, waiting for transfers between devices: 59 us -> 0.01 us  [body(): gathered = lax.all_gather(crossed, 'z', axis=0, tiled=False)]
    ppermute x0 -> x1, waiting for transfers between devices: none -> 46.2 us  [body(): beside = lax.ppermute(chip, 'xl', [(0, 1), (1, 0)])]
    pallas_call x1, Pallas kernels: 8.98 us -> 18.2 us  [lag_kernels(): pl.pallas_call(lag_kernel_body, grid_spec=pltpu.PrefetchScalarGridSpec(nu...]
    all_to_all x2, blocking collectives: 44.8 us -> 40.2 us  [the longest x1 21.4 us: body(): lax.all_to_all(split, ('xl', 'c', 'y'), 0, 0)]
    concatenate x1 -> x2, other arithmetic: 0.24 us -> 3.38 us  [the longest x1 1.81 us: body(): kernels = lag_kernels(core, jnp.concatenate([chip, beside], axis=1), lags)]
    ppermute x3, waiting for transfers between devices: 6.57 us -> 8.67 us  [body(): lax.ppermute(window, 'y', [(i, (i + d) % NY) for i in range(NY)])]
    ppermute x0 -> x1, starting transfers between devices: none -> 1.91 us  [body(): beside = lax.ppermute(chip, 'xl', [(0, 1), (1, 0)])]
  transfers between devices with their start and end apart: 6 -> 7, of which waited for: 5 -> 6; matrix products, arithmetic and copies ran while one was open for 2% -> 3% of each run, Pallas kernels for 5% -> 10%
where the time goes in v10:
time: 177 us; the launch traced here: 176 us
  waiting for transfers between devices  63.4 us (36%)
  blocking collectives  40.2 us (23%)
  Pallas kernels  33 us (19%)
  starting transfers between devices  18.9 us (11%)
  between operations  14.8 us (8%)
  other arithmetic  4.67 us (3%)
    ppermute x1, waiting for transfers between devices, body(): beside = lax.ppermute(chip, 'xl', [(0, 1), (1, 0)])  46.2 us
    all_to_all x1, blocking collectives, body(): lax.all_to_all(split, ('xl', 'c', 'y'), 0, 0)  21.4 us
    all_to_all x1, blocking collectives, body(): lax.all_to_all(sums.reshape(NY * LAGS, K * CQ, SLOTS * R_CH), ('xh', 'xl'...  18.9 us
    pallas_call x1, Pallas kernels, lag_kernels(): pl.pallas_call(lag_kernel_body, grid_spec=pltpu.PrefetchScalarGridSpec(nu...  18.2 us
    ppermute x3, starting transfers between devices, body(): lax.ppermute(window, 'y', [(i, (i + d) % NY) for i in range(NY)])  12.4 us
    pallas_call x1, Pallas kernels, correlate(): pl.pallas_call(correlate_body, grid_spec=pltpu.PrefetchScalarGridSpec(num...  9.14 us
    ppermute x3, waiting for transfers between devices, body(): lax.ppermute(window, 'y', [(i, (i + d) % NY) for i in range(NY)])  8.67 us
    ppermute x1, waiting for transfers between devices, body(): lax.ppermute(low, ('y', 'z'), [(p, p - 1) for p in range(1, pairs)])  6.2 us
  transfers between devices with their start and end apart: 7, of which 6 were waited for; matrix products, arithmetic and copies ran while one was open for 3% of the time, Pallas kernels for 10%

profile of v10, /device:TPU:1, one launch (start us, length us, event | category | flops | bytes accessed | tf_op | source)
XLA Modules:
  0.0 176.4 jit_solution(17711509421042252295)
XLA Ops:
  6.5 0.0 copy-start.3
  6.5 0.0 all-gather.2.cloned.1.call-start
  6.5 4.8 %whiten.1 = (bf16[16,2,8,1024]{3,2,1,0:T(8,128)(2,1)}, bf16[2,64,1024]{2,1,0:T(8,128)(2,1)}, bf16[2,64,1024]{2,1,0:T(8,128)(2,1)}) custom-call(bf16[2,2048,128]{2,1,0:T(8,128)(2,1)} %traces_hbm.1, bf16[2,512,1024]{2,1,0:T(8,128)(2,1)} %constant.76.clone.table_hbm), custom_call_target="tpu_custom_call" | custom-call | tf_op jit(solution)/shard_map/whiten/pallas_call | solution.py:99
  11.4 0.0 copy-start.1
  11.4 0.0 copy-start.2
  11.4 0.0 copy-start.4
  11.4 21.4 %all_to_all.10 = bf16[16,2,8,1024]{3,2,1,0:T(8,128)(2,1)} all-to-all(bf16[16,2,8,1024]{3,2,1,0:T(8,128)(2,1)} %get-tuple-element.14), channel_id=1, replica_groups=mesh['y'=4,'z'=16,'xh'=2,'xl'=2,'c'=2] {'xl','c','y'}, dimensions={0} | all-to-all | bytes 1048576 | tf_op jit(solution)/shard_map/all_to_all | solution.py:257
  32.8 0.0 all-gather.2.cloned.1.call-update
  32.8 1.3 collective-permute-start
  34.1 0.0 copy-done.3
  34.1 0.6 dynamic_slice.21
  36.0 6.2 %collective-permute-done = bf16[2,64,1024]{2,1,0:T(8,128)(2,1)S(1)} collective-permute-done((bf16[2,64,1024]{2,1,0:T(8,128)(2,1)}, bf16[2,64,1024]{2,1,0:T(8,128)(2,1)S(1)}, u32[]{:S(2)}, u32[]{:S(2)}) %collective-permute-start) | collective-permute-done | bytes 262176 | tf_op jit(solution)/shard_map/ppermute | solution.py:262
  42.2 1.1 fusion
  43.3 6.2 %collective-permute-start.1 = (bf16[2,64,1024]{2,1,0:T(8,128)(2,1)S(1)}, bf16[2,64,1024]{2,1,0:T(8,128)(2,1)S(1)}, u32[]{:S(2)}, u32[]{:S(2)}) collective-permute-start(bf16[2,64,1024]{2,1,0:T(8,128)(2,1)S(1)} %fusion), channel_id=1, source_target_pairs={{0,128},{128,256},{256,384},{384,0},{1,129},{129,257},{257,385},{3... | collective-permute-start | bytes 786440 | tf_op jit(solution)/shard_map/ppermute | solution.py:267
  49.5 4.0 %collective-permute-start.2 = (bf16[2,64,1024]{2,1,0:T(8,128)(2,1)S(1)}, bf16[2,64,1024]{2,1,0:T(8,128)(2,1)S(1)}, u32[]{:S(2)}, u32[]{:S(2)}) collective-permute-start(bf16[2,64,1024]{2,1,0:T(8,128)(2,1)S(1)} %fusion), channel_id=1, source_target_pairs={{0,256},{128,384},{256,0},{384,128},{1,257},{129,385},{257,1},{385... | collective-permute-start | bytes 786440 | tf_op jit(solution)/shard_map/ppermute | solution.py:267
  53.5 2.2 %collective-permute-start.3 = (bf16[2,64,1024]{2,1,0:T(8,128)(2,1)S(1)}, bf16[2,64,1024]{2,1,0:T(8,128)(2,1)S(1)}, u32[]{:S(2)}, u32[]{:S(2)}) collective-permute-start(bf16[2,64,1024]{2,1,0:T(8,128)(2,1)S(1)} %fusion), channel_id=1, source_target_pairs={{0,384},{128,0},{256,128},{384,256},{1,385},{129,1},{257,129},{385... | collective-permute-start | bytes 786440 | tf_op jit(solution)/shard_map/ppermute | solution.py:267
  55.7 0.9 collective-permute-done.1
  56.6 6.4 %collective-permute-done.2 = bf16[2,64,1024]{2,1,0:T(8,128)(2,1)S(1)} collective-permute-done((bf16[2,64,1024]{2,1,0:T(8,128)(2,1)S(1)}, bf16[2,64,1024]{2,1,0:T(8,128)(2,1)S(1)}, u32[]{:S(2)}, u32[]{:S(2)}) %collective-permute-start.2) | collective-permute-done | bytes 262176 | tf_op jit(solution)/shard_map/ppermute | solution.py:267
  63.0 1.4 collective-permute-done.3
  64.4 0.1 pad_maximum_fusion.2
  64.5 3.3 %collective-permute-start.4 = (bf16[4,2,64,1024]{3,2,1,0:T(8,128)(2,1)S(1)}, bf16[4,2,64,1024]{3,2,1,0:T(8,128)(2,1)S(1)}, u32[]{:S(2)}, u32[]{:S(2)}) collective-permute-start(bf16[4,2,64,1024]{3,2,1,0:T(8,128)(2,1)S(1)} %pad_maximum_fusion.2), channel_id=1, source_target_pairs={{0,1},{1,0},{2,3},{3,2},{4,5},{5,4},{6,7},{7,6},{8,9},{9,8},{10,11... | collective-permute-start | bytes 3145736 | tf_op jit(solution)/shard_map/ppermute | solution.py:269
  67.8 2.3 %collective-permute-done.4 = bf16[4,2,64,1024]{3,2,1,0:T(8,128)(2,1)S(1)} collective-permute-done((bf16[4,2,64,1024]{3,2,1,0:T(8,128)(2,1)S(1)}, bf16[4,2,64,1024]{3,2,1,0:T(8,128)(2,1)S(1)}, u32[]{:S(2)}, u32[]{:S(2)}) %collective-permute-start.4) | collective-permute-done | bytes 1048608 | tf_op jit(solution)/shard_map/ppermute | solution.py:269
  70.1 1.6 pad_maximum_fusion.1
  71.6 1.9 %collective-permute-start.5 = (bf16[4,4,64,1024]{3,2,1,0:T(8,128)(2,1)}, bf16[4,4,64,1024]{3,2,1,0:T(8,128)(2,1)}, u32[]{:S(2)}, u32[]{:S(2)}) collective-permute-start(bf16[4,4,64,1024]{3,2,1,0:T(8,128)(2,1)} %pad_maximum_fusion.1), channel_id=1, source_target_pairs={{0,2},{2,0},{1,3},{3,1},{4,6},{6,4},{5,7},{7,5},{8,10},{10,8},{9,1... | collective-permute-start | bytes 6291464 | tf_op jit(solution)/shard_map/ppermute | solution.py:271
  73.6 0.0 copy-done.1
  73.6 0.1 reshape.18
  73.7 0.1 constant_dynamic-slice_fusion
  73.7 0.1 copy.11
  73.8 0.1 reshape.19
  73.9 0.0 copy-done.2
  73.9 0.1 reshape.20
  74.0 0.2 dynamic-slice_reduce_fusion
  74.2 0.0 copy-done.4
  74.2 0.1 dynamic_slice.20
  74.3 0.1 concatenate.13.info_ref
  74.4 0.1 pad_add_fusion.core_ref
  74.5 0.0 copy-start
  74.5 46.2 %collective-permute-done.5 = bf16[4,4,64,1024]{3,2,1,0:T(8,128)(2,1)} collective-permute-done((bf16[4,4,64,1024]{3,2,1,0:T(8,128)(2,1)}, bf16[4,4,64,1024]{3,2,1,0:T(8,128)(2,1)}, u32[]{:S(2)}, u32[]{:S(2)}) %collective-permute-start.5) | collective-permute-done | bytes 2097184 | tf_op jit(solution)/shard_map/ppermute | solution.py:271
  120.7 1.8 %pad_maximum_fusion.window_ref = bf16[4,8,64,1024]{3,2,1,0:T(8,128)(2,1)S(1)} fusion(bf16[4,4,64,1024]{3,2,1,0:T(8,128)(2,1)} %collective-permute-done.5, bf16[4,2,64,1024]{3,2,1,0:T(8,128)(2,1)S(1)} %collective-permute-done.4, bf16[1,2,64,1024]{3,2,1,0:T(8,128)(2,1)S(1)} %bitcast.27, bf16[1,2,64,1024]{3,2,1,0:T(8,128)(2,1)S(1)} %bitcast.24, ...), kind=kLoop, calls=%fused_computation | loop fusion | flops 10485760 | bytes 8388608 | tf_op jit(solution)/shard_map/concatenate | solution.py:273
  122.5 0.0 copy-done
  122.5 18.2 %lag_kernels.1.kernel_ref = bf16[4,8,1024,256]{3,2,1,0:T(8,128)(2,1)} custom-call(s32[2]{0:T(128)S(1)} %pad_add_fusion.core_ref, bf16[4,8,64,1024]{3,2,1,0:T(8,128)(2,1)S(1)} %pad_maximum_fusion.window_ref, f32[2,8,512]{2,1,0:T(8,128)S(1)} %copy-done), custom_call_target="tpu_custom_call" | custom-call | tf_op jit(solution)/shard_map/lag_kernels/pallas_call | solution.py:144
  140.7 0.0 all-gather.2.cloned.1.call-done.refs_0_.refs_1_.refs_2_.refs_3_.refs_4_.refs_5_.refs_6_.refs_7_
  140.7 9.1 %correlate.1 = bf16[4,4,2,64,128]{4,3,2,1,0:T(8,128)(2,1)S(1)} custom-call(s32[77]{0:T(128)S(1)} %concatenate.13.info_ref, bf16[4,8,1024,256]{3,2,1,0:T(8,128)(2,1)} %lag_kernels.1.kernel_ref, f32[2,8,512]{2,1,0:T(8,128)S(1)} %copy-done, ...), custom_call_target="tpu_custom_call" | custom-call | tf_op jit(solution)/shard_map/correlate/pallas_call | solution.py:206
  149.8 18.9 %all_to_all.11.parts_ref = bf16[32,64,128]{2,1,0:T(8,128)(2,1)S(1)} all-to-all(bf16[32,64,128]{2,1,0:T(8,128)(2,1)S(1)} %bitcast.15), channel_id=1, replica_groups=mesh['y'=4,'z'=16,'xh'=2,'xl'=2,'c'=2] {'xh','xl','y','c'}, dimensions={0} | all-to-all | bytes 1048576 | tf_op jit(solution)/shard_map/all_to_all | solution.py:280
  168.7 0.8 finish.1
  (1 shorter events, 0.0 us)
Async XLA Ops:
  6.5 27.6 %copy-start.3 = (s32[64]{0:T(128)S(1)}, s32[64]{0:T(128)}, u32[]{:S(2)}) copy-start(s32[64]{0:T(128)} %param.10) | copy-start | bytes 772
  6.5 134.2 %all-gather.2.cloned.1.call-start = ((), (), s32[]{:S(2)}) async-start(), calls=%async_computation.2 | async-start | bytes 8912896 | tf_op jit(solution)/shard_map/all_gather | solution.py:258
  11.4 62.2 %copy-start.1 = (s32[64,8]{0,1:T(8,128)S(1)}, s32[64,8]{0,1:T(8,128)}, u32[]{:S(2)}) copy-start(s32[64,8]{0,1:T(8,128)} %param.8) | copy-start | bytes 6148
  11.4 62.6 %copy-start.2 = (s32[64]{0:T(128)S(1)}, s32[64]{0:T(128)}, u32[]{:S(2)}) copy-start(s32[64]{0:T(128)} %param.9) | copy-start | bytes 772
  11.4 62.8 %copy-start.4 = (s32[16]{0:T(128)S(1)}, s32[16]{0:T(128)}, u32[]{:S(2)}) copy-start(s32[16]{0:T(128)} %param.11) | copy-start | bytes 196
  32.8 9.4 %collective-permute-start = (bf16[2,64,1024]{2,1,0:T(8,128)(2,1)}, bf16[2,64,1024]{2,1,0:T(8,128)(2,1)S(1)}, u32[]{:S(2)}, u32[]{:S(2)}) collective-permute-start(bf16[2,64,1024]{2,1,0:T(8,128)(2,1)} %get-tuple-element.13), channel_id=1, source_target_pairs={{8,0},{16,8},{24,16},{32,24},{40,32},{48,40},{56,48},{64,56},{72,6... | collective-permute-start | bytes 786440 | tf_op jit(solution)/shard_map/ppermute | solution.py:262
  43.3 13.3 %collective-permute-start.1 = (bf16[2,64,1024]{2,1,0:T(8,128)(2,1)S(1)}, bf16[2,64,1024]{2,1,0:T(8,128)(2,1)S(1)}, u32[]{:S(2)}, u32[]{:S(2)}) collective-permute-start(bf16[2,64,1024]{2,1,0:T(8,128)(2,1)S(1)} %fusion), channel_id=1, source_target_pairs={{0,128},{128,256},{256,384},{384,0},{1,129},{129,257},{257,385},{3... | collective-permute-start | bytes 786440 | tf_op jit(solution)/shard_map/ppermute | solution.py:267
  49.5 13.5 %collective-permute-start.2 = (bf16[2,64,1024]{2,1,0:T(8,128)(2,1)S(1)}, bf16[2,64,1024]{2,1,0:T(8,128)(2,1)S(1)}, u32[]{:S(2)}, u32[]{:S(2)}) collective-permute-start(bf16[2,64,1024]{2,1,0:T(8,128)(2,1)S(1)} %fusion), channel_id=1, source_target_pairs={{0,256},{128,384},{256,0},{384,128},{1,257},{129,385},{257,1},{385... | collective-permute-start | bytes 786440 | tf_op jit(solution)/shard_map/ppermute | solution.py:267
  53.5 10.9 %collective-permute-start.3 = (bf16[2,64,1024]{2,1,0:T(8,128)(2,1)S(1)}, bf16[2,64,1024]{2,1,0:T(8,128)(2,1)S(1)}, u32[]{:S(2)}, u32[]{:S(2)}) collective-permute-start(bf16[2,64,1024]{2,1,0:T(8,128)(2,1)S(1)} %fusion), channel_id=1, source_target_pairs={{0,384},{128,0},{256,128},{384,256},{1,385},{129,1},{257,129},{385... | collective-permute-start | bytes 786440 | tf_op jit(solution)/shard_map/ppermute | solution.py:267
  64.5 5.6 %collective-permute-start.4 = (bf16[4,2,64,1024]{3,2,1,0:T(8,128)(2,1)S(1)}, bf16[4,2,64,1024]{3,2,1,0:T(8,128)(2,1)S(1)}, u32[]{:S(2)}, u32[]{:S(2)}) collective-permute-start(bf16[4,2,64,1024]{3,2,1,0:T(8,128)(2,1)S(1)} %pad_maximum_fusion.2), channel_id=1, source_target_pairs={{0,1},{1,0},{2,3},{3,2},{4,5},{5,4},{6,7},{7,6},{8,9},{9,8},{10,11... | collective-permute-start | bytes 3145736 | tf_op jit(solution)/shard_map/ppermute | solution.py:269
  71.6 49.0 %collective-permute-start.5 = (bf16[4,4,64,1024]{3,2,1,0:T(8,128)(2,1)}, bf16[4,4,64,1024]{3,2,1,0:T(8,128)(2,1)}, u32[]{:S(2)}, u32[]{:S(2)}) collective-permute-start(bf16[4,4,64,1024]{3,2,1,0:T(8,128)(2,1)} %pad_maximum_fusion.1), channel_id=1, source_target_pairs={{0,2},{2,0},{1,3},{3,1},{4,6},{6,4},{5,7},{7,5},{8,10},{10,8},{9,1... | collective-permute-start | bytes 6291464 | tf_op jit(solution)/shard_map/ppermute | solution.py:271
  74.5 48.0 %copy-start = (f32[2,8,512]{2,1,0:T(8,128)S(1)}, f32[2,8,512]{2,1,0:T(8,128)}, u32[]{:S(2)}) copy-start(f32[2,8,512]{2,1,0:T(8,128)} %constant.77.clone.lag_ref) | copy-start | bytes 98308
Sparse Core Ops, SparseCore 0:
  32.9 103.9 all-gather.1

commit v11 on v10

--- a/solution.py
+++ b/solution.py
@@ -117,7 +117,8 @@
     )(traces, table)
 
 
-def lag_kernel_body(core_ref, window_ref, lag_ref, out_ref):
+def lag_kernel_body(core_ref, window_ref, lag_ref, *refs):
+    out_ref = refs[-1]
     for b in range(NB):
         at = b * 2 * FB
         real = window_ref[0, 0, :, at : at + FB].astype(F32)
@@ -140,25 +141,28 @@
     return chip * half + lax.rem(lax.rem(s, half) + SEG * core[0], half)
 
 
-def lag_kernels(core, windows, lags):
+def lag_kernels(core, windows, lags, first, kernels):
+    earlier = [] if kernels is None else [kernels]
     return pl.pallas_call(
         lag_kernel_body,
         grid_spec=pltpu.PrefetchScalarGridSpec(
             num_scalar_prefetch=1,
-            grid=(NY, SEG_PAIR),
+            grid=(NY, SEG * NC),
             in_specs=[
                 pl.BlockSpec((1, 1, R_CH, KF), lambda o, s, core: (o, s, 0, 0)),
                 pl.BlockSpec((2, LAGS, NF), lambda o, s, core: (0, 0, 0)),
-            ],
+            ]
+            + [pl.BlockSpec(memory_space=pl.ANY)] * len(earlier),
             out_specs=pl.BlockSpec(
                 (1, 1, KF, EVEN * R_CH),
-                lambda o, s, core: (o, segment_place(s, core), 0, 0),
+                lambda o, s, core: (o, segment_place(s + first, core), 0, 0),
             ),
         ),
         out_shape=jax.ShapeDtypeStruct((NY, SEG_PAIR, KF, EVEN * R_CH), BF),
+        input_output_aliases={3: 0} if earlier else {},
         compiler_params=pltpu.CompilerParams(vmem_limit_bytes=VMEM),
         name="lag_kernels",
-    )(core, windows, lags)
+    )(core, windows, lags, *earlier)
 
 
 I_COUNT = 2 * NY * K
@@ -270,7 +274,8 @@
     chip = jnp.concatenate([own, other], axis=1)
     beside = lax.ppermute(chip, "xl", [(0, 1), (1, 0)])
     core = jnp.stack([lax.axis_index("c"), lax.axis_index("xl")]).astype(jnp.int32)
-    kernels = lag_kernels(core, jnp.concatenate([chip, beside], axis=1), lags)
+    kernels = lag_kernels(core, chip, lags, 0, None)
+    kernels = lag_kernels(core, beside, lags, SEG * NC, kernels)
 
     lists = lax.dynamic_index_in_dim(source_list.reshape(NY, NZ, K), z, 1, keepdims=False).reshape(-1)
     counts = lax.dynamic_index_in_dim(source_count.reshape(NY, NZ), z, 1, keepdims=False)

time: 177 us -> 173 us (0.977)
  Pallas kernels: 33 us -> 37.3 us
  waiting for transfers between devices: 63.4 us -> 59.2 us
  other arithmetic: 4.67 us -> 1.57 us
    ppermute x1, waiting for transfers between devices: 46.2 us -> 36.4 us  [body(): beside = lax.ppermute(chip, 'xl', [(0, 1), (1, 0)])]
    pallas_call x1 -> x2, Pallas kernels: 18.2 us -> 22.5 us  [lag_kernels(): pl.pallas_call(lag_kernel_body, grid_spec=pltpu.PrefetchScalarGridSpec(nu...]
    ppermute x3, waiting for transfers between devices: 8.67 us -> 12.2 us  [body(): lax.ppermute(window, 'y', [(i, (i + d) % NY) for i in range(NY)])]
    all_gather x1, waiting for transfers between devices: 0.01 us -> 2.29 us  [body(): gathered = lax.all_gather(crossed, 'z', axis=0, tiled=False)]
    concatenate x1 -> x0, other arithmetic: 1.81 us -> none  [body(): kernels = lag_kernels(core, jnp.concatenate([chip, beside], axis=1), lags)]
  transfers between devices with their start and end apart: 7 -> 7, of which waited for: 6 -> 7; matrix products, arithmetic and copies ran while one was open for 3% -> 2% of each run, Pallas kernels for 10% -> 13%
where the time goes in v11:
time: 173 us
  waiting for transfers between devices  59.2 us (34%)
  blocking collectives  40.2 us (23%)
  Pallas kernels  37.3 us (22%)
  starting transfers between devices  17.9 us (10%)
  between operations  14.9 us (9%)
    ppermute x1, waiting for transfers between devices, body(): beside = lax.ppermute(chip, 'xl', [(0, 1), (1, 0)])  36.4 us
    pallas_call x2, Pallas kernels, lag_kernels(): pl.pallas_call(lag_kernel_body, grid_spec=pltpu.PrefetchScalarGridSpec(nu...  22.5 us
    all_to_all x1, blocking collectives, body(): lax.all_to_all(split, ('xl', 'c', 'y'), 0, 0)  21.2 us
    all_to_all x1, blocking collectives, body(): lax.all_to_all(sums.reshape(NY * LAGS, K * CQ, SLOTS * R_CH), ('xh', 'xl'...  19 us
    ppermute x3, waiting for transfers between devices, body(): lax.ppermute(window, 'y', [(i, (i + d) % NY) for i in range(NY)])  12.2 us
    ppermute x3, starting transfers between devices, body(): lax.ppermute(window, 'y', [(i, (i + d) % NY) for i in range(NY)])  11.8 us
    pallas_call x1, Pallas kernels, correlate(): pl.pallas_call(correlate_body, grid_spec=pltpu.PrefetchScalarGridSpec(num...  9.18 us
    ppermute x1, waiting for transfers between devices, body(): lax.ppermute(low, ('y', 'z'), [(p, p - 1) for p in range(1, pairs)])  6.04 us
  transfers between devices with their start and end apart: 7, of which 7 were waited for; matrix products, arithmetic and copies ran while one was open for 2% of the time, Pallas kernels for 13%

profile of v11, /device:TPU:1, one launch (start us, length us, event | category | flops | bytes accessed | tf_op | source)
XLA Modules:
  0.0 172.6 jit_solution(15398016349333984399)
XLA Ops:
  6.5 0.0 copy-start.3
  6.5 0.0 all-gather.2.cloned.1.call-start
  6.5 4.8 %whiten.1 = (bf16[16,2,8,1024]{3,2,1,0:T(8,128)(2,1)}, bf16[2,64,1024]{2,1,0:T(8,128)(2,1)}, bf16[2,64,1024]{2,1,0:T(8,128)(2,1)}) custom-call(bf16[2,2048,128]{2,1,0:T(8,128)(2,1)} %traces_hbm.1, bf16[2,512,1024]{2,1,0:T(8,128)(2,1)} %constant.76.clone.table_hbm), custom_call_target="tpu_custom_call" | custom-call | tf_op jit(solution)/shard_map/whiten/pallas_call | solution.py:99
  11.4 21.2 %all_to_all.10 = bf16[16,2,8,1024]{3,2,1,0:T(8,128)(2,1)} all-to-all(bf16[16,2,8,1024]{3,2,1,0:T(8,128)(2,1)} %get-tuple-element.14), channel_id=1, replica_groups=mesh['y'=4,'z'=16,'xh'=2,'xl'=2,'c'=2] {'xl','c','y'}, dimensions={0} | all-to-all | bytes 1048576 | tf_op jit(solution)/shard_map/all_to_all | solution.py:261
  32.6 0.0 all-gather.2.cloned.1.call-update
  32.6 1.3 collective-permute-start
  33.9 0.0 copy-done.3
  33.9 0.7 dynamic_slice.21
  36.0 6.0 %collective-permute-done = bf16[2,64,1024]{2,1,0:T(8,128)(2,1)S(1)} collective-permute-done((bf16[2,64,1024]{2,1,0:T(8,128)(2,1)}, bf16[2,64,1024]{2,1,0:T(8,128)(2,1)S(1)}, u32[]{:S(2)}, u32[]{:S(2)}) %collective-permute-start) | collective-permute-done | bytes 262176 | tf_op jit(solution)/shard_map/ppermute | solution.py:266
  42.0 1.1 fusion
  43.1 7.1 %collective-permute-start.3 = (bf16[2,64,1024]{2,1,0:T(8,128)(2,1)S(1)}, bf16[2,64,1024]{2,1,0:T(8,128)(2,1)S(1)}, u32[]{:S(2)}, u32[]{:S(2)}) collective-permute-start(bf16[2,64,1024]{2,1,0:T(8,128)(2,1)S(1)} %fusion), channel_id=1, source_target_pairs={{0,384},{128,0},{256,128},{384,256},{1,385},{129,1},{257,129},{385... | collective-permute-start | bytes 786440 | tf_op jit(solution)/shard_map/ppermute | solution.py:271
  50.2 2.9 %collective-permute-start.2 = (bf16[2,64,1024]{2,1,0:T(8,128)(2,1)S(1)}, bf16[2,64,1024]{2,1,0:T(8,128)(2,1)S(1)}, u32[]{:S(2)}, u32[]{:S(2)}) collective-permute-start(bf16[2,64,1024]{2,1,0:T(8,128)(2,1)S(1)} %fusion), channel_id=1, source_target_pairs={{0,256},{128,384},{256,0},{384,128},{1,257},{129,385},{257,1},{385... | collective-permute-start | bytes 786440 | tf_op jit(solution)/shard_map/ppermute | solution.py:271
  53.1 1.9 %collective-permute-start.1 = (bf16[2,64,1024]{2,1,0:T(8,128)(2,1)S(1)}, bf16[2,64,1024]{2,1,0:T(8,128)(2,1)S(1)}, u32[]{:S(2)}, u32[]{:S(2)}) collective-permute-start(bf16[2,64,1024]{2,1,0:T(8,128)(2,1)S(1)} %fusion), channel_id=1, source_target_pairs={{0,128},{128,256},{256,384},{384,0},{1,129},{129,257},{257,385},{3... | collective-permute-start | bytes 786440 | tf_op jit(solution)/shard_map/ppermute | solution.py:271
  55.0 1.4 collective-permute-done.3
  56.4 4.1 %collective-permute-done.2 = bf16[2,64,1024]{2,1,0:T(8,128)(2,1)S(1)} collective-permute-done((bf16[2,64,1024]{2,1,0:T(8,128)(2,1)S(1)}, bf16[2,64,1024]{2,1,0:T(8,128)(2,1)S(1)}, u32[]{:S(2)}, u32[]{:S(2)}) %collective-permute-start.2) | collective-permute-done | bytes 262176 | tf_op jit(solution)/shard_map/ppermute | solution.py:271
  60.5 6.6 %collective-permute-done.1 = bf16[2,64,1024]{2,1,0:T(8,128)(2,1)S(1)} collective-permute-done((bf16[2,64,1024]{2,1,0:T(8,128)(2,1)S(1)}, bf16[2,64,1024]{2,1,0:T(8,128)(2,1)S(1)}, u32[]{:S(2)}, u32[]{:S(2)}) %collective-permute-start.1) | collective-permute-done | bytes 262176 | tf_op jit(solution)/shard_map/ppermute | solution.py:271
  67.2 0.1 pad_maximum_fusion.1
  67.3 0.0 copy-start.1
  67.3 0.0 copy-start.2
  67.3 0.0 copy-start.4
  67.3 0.0 copy-start
  67.4 2.8 %collective-permute-start.4 = (bf16[4,2,64,1024]{3,2,1,0:T(8,128)(2,1)S(1)}, bf16[4,2,64,1024]{3,2,1,0:T(8,128)(2,1)S(1)}, u32[]{:S(2)}, u32[]{:S(2)}) collective-permute-start(bf16[4,2,64,1024]{3,2,1,0:T(8,128)(2,1)S(1)} %pad_maximum_fusion.1), channel_id=1, source_target_pairs={{0,1},{1,0},{2,3},{3,2},{4,5},{5,4},{6,7},{7,6},{8,9},{9,8},{10,11... | collective-permute-start | bytes 3145736 | tf_op jit(solution)/shard_map/ppermute | solution.py:273
  70.2 2.3 %collective-permute-done.4 = bf16[4,2,64,1024]{3,2,1,0:T(8,128)(2,1)S(1)} collective-permute-done((bf16[4,2,64,1024]{3,2,1,0:T(8,128)(2,1)S(1)}, bf16[4,2,64,1024]{3,2,1,0:T(8,128)(2,1)S(1)}, u32[]{:S(2)}, u32[]{:S(2)}) %collective-permute-start.4) | collective-permute-done | bytes 1048608 | tf_op jit(solution)/shard_map/ppermute | solution.py:273
  72.4 0.2 pad_maximum_fusion.window_ref
  72.7 1.9 %collective-permute-start.5 = (bf16[4,4,64,1024]{3,2,1,0:T(8,128)(2,1)S(1)}, bf16[4,4,64,1024]{3,2,1,0:T(8,128)(2,1)}, u32[]{:S(2)}, u32[]{:S(2)}) collective-permute-start(bf16[4,4,64,1024]{3,2,1,0:T(8,128)(2,1)S(1)} %pad_maximum_fusion.window_ref), channel_id=1, source_target_pairs={{0,2},{2,0},{1,3},{3,1},{4,6},{6,4},{5,7},{7,5},{8,10},{10,8},{9,1... | collective-permute-start | bytes 6291464 | tf_op jit(solution)/shard_map/ppermute | solution.py:275
  74.6 0.0 copy-done.1
  74.6 0.1 reshape.18
  74.7 0.1 constant_dynamic-slice_fusion
  74.8 0.1 copy.12
  74.9 0.1 reshape.19
  75.0 0.0 copy-done.2
  75.0 0.1 reshape.20
  75.1 0.2 dynamic-slice_reduce_fusion
  75.3 0.0 copy-done.4
  75.3 0.1 dynamic_slice.20
  75.4 0.1 concatenate.9.info_ref
  75.4 0.1 pad_add_fusion.core_ref
  75.5 0.0 copy-done
  75.5 9.6 %lag_kernels.2.refs_0_ = bf16[4,8,1024,256]{3,2,1,0:T(8,128)(2,1)} custom-call(s32[2]{0:T(128)S(1)} %pad_add_fusion.core_ref, bf16[4,4,64,1024]{3,2,1,0:T(8,128)(2,1)S(1)} %pad_maximum_fusion.window_ref, f32[2,8,512]{2,1,0:T(8,128)S(1)} %copy-done), custom_call_target="tpu_custom_call" | custom-call | tf_op jit(solution)/shard_map/lag_kernels/pallas_call | solution.py:146
  85.1 36.4 %collective-permute-done.5.window_ref = bf16[4,4,64,1024]{3,2,1,0:T(8,128)(2,1)} collective-permute-done((bf16[4,4,64,1024]{3,2,1,0:T(8,128)(2,1)S(1)}, bf16[4,4,64,1024]{3,2,1,0:T(8,128)(2,1)}, u32[]{:S(2)}, u32[]{:S(2)}) %collective-permute-start.5) | collective-permute-done | bytes 2097184 | tf_op jit(solution)/shard_map/ppermute | solution.py:275
  121.5 12.9 %lag_kernels.3.kernel_ref = bf16[4,8,1024,256]{3,2,1,0:T(8,128)(2,1)} custom-call(s32[2]{0:T(128)S(1)} %pad_add_fusion.core_ref, bf16[4,4,64,1024]{3,2,1,0:T(8,128)(2,1)} %collective-permute-done.5.window_ref, f32[2,8,512]{2,1,0:T(8,128)S(1)} %copy-done, bf16[4,8,1024,256]{3,2,1,0:T(8,128)(2,1)} %lag_kernels.2.refs_0_), custom_call_target="tpu_custom_call", output_to_operand_aliasing={{}: (3, {})} | custom-call | tf_op jit(solution)/shard_map/lag_kernels/pallas_call | solution.py:146
  134.4 2.3 %all-gather.2.cloned.1.call-done.refs_0_.refs_1_.refs_2_.refs_3_.refs_4_.refs_5_.refs_6_.refs_7_ = bf16[16,2,2,4,2,8,1024]{6,5,4,3,2,1,0:T(8,128)(2,1)} async-done(((bf16[1,2,2,4,2,8,1024]{6,5,4,3,2,1,0:T(8,128)(2,1)}), bf16[16,2,2,4,2,8,1024]{6,5,4,3,2,1,0:T(8,128)(2,1)}) %all-gather.2.cloned.1.call-update) | async-done | bytes 8388624 | tf_op jit(solution)/shard_map/all_gather | solution.py:262
  136.7 9.2 %correlate.1 = bf16[4,4,2,64,128]{4,3,2,1,0:T(8,128)(2,1)S(1)} custom-call(s32[77]{0:T(128)S(1)} %concatenate.9.info_ref, bf16[4,8,1024,256]{3,2,1,0:T(8,128)(2,1)} %lag_kernels.3.kernel_ref, f32[2,8,512]{2,1,0:T(8,128)S(1)} %copy-done, ...), custom_call_target="tpu_custom_call" | custom-call | tf_op jit(solution)/shard_map/correlate/pallas_call | solution.py:210
  145.9 19.0 %all_to_all.11.parts_ref = bf16[32,64,128]{2,1,0:T(8,128)(2,1)S(1)} all-to-all(bf16[32,64,128]{2,1,0:T(8,128)(2,1)S(1)} %bitcast.15), channel_id=1, replica_groups=mesh['y'=4,'z'=16,'xh'=2,'xl'=2,'c'=2] {'xh','xl','y','c'}, dimensions={0} | all-to-all | bytes 1048576 | tf_op jit(solution)/shard_map/all_to_all | solution.py:285
  164.9 0.8 finish.1
  (1 shorter events, 0.0 us)
Async XLA Ops:
  6.5 27.4 %copy-start.3 = (s32[64]{0:T(128)S(1)}, s32[64]{0:T(128)}, u32[]{:S(2)}) copy-start(s32[64]{0:T(128)} %param.10) | copy-start | bytes 772
  6.5 130.2 %all-gather.2.cloned.1.call-start = ((), (), s32[]{:S(2)}) async-start(), calls=%async_computation.2 | async-start | bytes 8912896 | tf_op jit(solution)/shard_map/all_gather | solution.py:262
  32.6 9.4 %collective-permute-start = (bf16[2,64,1024]{2,1,0:T(8,128)(2,1)}, bf16[2,64,1024]{2,1,0:T(8,128)(2,1)S(1)}, u32[]{:S(2)}, u32[]{:S(2)}) collective-permute-start(bf16[2,64,1024]{2,1,0:T(8,128)(2,1)} %get-tuple-element.13), channel_id=1, source_target_pairs={{8,0},{16,8},{24,16},{32,24},{40,32},{48,40},{56,48},{64,56},{72,6... | collective-permute-start | bytes 786440 | tf_op jit(solution)/shard_map/ppermute | solution.py:266
  43.1 13.3 %collective-permute-start.3 = (bf16[2,64,1024]{2,1,0:T(8,128)(2,1)S(1)}, bf16[2,64,1024]{2,1,0:T(8,128)(2,1)S(1)}, u32[]{:S(2)}, u32[]{:S(2)}) collective-permute-start(bf16[2,64,1024]{2,1,0:T(8,128)(2,1)S(1)} %fusion), channel_id=1, source_target_pairs={{0,384},{128,0},{256,128},{384,256},{1,385},{129,1},{257,129},{385... | collective-permute-start | bytes 786440 | tf_op jit(solution)/shard_map/ppermute | solution.py:271
  50.2 10.3 %collective-permute-start.2 = (bf16[2,64,1024]{2,1,0:T(8,128)(2,1)S(1)}, bf16[2,64,1024]{2,1,0:T(8,128)(2,1)S(1)}, u32[]{:S(2)}, u32[]{:S(2)}) collective-permute-start(bf16[2,64,1024]{2,1,0:T(8,128)(2,1)S(1)} %fusion), channel_id=1, source_target_pairs={{0,256},{128,384},{256,0},{384,128},{1,257},{129,385},{257,1},{385... | collective-permute-start | bytes 786440 | tf_op jit(solution)/shard_map/ppermute | solution.py:271
  53.1 14.1 %collective-permute-start.1 = (bf16[2,64,1024]{2,1,0:T(8,128)(2,1)S(1)}, bf16[2,64,1024]{2,1,0:T(8,128)(2,1)S(1)}, u32[]{:S(2)}, u32[]{:S(2)}) collective-permute-start(bf16[2,64,1024]{2,1,0:T(8,128)(2,1)S(1)} %fusion), channel_id=1, source_target_pairs={{0,128},{128,256},{256,384},{384,0},{1,129},{129,257},{257,385},{3... | collective-permute-start | bytes 786440 | tf_op jit(solution)/shard_map/ppermute | solution.py:271
  67.3 7.3 %copy-start.1 = (s32[64,8]{0,1:T(8,128)S(1)}, s32[64,8]{0,1:T(8,128)}, u32[]{:S(2)}) copy-start(s32[64,8]{0,1:T(8,128)} %param.8) | copy-start | bytes 6148
  67.3 7.6 %copy-start.2 = (s32[64]{0:T(128)S(1)}, s32[64]{0:T(128)}, u32[]{:S(2)}) copy-start(s32[64]{0:T(128)} %param.9) | copy-start | bytes 772
  67.3 7.9 %copy-start.4 = (s32[16]{0:T(128)S(1)}, s32[16]{0:T(128)}, u32[]{:S(2)}) copy-start(s32[16]{0:T(128)} %param.11) | copy-start | bytes 196
  67.3 8.2 %copy-start = (f32[2,8,512]{2,1,0:T(8,128)S(1)}, f32[2,8,512]{2,1,0:T(8,128)}, u32[]{:S(2)}) copy-start(f32[2,8,512]{2,1,0:T(8,128)} %constant.77.clone.lag_ref) | copy-start | bytes 98308
  67.4 5.1 %collective-permute-start.4 = (bf16[4,2,64,1024]{3,2,1,0:T(8,128)(2,1)S(1)}, bf16[4,2,64,1024]{3,2,1,0:T(8,128)(2,1)S(1)}, u32[]{:S(2)}, u32[]{:S(2)}) collective-permute-start(bf16[4,2,64,1024]{3,2,1,0:T(8,128)(2,1)S(1)} %pad_maximum_fusion.1), channel_id=1, source_target_pairs={{0,1},{1,0},{2,3},{3,2},{4,5},{5,4},{6,7},{7,6},{8,9},{9,8},{10,11... | collective-permute-start | bytes 3145736 | tf_op jit(solution)/shard_map/ppermute | solution.py:273
  72.7 48.8 %collective-permute-start.5 = (bf16[4,4,64,1024]{3,2,1,0:T(8,128)(2,1)S(1)}, bf16[4,4,64,1024]{3,2,1,0:T(8,128)(2,1)}, u32[]{:S(2)}, u32[]{:S(2)}) collective-permute-start(bf16[4,4,64,1024]{3,2,1,0:T(8,128)(2,1)S(1)} %pad_maximum_fusion.window_ref), channel_id=1, source_target_pairs={{0,2},{2,0},{1,3},{3,1},{4,6},{6,4},{5,7},{7,5},{8,10},{10,8},{9,1... | collective-permute-start | bytes 6291464 | tf_op jit(solution)/shard_map/ppermute | solution.py:275
Sparse Core Ops, SparseCore 0:
  32.7 103.9 all-gather.1

commit v12 on v11

--- a/solution.py
+++ b/solution.py
@@ -279,6 +279,10 @@
 
     lists = lax.dynamic_index_in_dim(source_list.reshape(NY, NZ, K), z, 1, keepdims=False).reshape(-1)
     counts = lax.dynamic_index_in_dim(source_count.reshape(NY, NZ), z, 1, keepdims=False)
+    rows = list(lists.reshape(NY, K))
+    for o in range(1, NY):
+        rows[o] = jnp.where(jnp.arange(K, dtype=jnp.int32) < counts[o], rows[o], rows[o - 1])
+    lists = jnp.concatenate(rows)
     slots = lax.dynamic_slice_in_dim(segment_slot, lax.axis_index("xh") * SEG_PAIR, SEG_PAIR, 0)
     info = jnp.concatenate([lists % NZ, lists // NZ, counts, slots, y[None].astype(jnp.int32)])
     sums = correlate(info, kernels, lags, gathered)

time: 173 us -> 173 us (level)
  other arithmetic: 1.57 us -> 3.58 us
    ppermute x1, waiting for transfers between devices: 36.4 us -> 34.1 us  [body(): beside = lax.ppermute(chip, 'xl', [(0, 1), (1, 0)])]
    select_n x0 -> x2, other arithmetic: none -> 1.92 us  [the longest x1 1.91 us: body(): jnp.where(jnp.arange(K, dtype=jnp.int32) < counts[o], rows[o], rows[o - 1])]
  transfers between devices with their start and end apart: 7 -> 7, of which waited for: 7 -> 7; matrix products, arithmetic and copies ran while one was open for 2% -> 3% of each run, Pallas kernels for 13% -> 13%
where the time goes in v12:
time: 173 us; the launch traced here: 172 us
  waiting for transfers between devices  57.7 us (33%)
  blocking collectives  40.2 us (23%)
  Pallas kernels  36.9 us (21%)
  starting transfers between devices  17.5 us (10%)
  between operations  14.6 us (8%)
  other arithmetic  3.58 us (2%)
    ppermute x1, waiting for transfers between devices, body(): beside = lax.ppermute(chip, 'xl', [(0, 1), (1, 0)])  34.1 us
    pallas_call x2, Pallas kernels, lag_kernels(): pl.pallas_call(lag_kernel_body, grid_spec=pltpu.PrefetchScalarGridSpec(nu...  22.4 us
    all_to_all x1, blocking collectives, body(): lax.all_to_all(split, ('xl', 'c', 'y'), 0, 0)  21.2 us
    all_to_all x1, blocking collectives, body(): lax.all_to_all(sums.reshape(NY * LAGS, K * CQ, SLOTS * R_CH), ('xh', 'xl'...  18.9 us
    ppermute x3, waiting for transfers between devices, body(): lax.ppermute(window, 'y', [(i, (i + d) % NY) for i in range(NY)])  12.6 us
    ppermute x3, starting transfers between devices, body(): lax.ppermute(window, 'y', [(i, (i + d) % NY) for i in range(NY)])  11.6 us
    pallas_call x1, Pallas kernels, correlate(): pl.pallas_call(correlate_body, grid_spec=pltpu.PrefetchScalarGridSpec(num...  8.85 us
    ppermute x1, waiting for transfers between devices, body(): lax.ppermute(low, ('y', 'z'), [(p, p - 1) for p in range(1, pairs)])  6.43 us
  transfers between devices with their start and end apart: 7, of which 7 were waited for; matrix products, arithmetic and copies ran while one was open for 3% of the time, Pallas kernels for 13%

profile of v12, /device:TPU:1, one launch (start us, length us, event | category | flops | bytes accessed | tf_op | source)
XLA Modules:
  0.0 172.2 jit_solution(8089578541429716173)
XLA Ops:
  6.5 0.0 copy-start.3
  6.5 0.0 all-gather.2.cloned.1.call-start
  6.5 4.8 %whiten.1 = (bf16[16,2,8,1024]{3,2,1,0:T(8,128)(2,1)}, bf16[2,64,1024]{2,1,0:T(8,128)(2,1)}, bf16[2,64,1024]{2,1,0:T(8,128)(2,1)}) custom-call(bf16[2,2048,128]{2,1,0:T(8,128)(2,1)} %traces_hbm.1, bf16[2,512,1024]{2,1,0:T(8,128)(2,1)} %constant.76.clone.table_hbm), custom_call_target="tpu_custom_call" | custom-call | tf_op jit(solution)/shard_map/whiten/pallas_call | solution.py:99
  11.4 21.2 %all_to_all.10 = bf16[16,2,8,1024]{3,2,1,0:T(8,128)(2,1)} all-to-all(bf16[16,2,8,1024]{3,2,1,0:T(8,128)(2,1)} %get-tuple-element.14), channel_id=1, replica_groups=mesh['y'=4,'z'=16,'xh'=2,'xl'=2,'c'=2] {'xl','c','y'}, dimensions={0} | all-to-all | bytes 1048576 | tf_op jit(solution)/shard_map/all_to_all | solution.py:261
  32.6 0.0 all-gather.2.cloned.1.call-update
  32.6 1.3 collective-permute-start
  33.9 0.0 copy-done.3
  33.9 0.6 dynamic_slice.21
  35.6 6.4 %collective-permute-done = bf16[2,64,1024]{2,1,0:T(8,128)(2,1)S(1)} collective-permute-done((bf16[2,64,1024]{2,1,0:T(8,128)(2,1)}, bf16[2,64,1024]{2,1,0:T(8,128)(2,1)S(1)}, u32[]{:S(2)}, u32[]{:S(2)}) %collective-permute-start) | collective-permute-done | bytes 262176 | tf_op jit(solution)/shard_map/ppermute | solution.py:266
  42.0 1.1 fusion
  43.1 7.1 %collective-permute-start.3 = (bf16[2,64,1024]{2,1,0:T(8,128)(2,1)S(1)}, bf16[2,64,1024]{2,1,0:T(8,128)(2,1)S(1)}, u32[]{:S(2)}, u32[]{:S(2)}) collective-permute-start(bf16[2,64,1024]{2,1,0:T(8,128)(2,1)S(1)} %fusion), channel_id=1, source_target_pairs={{0,384},{128,0},{256,128},{384,256},{1,385},{129,1},{257,129},{385... | collective-permute-start | bytes 786440 | tf_op jit(solution)/shard_map/ppermute | solution.py:271
  50.2 2.6 %collective-permute-start.2 = (bf16[2,64,1024]{2,1,0:T(8,128)(2,1)S(1)}, bf16[2,64,1024]{2,1,0:T(8,128)(2,1)S(1)}, u32[]{:S(2)}, u32[]{:S(2)}) collective-permute-start(bf16[2,64,1024]{2,1,0:T(8,128)(2,1)S(1)} %fusion), channel_id=1, source_target_pairs={{0,256},{128,384},{256,0},{384,128},{1,257},{129,385},{257,1},{385... | collective-permute-start | bytes 786440 | tf_op jit(solution)/shard_map/ppermute | solution.py:271
  52.9 1.9 %collective-permute-start.1 = (bf16[2,64,1024]{2,1,0:T(8,128)(2,1)S(1)}, bf16[2,64,1024]{2,1,0:T(8,128)(2,1)S(1)}, u32[]{:S(2)}, u32[]{:S(2)}) collective-permute-start(bf16[2,64,1024]{2,1,0:T(8,128)(2,1)S(1)} %fusion), channel_id=1, source_target_pairs={{0,128},{128,256},{256,384},{384,0},{1,129},{129,257},{257,385},{3... | collective-permute-start | bytes 786440 | tf_op jit(solution)/shard_map/ppermute | solution.py:271
  54.8 1.9 %collective-permute-done.3 = bf16[2,64,1024]{2,1,0:T(8,128)(2,1)S(1)} collective-permute-done((bf16[2,64,1024]{2,1,0:T(8,128)(2,1)S(1)}, bf16[2,64,1024]{2,1,0:T(8,128)(2,1)S(1)}, u32[]{:S(2)}, u32[]{:S(2)}) %collective-permute-start.3) | collective-permute-done | bytes 262176 | tf_op jit(solution)/shard_map/ppermute | solution.py:271
  56.7 3.9 %collective-permute-done.2 = bf16[2,64,1024]{2,1,0:T(8,128)(2,1)S(1)} collective-permute-done((bf16[2,64,1024]{2,1,0:T(8,128)(2,1)S(1)}, bf16[2,64,1024]{2,1,0:T(8,128)(2,1)S(1)}, u32[]{:S(2)}, u32[]{:S(2)}) %collective-permute-start.2) | collective-permute-done | bytes 262176 | tf_op jit(solution)/shard_map/ppermute | solution.py:271
  60.6 6.8 %collective-permute-done.1 = bf16[2,64,1024]{2,1,0:T(8,128)(2,1)S(1)} collective-permute-done((bf16[2,64,1024]{2,1,0:T(8,128)(2,1)S(1)}, bf16[2,64,1024]{2,1,0:T(8,128)(2,1)S(1)}, u32[]{:S(2)}, u32[]{:S(2)}) %collective-permute-start.1) | collective-permute-done | bytes 262176 | tf_op jit(solution)/shard_map/ppermute | solution.py:271
  67.4 0.1 pad_maximum_fusion.1
  67.5 0.0 copy-start.1
  67.5 0.0 copy-start.2
  67.5 0.0 copy-start.4
  67.5 0.0 copy-start
  67.6 2.6 %collective-permute-start.4 = (bf16[4,2,64,1024]{3,2,1,0:T(8,128)(2,1)S(1)}, bf16[4,2,64,1024]{3,2,1,0:T(8,128)(2,1)S(1)}, u32[]{:S(2)}, u32[]{:S(2)}) collective-permute-start(bf16[4,2,64,1024]{3,2,1,0:T(8,128)(2,1)S(1)} %pad_maximum_fusion.1), channel_id=1, source_target_pairs={{0,1},{1,0},{2,3},{3,2},{4,5},{5,4},{6,7},{7,6},{8,9},{9,8},{10,11... | collective-permute-start | bytes 3145736 | tf_op jit(solution)/shard_map/ppermute | solution.py:273
  70.2 2.3 %collective-permute-done.4 = bf16[4,2,64,1024]{3,2,1,0:T(8,128)(2,1)S(1)} collective-permute-done((bf16[4,2,64,1024]{3,2,1,0:T(8,128)(2,1)S(1)}, bf16[4,2,64,1024]{3,2,1,0:T(8,128)(2,1)S(1)}, u32[]{:S(2)}, u32[]{:S(2)}) %collective-permute-start.4) | collective-permute-done | bytes 1048608 | tf_op jit(solution)/shard_map/ppermute | solution.py:273
  72.5 0.2 pad_maximum_fusion.window_ref
  72.7 1.9 %collective-permute-start.5 = (bf16[4,4,64,1024]{3,2,1,0:T(8,128)(2,1)S(1)}, bf16[4,4,64,1024]{3,2,1,0:T(8,128)(2,1)}, u32[]{:S(2)}, u32[]{:S(2)}) collective-permute-start(bf16[4,4,64,1024]{3,2,1,0:T(8,128)(2,1)S(1)} %pad_maximum_fusion.window_ref), channel_id=1, source_target_pairs={{0,2},{2,0},{1,3},{3,1},{4,6},{6,4},{5,7},{7,5},{8,10},{10,8},{9,1... | collective-permute-start | bytes 6291464 | tf_op jit(solution)/shard_map/ppermute | solution.py:275
  74.6 0.0 copy-done.1
  74.7 0.1 copy.12
  74.7 0.0 copy-done.2
  74.7 0.1 reshape.29
  74.8 0.0 copy-done.4
  74.8 0.1 dynamic_slice.20
  74.9 0.2 fusion.5
  75.1 0.6 fusion.7
  75.7 1.9 %compare_select_fusion = (s32[8]{0:T(128)S(1)}, s32[8]{0:T(128)S(1)}, s32[8]{0:T(128)S(1)}, s32[8]{0:T(128)S(1)}) fusion(s32[4,16,8]{2,1,0:T(8,128)S(1)} %bitcast.42, s32[]{:T(128)S(6)} %add.47, s32[]{:T(128)S(6)} %select_n.38, s32[]{:T(128)} %bitcast.6, s32[]{:T(128)S(6)} %add.46, s32[]{:T(128)} %bitcast.4, s32[]{:T(128)S(6)} %add.45, s32[]{:T(128)} %bitcast.2), kind=kLoop, calls=%fused_computation.7 | loop fusion | flops 48 | bytes 284 | tf_op jit(solution)/shard_map/jit(_where)/select_n | solution.py:284
  77.6 0.1 and_select_fusion
  77.7 0.1 concatenate.13.info_ref
  77.8 0.1 pad_add_fusion.1.core_ref
  77.9 0.0 copy-done
  77.9 9.5 %lag_kernels.2.refs_0_ = bf16[4,8,1024,256]{3,2,1,0:T(8,128)(2,1)} custom-call(s32[2]{0:T(128)S(1)} %pad_add_fusion.1.core_ref, bf16[4,4,64,1024]{3,2,1,0:T(8,128)(2,1)S(1)} %pad_maximum_fusion.window_ref, f32[2,8,512]{2,1,0:T(8,128)S(1)} %copy-done), custom_call_target="tpu_custom_call" | custom-call | tf_op jit(solution)/shard_map/lag_kernels/pallas_call | solution.py:146
  87.4 34.1 %collective-permute-done.5.window_ref = bf16[4,4,64,1024]{3,2,1,0:T(8,128)(2,1)} collective-permute-done((bf16[4,4,64,1024]{3,2,1,0:T(8,128)(2,1)S(1)}, bf16[4,4,64,1024]{3,2,1,0:T(8,128)(2,1)}, u32[]{:S(2)}, u32[]{:S(2)}) %collective-permute-start.5) | collective-permute-done | bytes 2097184 | tf_op jit(solution)/shard_map/ppermute | solution.py:275
  121.6 12.9 %lag_kernels.3.kernel_ref = bf16[4,8,1024,256]{3,2,1,0:T(8,128)(2,1)} custom-call(s32[2]{0:T(128)S(1)} %pad_add_fusion.1.core_ref, bf16[4,4,64,1024]{3,2,1,0:T(8,128)(2,1)} %collective-permute-done.5.window_ref, f32[2,8,512]{2,1,0:T(8,128)S(1)} %copy-done, bf16[4,8,1024,256]{3,2,1,0:T(8,128)(2,1)} %lag_kernels.2.refs_0_), custom_call_target="tpu_custom_call", output_to_operand_aliasing={{}: (3, {})} | custom-call | tf_op jit(solution)/shard_map/lag_kernels/pallas_call | solution.py:146
  134.4 2.3 %all-gather.2.cloned.1.call-done.refs_0_.refs_1_.refs_2_.refs_3_.refs_4_.refs_5_.refs_6_.refs_7_ = bf16[16,2,2,4,2,8,1024]{6,5,4,3,2,1,0:T(8,128)(2,1)} async-done(((bf16[1,2,2,4,2,8,1024]{6,5,4,3,2,1,0:T(8,128)(2,1)}), bf16[16,2,2,4,2,8,1024]{6,5,4,3,2,1,0:T(8,128)(2,1)}) %all-gather.2.cloned.1.call-update) | async-done | bytes 8388624 | tf_op jit(solution)/shard_map/all_gather | solution.py:262
  136.7 8.8 %correlate.1 = bf16[4,4,2,64,128]{4,3,2,1,0:T(8,128)(2,1)S(1)} custom-call(s32[77]{0:T(128)S(1)} %concatenate.13.info_ref, bf16[4,8,1024,256]{3,2,1,0:T(8,128)(2,1)} %lag_kernels.3.kernel_ref, f32[2,8,512]{2,1,0:T(8,128)S(1)} %copy-done, ...), custom_call_target="tpu_custom_call" | custom-call | tf_op jit(solution)/shard_map/correlate/pallas_call | solution.py:210
  145.6 18.9 %all_to_all.11.parts_ref = bf16[32,64,128]{2,1,0:T(8,128)(2,1)S(1)} all-to-all(bf16[32,64,128]{2,1,0:T(8,128)(2,1)S(1)} %bitcast.32), channel_id=1, replica_groups=mesh['y'=4,'z'=16,'xh'=2,'xl'=2,'c'=2] {'xh','xl','y','c'}, dimensions={0} | all-to-all | bytes 1048576 | tf_op jit(solution)/shard_map/all_to_all | solution.py:289
  164.5 0.8 finish.1
  (1 shorter events, 0.0 us)
Async XLA Ops:
  6.5 27.4 %copy-start.3 = (s32[64]{0:T(128)S(1)}, s32[64]{0:T(128)}, u32[]{:S(2)}) copy-start(s32[64]{0:T(128)} %param.10) | copy-start | bytes 772
  6.5 130.2 %all-gather.2.cloned.1.call-start = ((), (), s32[]{:S(2)}) async-start(), calls=%async_computation.2 | async-start | bytes 8912896 | tf_op jit(solution)/shard_map/all_gather | solution.py:262
  32.6 9.4 %collective-permute-start = (bf16[2,64,1024]{2,1,0:T(8,128)(2,1)}, bf16[2,64,1024]{2,1,0:T(8,128)(2,1)S(1)}, u32[]{:S(2)}, u32[]{:S(2)}) collective-permute-start(bf16[2,64,1024]{2,1,0:T(8,128)(2,1)} %get-tuple-element.13), channel_id=1, source_target_pairs={{8,0},{16,8},{24,16},{32,24},{40,32},{48,40},{56,48},{64,56},{72,6... | collective-permute-start | bytes 786440 | tf_op jit(solution)/shard_map/ppermute | solution.py:266
  43.1 13.5 %collective-permute-start.3 = (bf16[2,64,1024]{2,1,0:T(8,128)(2,1)S(1)}, bf16[2,64,1024]{2,1,0:T(8,128)(2,1)S(1)}, u32[]{:S(2)}, u32[]{:S(2)}) collective-permute-start(bf16[2,64,1024]{2,1,0:T(8,128)(2,1)S(1)} %fusion), channel_id=1, source_target_pairs={{0,384},{128,0},{256,128},{384,256},{1,385},{129,1},{257,129},{385... | collective-permute-start | bytes 786440 | tf_op jit(solution)/shard_map/ppermute | solution.py:271
  50.2 10.4 %collective-permute-start.2 = (bf16[2,64,1024]{2,1,0:T(8,128)(2,1)S(1)}, bf16[2,64,1024]{2,1,0:T(8,128)(2,1)S(1)}, u32[]{:S(2)}, u32[]{:S(2)}) collective-permute-start(bf16[2,64,1024]{2,1,0:T(8,128)(2,1)S(1)} %fusion), channel_id=1, source_target_pairs={{0,256},{128,384},{256,0},{384,128},{1,257},{129,385},{257,1},{385... | collective-permute-start | bytes 786440 | tf_op jit(solution)/shard_map/ppermute | solution.py:271
  52.9 14.5 %collective-permute-start.1 = (bf16[2,64,1024]{2,1,0:T(8,128)(2,1)S(1)}, bf16[2,64,1024]{2,1,0:T(8,128)(2,1)S(1)}, u32[]{:S(2)}, u32[]{:S(2)}) collective-permute-start(bf16[2,64,1024]{2,1,0:T(8,128)(2,1)S(1)} %fusion), channel_id=1, source_target_pairs={{0,128},{128,256},{256,384},{384,0},{1,129},{129,257},{257,385},{3... | collective-permute-start | bytes 786440 | tf_op jit(solution)/shard_map/ppermute | solution.py:271
  67.5 7.1 %copy-start.1 = (s32[64,8]{0,1:T(8,128)S(1)}, s32[64,8]{0,1:T(8,128)}, u32[]{:S(2)}) copy-start(s32[64,8]{0,1:T(8,128)} %param.8) | copy-start | bytes 6148
  67.5 7.2 %copy-start.2 = (s32[64]{0:T(128)S(1)}, s32[64]{0:T(128)}, u32[]{:S(2)}) copy-start(s32[64]{0:T(128)} %param.9) | copy-start | bytes 772
  67.5 7.3 %copy-start.4 = (s32[16]{0:T(128)S(1)}, s32[16]{0:T(128)}, u32[]{:S(2)}) copy-start(s32[16]{0:T(128)} %param.11) | copy-start | bytes 196
  67.5 10.3 %copy-start = (f32[2,8,512]{2,1,0:T(8,128)S(1)}, f32[2,8,512]{2,1,0:T(8,128)}, u32[]{:S(2)}) copy-start(f32[2,8,512]{2,1,0:T(8,128)} %constant.77.clone.lag_ref) | copy-start | bytes 98308
  67.6 4.9 %collective-permute-start.4 = (bf16[4,2,64,1024]{3,2,1,0:T(8,128)(2,1)S(1)}, bf16[4,2,64,1024]{3,2,1,0:T(8,128)(2,1)S(1)}, u32[]{:S(2)}, u32[]{:S(2)}) collective-permute-start(bf16[4,2,64,1024]{3,2,1,0:T(8,128)(2,1)S(1)} %pad_maximum_fusion.1), channel_id=1, source_target_pairs={{0,1},{1,0},{2,3},{3,2},{4,5},{5,4},{6,7},{7,6},{8,9},{9,8},{10,11... | collective-permute-start | bytes 3145736 | tf_op jit(solution)/shard_map/ppermute | solution.py:273
  72.7 48.8 %collective-permute-start.5 = (bf16[4,4,64,1024]{3,2,1,0:T(8,128)(2,1)S(1)}, bf16[4,4,64,1024]{3,2,1,0:T(8,128)(2,1)}, u32[]{:S(2)}, u32[]{:S(2)}) collective-permute-start(bf16[4,4,64,1024]{3,2,1,0:T(8,128)(2,1)S(1)} %pad_maximum_fusion.window_ref), channel_id=1, source_target_pairs={{0,2},{2,0},{1,3},{3,1},{4,6},{6,4},{5,7},{7,5},{8,10},{10,8},{9,1... | collective-permute-start | bytes 6291464 | tf_op jit(solution)/shard_map/ppermute | solution.py:275
Sparse Core Ops, SparseCore 0:
  32.7 103.9 all-gather.1
